TPU v7x, 32 devices: a whole 2x2x4 slice. The times are simulated.
32 devices in a mesh: occ: 2 (over core), vir: 16 (over z, y, x).
Axes of the slice: x: 2, y: 2, z: 4, core: 2. Of those that a mesh axis runs over, the one named last changes fastest.
Arguments:
- amplitudes: bfloat16 [2256, 6144], P('occ', 'vir'), may hold values from -6 to 6
- ladder_ints: bfloat16 [6144, 6144], P('vir', 'occ'), as said below
- tile_map: int32 [48, 48], replicated, may hold values from 0 to 1, as said below
- hole_ints: bfloat16 [2256, 2256], P('occ'), may hold values from -0.125 to 0.125
- occ_energy: float32 [48], replicated, may hold values from -2 to -0.3
- pair_list: int32 [2256, 2], P('occ'), may hold values from 0 to 47, as said below
- mirror_row: int32 [2256], P('occ'), may hold values from 0 to 2255, as said below
Outputs:
- residual: float32 [2256, 6144], P('occ', 'vir')
Inputs may be any that keep to these rules, and one draw needn't show every extreme that they name: symmetric: ladder_ints[ab, cd] equals ladder_ints[cd, ab]. `tile_map`: symmetric. `pair_list`: each ordered pair of distinct orbitals of the 48 occupied ones stands in exactly one row. Row mirror_row[r] holds the pair of row r reversed.
All inputs are finite; a program needn't handle non-finite values.
Results may differ from a plain program's by a relative error of at most 0.0003.
Values may be sent and summed in bfloat16 or wider, within the bound.
No kernel may reach another device: no remote copies, remote signals or barrier semaphores. Data moves between devices by JAX's collectives and lax.ppermute only.
A program may use at most 64 MiB of HBM per device.

v0:
```python
import functools

import jax
import jax.numpy as jnp
from jax import lax
from jax.experimental import pallas as pl
from jax.experimental.pallas import tpu as pltpu
from jax.sharding import PartitionSpec as P


TILE = 128
SHARES = (360, 320, 256, 192)


LIMIT = 16 * 1024 * 1024
MIRROR_LIMIT = 24 * 1024 * 1024

SMEM = pl.BlockSpec(memory_space=pltpu.SMEM)
VMEM = pl.BlockSpec(memory_space=pltpu.VMEM)
HBM = pl.BlockSpec(memory_space=pltpu.HBM)


def row_chunks(rows, shares):
    edges = [0]
    for k in range(1, len(shares)):
        edges.append(rows * sum(shares[:k]) // sum(shares) // 8 * 8)
    edges.append(rows)
    return [(a, b - a) for a, b in zip(edges, edges[1:]) if b > a]


def other_core(a):
    return lax.ppermute(a, "occ", [(0, 1), (1, 0)])


def parts_kernel(chunks, side_ref, *refs):
    sources = refs[: 1 + bool(chunks)]
    *outs, sems = refs[len(sources) :]
    v_hbm, sent = sources[0], outs[0]
    cols = sent.shape[0]
    copies = []
    for k, ((start, length), out) in enumerate(zip(chunks, outs[1:])):
        copies.append(pltpu.make_async_copy(sources[1].at[pl.ds(start, length)], out, sems.at[k]))
    for j in range(sent.shape[1] // cols):
        at = pl.multiple_of((2 * j + side_ref[0]) * cols, TILE)
        copies.append(
            pltpu.make_async_copy(
                v_hbm.at[:, pl.ds(at, cols)],
                sent.at[:, pl.ds(j * cols, cols)],
                sems.at[len(chunks) + j],
            )
        )
    for copy in copies:
        copy.start()
    for copy in copies:
        copy.wait()


def parts(side, integrals, amplitudes=None, chunks=()):
    cols, width = integrals.shape
    shapes = [jax.ShapeDtypeStruct((cols, width // 2), integrals.dtype)]
    shapes += [jax.ShapeDtypeStruct((length, cols), integrals.dtype) for _, length in chunks]
    given = [amplitudes] if chunks else []
    return pl.pallas_call(
        functools.partial(parts_kernel, tuple(chunks)),
        out_shape=shapes,
        in_specs=[SMEM] + [HBM] * (1 + len(given)),
        out_specs=[VMEM] * len(shapes),
        scratch_shapes=[pltpu.SemaphoreType.DMA((len(chunks) + width // cols // 2,))],
        compiler_params=pltpu.CompilerParams(vmem_limit_bytes=None if chunks else LIMIT),
        cost_estimate=pl.CostEstimate(
            flops=0, bytes_accessed=4 * integrals.size, transcendentals=0
        ),
        name="parts",
    )(side, integrals, *given)


def prepare_kernel(cols, index_ref, map_hbm, *refs):
    *pieces, out_ref, map_ref, sem = refs
    copy = pltpu.make_async_copy(map_hbm, map_ref, sem)
    copy.start()
    copy.wait()
    count = out_ref.shape[0] // cols
    per_piece = pieces[0].shape[1] // cols
    first_row = index_ref[2 * count]
    for k in range(count):
        for p, piece in enumerate(pieces):
            at = index_ref[k] - p * per_piece

            @pl.when((at >= 0) & (at < per_piece))
            def _():
                for c in range(0, cols, TILE):
                    for r in range(0, out_ref.shape[1], TILE):
                        allowed = map_ref[first_row + r // TILE, index_ref[count + k] + c // TILE]
                        from_col = pl.multiple_of(at * cols + c, TILE)
                        tile = piece[r : r + TILE, pl.ds(from_col, TILE)]
                        tile = jnp.where(allowed == 1, tile, jnp.zeros_like(tile))
                        out_ref[k * cols + c : k * cols + c + TILE, r : r + TILE] = tile.T


def prepare(index, tile_map, pieces, cols):
    depth = sum(piece.shape[1] for piece in pieces)
    width = pieces[0].shape[0]
    return pl.pallas_call(
        functools.partial(prepare_kernel, cols),
        out_shape=jax.ShapeDtypeStruct((depth, width), pieces[0].dtype),
        in_specs=[SMEM, HBM] + [VMEM] * len(pieces),
        out_specs=VMEM,
        scratch_shapes=[pltpu.SMEM(tile_map.shape, tile_map.dtype), pltpu.SemaphoreType.DMA],
        compiler_params=pltpu.CompilerParams(vmem_limit_bytes=LIMIT),
        cost_estimate=pl.CostEstimate(
            flops=0, bytes_accessed=4 * depth * width, transcendentals=0
        ),
        name="prepare",
    )(index, tile_map, *pieces)


def product_kernel(count, start, *refs):
    integrals, out = refs[count], refs[-1]
    row = jnp.concatenate([block[...] for block in refs[:count]], axis=1)
    result = jnp.dot(row, integrals[...], preferred_element_type=jnp.float32)
    if start is not None:
        result = result + refs[count + 1][start : start + out.shape[0], :]
    out[...] = result


def product(blocks, integrals, base=None, start=None):
    length, _ = blocks[0].shape
    given = [] if base is None else [base]
    depth, width = integrals.shape
    return pl.pallas_call(
        functools.partial(product_kernel, len(blocks), start),
        out_shape=jax.ShapeDtypeStruct((length, width), jnp.float32),
        in_specs=[VMEM] * (len(blocks) + 1 + len(given)),
        out_specs=VMEM,
        compiler_params=pltpu.CompilerParams(vmem_limit_bytes=LIMIT),
        cost_estimate=pl.CostEstimate(
            flops=2 * length * depth * width,
            bytes_accessed=2 * depth * (length + width),
            transcendentals=0,
        ),
        name="product",
    )(*blocks, integrals, *given)


def for_groups(count, most, body):
    inline = max(u for u in range(1, most + 1) if count % u == 0)

    def step(i, carry):
        for u in range(inline):
            body(i * inline + u)
        return carry

    lax.fori_loop(0, count // inline, step, 0)


def mirror_kernel(offsets, own_count, index_ref, *refs):
    *pieces, out_ref, whole, picked = refs
    rows, cols = out_ref.shape
    lanes = cols // TILE

    for piece, offset in zip(pieces, offsets):

        def spread(g):
            at = pl.multiple_of(g * 8, 8)
            for c in range(lanes):
                whole[pl.ds(offset + at, 8), c, :] = piece[pl.ds(at, 8), c * TILE : (c + 1) * TILE]

        for_groups(piece.shape[0] // 8, 6, spread)

    def pick(g):
        for j in range(8):
            picked[g, :, j, :] = whole[index_ref[g * 8 + j]]

    for_groups(rows // 8, 6, pick)
    for j in range(rows % 8):
        picked[rows // 8, :, j, :] = whole[index_ref[rows // 8 * 8 + j]]

    odd = lax.broadcasted_iota(jnp.int32, (8, TILE), 1) % 2 == 1

    def finish(own, offset, g, size):
        at = g * 8 if isinstance(g, int) else pl.multiple_of(g * 8, 8)
        for c in range(lanes):
            part = picked[offset // 8 + g, c]
            swapped = jnp.where(odd, pltpu.roll(part, 1, 1), pltpu.roll(part, TILE - 1, 1))
            out_ref[pl.ds(offset + at, size), c * TILE : (c + 1) * TILE] = (
                own[pl.ds(at, size), c * TILE : (c + 1) * TILE] + swapped[:size]
            )

    for own, offset in zip(pieces[:own_count], offsets):
        length = min(own.shape[0], rows - offset)
        for_groups(length // 8, 48, functools.partial(finish, own, offset, size=8))
        if length % 8:
            finish(own, offset, length // 8, length % 8)


def add_mirror(index, rows, own, others):
    cols = own[0].shape[1]
    offsets, total = [], 0
    for piece in (*own, *others):
        offsets.append(total)
        total += piece.shape[0]
    return pl.pallas_call(
        functools.partial(mirror_kernel, tuple(offsets), len(own)),
        out_shape=jax.ShapeDtypeStruct((rows, cols), jnp.float32),
        in_specs=[SMEM] + [VMEM] * (len(own) + len(others)),
        out_specs=VMEM,
        scratch_shapes=[
            pltpu.VMEM((total, cols // TILE, TILE), jnp.float32),
            pltpu.VMEM((-(-rows // 8), cols // TILE, 8, TILE), jnp.float32),
        ],
        compiler_params=pltpu.CompilerParams(vmem_limit_bytes=MIRROR_LIMIT),
        cost_estimate=pl.CostEstimate(
            flops=rows * cols, bytes_accessed=(total + rows) * cols * 4, transcendentals=0
        ),
        name="mirror",
    )(index, *own, *others)


def spread_rows(piece, whole, offset):
    def spread(g):
        at = pl.multiple_of(g * 8, 8)
        for c in range(piece.shape[1] // TILE):
            whole[pl.ds(offset + at, 8), c, :] = piece[pl.ds(at, 8), c * TILE : (c + 1) * TILE]

    for_groups(piece.shape[0] // 8, 6, spread)


def early_kernel(index_ref, *refs):
    *pieces, picked, whole = refs
    offset = 0
    for piece in pieces:
        spread_rows(piece, whole, offset)
        offset += piece.shape[0]

    def pick(g):
        for j in range(8):
            picked[g * 8 + j] = whole[index_ref[g * 8 + j]]

    for_groups(index_ref.shape[0] // 8, 6, pick)


def late_kernel(target_ref, *refs):
    *own, other, _, out_hbm, picked, whole, out_ref, sems = refs
    spread_rows(own[-1], whole, 0)
    spread_rows(other, whole, other.shape[0])

    def put(g):
        for j in range(8):
            picked[target_ref[g * 8 + j]] = whole[g * 8 + j]

    for_groups(target_ref.shape[0] // 8, 6, put)

    odd = lax.broadcasted_iota(jnp.int32, (8, TILE), 1) % 2 == 1

    def finish(piece, offset, g):
        at = pl.multiple_of(g * 8, 8)
        for c in range(piece.shape[1] // TILE):
            part = picked[pl.ds(offset + at, 8), c, :]
            swapped = jnp.where(odd, pltpu.roll(part, 1, 1), pltpu.roll(part, TILE - 1, 1))
            out_ref[pl.ds(offset + at, 8), c * TILE : (c + 1) * TILE] = (
                piece[pl.ds(at, 8), c * TILE : (c + 1) * TILE] + swapped
            )

    offset = 0
    copies = []
    for k, piece in enumerate(own):
        for_groups(piece.shape[0] // 8, 48, functools.partial(finish, piece, offset))
        band = pl.ds(offset, piece.shape[0])
        copies.append(pltpu.make_async_copy(out_ref.at[band], out_hbm.at[band], sems.at[k]))
        copies[-1].start()
        offset += piece.shape[0]
    for copy in copies:
        copy.wait()


def add_mirror_in_steps(index, target, rows, own, others):
    cols = own[0].shape[1]
    early = [*own[:-1], *others[:-1]]
    slab = (cols // TILE, TILE)
    picked_shape = jax.ShapeDtypeStruct((rows + 8, *slab), jnp.float32)
    cost = pl.CostEstimate(flops=rows * cols, bytes_accessed=12 * rows * cols, transcendentals=0)
    params = pltpu.CompilerParams(vmem_limit_bytes=MIRROR_LIMIT)
    picked = pl.pallas_call(
        early_kernel,
        out_shape=picked_shape,
        in_specs=[SMEM] + [VMEM] * len(early),
        out_specs=VMEM,
        scratch_shapes=[pltpu.VMEM((sum(p.shape[0] for p in early), *slab), jnp.float32)],
        compiler_params=params,
        cost_estimate=cost,
        name="mirror_early",
    )(index, *early)
    return pl.pallas_call(
        late_kernel,
        out_shape=[jax.ShapeDtypeStruct((rows, cols), jnp.float32), picked_shape],
        in_specs=[SMEM] + [VMEM] * (len(own) + 2),
        out_specs=[HBM, VMEM],
        scratch_shapes=[
            pltpu.VMEM((2 * own[-1].shape[0], *slab), jnp.float32),
            pltpu.VMEM((rows, cols), jnp.float32),
            pltpu.SemaphoreType.DMA((len(own),)),
        ],
        input_output_aliases={len(own) + 2: 1},
        compiler_params=params,
        cost_estimate=cost,
        name="mirror_late",
    )(target, *own, others[-1], picked)[0]


def shards(cores, chips, amplitudes, ladder_ints, tile_map, hole_ints, occ_energy, pair_list, mirror_row):
    rows, cols = amplitudes.shape
    integral_cols = ladder_ints.shape[1]
    vir_place = lax.axis_index("vir")
    occ_place = lax.axis_index("occ")
    members = chips // 2
    half_blocks = integral_cols // cols // 2
    side = vir_place % 2
    group = vir_place // 2
    across = [(v, v ^ 1) for v in range(chips)]

    evens = (members + 1) // 2
    order = [2 * p if p < evens else 2 * (members - p) - 1 for p in range(members)]
    forward, backward = [], []
    for s in range(2):
        for k in range(members):
            here, there = 2 * order[k] + s, 2 * order[(k + 1) % members] + s
            forward.append((here, there))
            backward.append((there, here))
    place = jnp.where(group % 2 == 0, group // 2, members - (group + 1) // 2)
    own_half = occ_place * half_blocks if cores == 2 else 0

    ring_steps = sorted([*range((members + 1) // 2), *range(-(members // 2), 0)], key=abs)

    ring_place = (place - jnp.array(ring_steps, jnp.int32)) % members
    ring_group = jnp.where(ring_place < evens, 2 * ring_place, 2 * (members - ring_place) - 1)
    tiles = cols // TILE

    def tile_index(row_block):
        parts_of = [(ring_group - own_half) % members, (2 * ring_group + side) * tiles, row_block[None] * tiles]
        return jnp.concatenate([part.astype(jnp.int32) for part in parts_of])

    def whole_k(a):
        if cores == 2:
            return [a, other_core(a)]
        return [lax.all_gather(a, "occ", axis=1, tiled=True)]

    chunks = row_chunks(rows, SHARES)
    if rows % 8 == 0:
        send, *mine = parts((1 - side)[None].astype(jnp.int32), ladder_ints, amplitudes, chunks)
    else:
        (send,) = parts((1 - side)[None].astype(jnp.int32), ladder_ints)
        mine = [amplitudes[start : start + length] for start, length in chunks]
    near = lax.ppermute(send, "vir", across)
    (kept,) = parts(side[None].astype(jnp.int32), ladder_ints)
    kept_all = prepare(tile_index(vir_place), tile_map, whole_k(kept), cols)
    near_all = prepare(tile_index(vir_place + 1 - 2 * side), tile_map, whole_k(near), cols)

    if cores == 2:
        both = jnp.zeros((2 * rows, cols), amplitudes.dtype)
        both = lax.dynamic_update_slice(both, amplitudes, (occ_place * rows, 0))
        both = lax.dynamic_update_slice(both, other_core(amplitudes), ((1 - occ_place) * rows, 0))
    else:
        both = lax.all_gather(amplitudes, "occ", axis=0, tiled=True)
    orbital_ids = jnp.arange(occ_energy.shape[0], dtype=jnp.int32)
    one_hot = (pair_list[:, :, None] == orbital_ids[None, None, :]).astype(jnp.float32)
    pair_energy = jnp.sum(one_hot * occ_energy[None, None, :], axis=(1, 2))
    base = jnp.dot(hole_ints, both, preferred_element_type=jnp.float32)
    base = base - pair_energy[:, None] * amplitudes.astype(jnp.float32)

    raws = []
    for index, (start, length) in enumerate(chunks):
        ups = members // 2 if index % 2 == 0 else (members - 1) // 2
        blocks = {0: mine[index]}
        for step in range(1, ups + 1):
            blocks[step] = lax.ppermute(blocks[step - 1], "vir", forward)
        for step in range(1, members - ups):
            blocks[-step] = lax.ppermute(blocks[1 - step], "vir", backward)
        arrived = [blocks[step] if step in blocks else blocks[step + members] for step in ring_steps]
        for_near = product(arrived, near_all)
        from_near = lax.ppermute(for_near, "vir", across)
        rest = product(arrived, kept_all, base, start)
        raws.append(rest + from_near)

    if cores == 2:
        others = [other_core(raw) for raw in raws]
        index = (mirror_row - occ_place * rows) % (2 * rows)
        if rows % 8 or len(chunks) < 2:
            return add_mirror(index, rows, raws, others)
        ahead = chunks[-1][0]
        late = jnp.concatenate([mirror_row[ahead:], other_core(mirror_row)[ahead:]])
        late = late - occ_place * rows
        target = jnp.where((late >= 0) & (late < rows), late, rows)
        index = jnp.where(index < ahead, index, index - rows + ahead)
        index = jnp.where(index >= 2 * ahead, 0, jnp.maximum(index, 0))
        return add_mirror_in_steps(index, target, rows, raws, others)
    own = jnp.concatenate(raws, axis=0)
    whole = lax.all_gather(own, "occ", axis=0, tiled=True)
    padded = -(-rows // 8) * 8
    own = jnp.pad(own, ((0, padded - rows), (0, 0)))
    return add_mirror(mirror_row + padded, rows, [own], [whole])


def solution(mesh):
    cores, chips = mesh.shape["occ"], mesh.shape["vir"]

    def body(*arrays):
        return shards(cores, chips, *arrays)

    return jax.shard_map(
        body,
        mesh=mesh,
        in_specs=(
            P("occ", "vir"),
            P("vir", "occ"),
            P(),
            P("occ", None),
            P(),
            P("occ", None),
            P("occ"),
        ),
        out_specs=P("occ", "vir"),
        check_vma=False,
    )
```

profile of v0, /device:TPU:0, one launch (start us, length us, event | category | flops | bytes accessed | tf_op | source)
XLA Modules:
  0.0 134.9 jit_solution(4696591853304032746)
XLA Ops:
  0.0 3.1 %parts.2 = (bf16[384,1536]{1,0:T(8,128)(2,1)}, bf16[360,384]{1,0:T(8,128)(2,1)}, bf16[320,384]{1,0:T(8,128)(2,1)}, bf16[256,384]{1,0:T(8,128)(2,1)}, bf16[192,384]{1,0:T(8,128)(2,1)}) custom-call(s32[1]{0:T(128)} %bitcast.side_ref, bf16[384,3072]{1,0:T(8,128)(2,1)} %refs_0_.3, bf16[1128,384]{1,0:T(8,128)(2,1)} %refs_1_.1), custom_call_target="tpu_custom_call" | custom-call | bytes 4718592 | tf_op jit(solution)/shard_map/parts/pallas_call | solution.py:63
  3.1 3.0 %collective-permute-start.10 = (bf16[384,1536]{1,0:T(8,128)(2,1)}, bf16[384,1536]{1,0:T(8,128)(2,1)}, u32[]{:S(2)}, u32[]{:S(2)}) collective-permute-start(bf16[384,1536]{1,0:T(8,128)(2,1)} %get-tuple-element.12), channel_id=1, source_target_pairs={{0,1},{1,0},{2,3},{3,2},{4,5},{5,4},{6,7},{7,6},{8,9},{9,8},{10,11... | collective-permute-start | bytes 3538952 | tf_op jit(solution)/shard_map/ppermute | solution.py:353
  6.1 1.6 %collective-permute-start.21 = (bf16[256,384]{1,0:T(8,128)(2,1)}, bf16[256,384]{1,0:T(8,128)(2,1)S(1)}, u32[]{:S(2)}, u32[]{:S(2)}) collective-permute-start(bf16[256,384]{1,0:T(8,128)(2,1)} %get-tuple-element.14.refs_0_), channel_id=1, source_target_pairs={{0,4},{4,8},{8,12},{12,14},{14,10},{10,6},{6,2},{2,0},{1,5},{5,9},... | collective-permute-start | bytes 589832 | tf_op jit(solution)/shard_map/ppermute | solution.py:375
  8.2 1.6 %collective-permute-start.29 = (bf16[192,384]{1,0:T(8,128)(2,1)}, bf16[192,384]{1,0:T(8,128)(2,1)S(1)}, u32[]{:S(2)}, u32[]{:S(2)}) collective-permute-start(bf16[192,384]{1,0:T(8,128)(2,1)} %get-tuple-element.15.refs_0_), channel_id=1, source_target_pairs={{0,4},{4,8},{8,12},{12,14},{14,10},{10,6},{6,2},{2,0},{1,5},{5,9},... | collective-permute-start | bytes 442376 | tf_op jit(solution)/shard_map/ppermute | solution.py:375
  10.2 4.5 %collective-permute-done.30.refs_2_ = bf16[192,384]{1,0:T(8,128)(2,1)S(1)} collective-permute-done((bf16[192,384]{1,0:T(8,128)(2,1)}, bf16[192,384]{1,0:T(8,128)(2,1)S(1)}, u32[]{:S(2)}, u32[]{:S(2)}) %collective-permute-start.30) | collective-permute-done | bytes 147488 | tf_op jit(solution)/shard_map/ppermute | solution.py:377
  14.7 1.6 %collective-permute-start.1 = (bf16[360,384]{1,0:T(8,128)(2,1)}, bf16[360,384]{1,0:T(8,128)(2,1)}, u32[]{:S(2)}, u32[]{:S(2)}) collective-permute-start(bf16[360,384]{1,0:T(8,128)(2,1)} %get-tuple-element.11.refs_0_), channel_id=1, source_target_pairs={{0,4},{4,8},{8,12},{12,14},{14,10},{10,6},{6,2},{2,0},{1,5},{5,9},... | collective-permute-start | bytes 829448 | tf_op jit(solution)/shard_map/ppermute | solution.py:375
  16.2 1.1 collective-permute-done.29.refs_1_
  17.3 1.5 %collective-permute-start.14 = (bf16[320,384]{1,0:T(8,128)(2,1)}, bf16[320,384]{1,0:T(8,128)(2,1)}, u32[]{:S(2)}, u32[]{:S(2)}) collective-permute-start(bf16[320,384]{1,0:T(8,128)(2,1)} %get-tuple-element.13.refs_0_), channel_id=1, source_target_pairs={{4,0},{8,4},{12,8},{14,12},{10,14},{6,10},{2,6},{0,2},{5,1},{9,5},... | collective-permute-start | bytes 737288 | tf_op jit(solution)/shard_map/ppermute | solution.py:377
  19.3 1.5 %collective-permute-start.2 = (bf16[360,384]{1,0:T(8,128)(2,1)}, bf16[360,384]{1,0:T(8,128)(2,1)}, u32[]{:S(2)}, u32[]{:S(2)}) collective-permute-start(bf16[360,384]{1,0:T(8,128)(2,1)} %get-tuple-element.11.refs_0_), channel_id=1, source_target_pairs={{4,0},{8,4},{12,8},{14,12},{10,14},{6,10},{2,6},{0,2},{5,1},{9,5},... | collective-permute-start | bytes 829448 | tf_op jit(solution)/shard_map/ppermute | solution.py:377
  20.8 5.0 %collective-permute-done.14.refs_2_ = bf16[320,384]{1,0:T(8,128)(2,1)} collective-permute-done((bf16[320,384]{1,0:T(8,128)(2,1)}, bf16[320,384]{1,0:T(8,128)(2,1)}, u32[]{:S(2)}, u32[]{:S(2)}) %collective-permute-start.14) | collective-permute-done | bytes 245792 | tf_op jit(solution)/shard_map/ppermute | solution.py:377
  25.8 1.6 %collective-permute-start.23 = (bf16[256,384]{1,0:T(8,128)(2,1)S(1)}, bf16[256,384]{1,0:T(8,128)(2,1)S(1)}, u32[]{:S(2)}, u32[]{:S(2)}) collective-permute-start(bf16[256,384]{1,0:T(8,128)(2,1)S(1)} %collective-permute-done.21.refs_1_), channel_id=1, source_target_pairs={{0,4},{4,8},{8,12},{12,14},{14,10},{10,6},{6,2},{2,0},{1,5},{5,9},... | collective-permute-start | bytes 589832 | tf_op jit(solution)/shard_map/ppermute | solution.py:375
  28.1 1.2 collective-permute-done.13.refs_1_
  29.3 0.9 collective-permute-start.32
  30.8 1.1 collective-permute-start.31
  32.6 0.9 collective-permute-start.24
  34.2 1.8 %collective-permute-done.32.refs_4_ = bf16[192,384]{1,0:T(8,128)(2,1)S(1)} collective-permute-done((bf16[192,384]{1,0:T(8,128)(2,1)S(1)}, bf16[192,384]{1,0:T(8,128)(2,1)S(1)}, u32[]{:S(2)}, u32[]{:S(2)}) %collective-permute-start.32) | collective-permute-done | bytes 147488 | tf_op jit(solution)/shard_map/ppermute | solution.py:377
  36.0 0.9 collective-permute-start.16
  36.9 1.1 collective-permute-start.15
  38.0 1.0 collective-permute-start.34
  39.7 1.2 collective-permute-start.3
  40.9 4.7 %collective-permute-done.34.refs_6_ = bf16[192,384]{1,0:T(8,128)(2,1)S(1)} collective-permute-done((bf16[192,384]{1,0:T(8,128)(2,1)S(1)}, bf16[192,384]{1,0:T(8,128)(2,1)S(1)}, u32[]{:S(2)}, u32[]{:S(2)}) %collective-permute-start.34) | collective-permute-done | bytes 147488 | tf_op jit(solution)/shard_map/ppermute | solution.py:377
  46.2 1.4 %collective-permute-start.4 = (bf16[360,384]{1,0:T(8,128)(2,1)}, bf16[360,384]{1,0:T(8,128)(2,1)}, u32[]{:S(2)}, u32[]{:S(2)}) collective-permute-start(bf16[360,384]{1,0:T(8,128)(2,1)} %collective-permute-done.2.refs_2_), channel_id=1, source_target_pairs={{4,0},{8,4},{12,8},{14,12},{10,14},{6,10},{2,6},{0,2},{5,1},{9,5},... | collective-permute-start | bytes 829448 | tf_op jit(solution)/shard_map/ppermute | solution.py:377
  49.5 4.7 %collective-permute-done.4.refs_4_ = bf16[360,384]{1,0:T(8,128)(2,1)} collective-permute-done((bf16[360,384]{1,0:T(8,128)(2,1)}, bf16[360,384]{1,0:T(8,128)(2,1)}, u32[]{:S(2)}, u32[]{:S(2)}) %collective-permute-start.4) | collective-permute-done | bytes 276512 | tf_op jit(solution)/shard_map/ppermute | solution.py:377
  55.4 1.6 %collective-permute-start.18 = (bf16[320,384]{1,0:T(8,128)(2,1)}, bf16[320,384]{1,0:T(8,128)(2,1)}, u32[]{:S(2)}, u32[]{:S(2)}) collective-permute-start(bf16[320,384]{1,0:T(8,128)(2,1)} %collective-permute-done.16.refs_4_), channel_id=1, source_target_pairs={{4,0},{8,4},{12,8},{14,12},{10,14},{6,10},{2,6},{0,2},{5,1},{9,5},... | collective-permute-start | bytes 737288 | tf_op jit(solution)/shard_map/ppermute | solution.py:377
  57.2 5.0 %collective-permute-done.26.refs_6_ = bf16[256,384]{1,0:T(8,128)(2,1)S(1)} collective-permute-done((bf16[256,384]{1,0:T(8,128)(2,1)}, bf16[256,384]{1,0:T(8,128)(2,1)S(1)}, u32[]{:S(2)}, u32[]{:S(2)}) %collective-permute-start.26) | collective-permute-done | bytes 196640 | tf_op jit(solution)/shard_map/ppermute | solution.py:377
  62.9 1.7 %collective-permute-start.5 = (bf16[360,384]{1,0:T(8,128)(2,1)}, bf16[360,384]{1,0:T(8,128)(2,1)S(1)}, u32[]{:S(2)}, u32[]{:S(2)}) collective-permute-start(bf16[360,384]{1,0:T(8,128)(2,1)} %collective-permute-done.3.refs_3_), channel_id=1, source_target_pairs={{0,4},{4,8},{8,12},{12,14},{14,10},{10,6},{6,2},{2,0},{1,5},{5,9},... | collective-permute-start | bytes 829448 | tf_op jit(solution)/shard_map/ppermute | solution.py:375
  65.3 1.6 %collective-permute-start.27 = (bf16[256,384]{1,0:T(8,128)(2,1)S(1)}, bf16[256,384]{1,0:T(8,128)(2,1)S(1)}, u32[]{:S(2)}, u32[]{:S(2)}) collective-permute-start(bf16[256,384]{1,0:T(8,128)(2,1)S(1)} %collective-permute-done.25.refs_5_), channel_id=1, source_target_pairs={{0,4},{4,8},{8,12},{12,14},{14,10},{10,6},{6,2},{2,0},{1,5},{5,9},... | collective-permute-start | bytes 589832 | tf_op jit(solution)/shard_map/ppermute | solution.py:375
  67.2 6.0 %collective-permute-done.27.refs_7_ = bf16[256,384]{1,0:T(8,128)(2,1)S(1)} collective-permute-done((bf16[256,384]{1,0:T(8,128)(2,1)S(1)}, bf16[256,384]{1,0:T(8,128)(2,1)S(1)}, u32[]{:S(2)}, u32[]{:S(2)}) %collective-permute-start.27) | collective-permute-done | bytes 196640 | tf_op jit(solution)/shard_map/ppermute | solution.py:375
  73.2 2.5 %collective-permute-start.17 = (bf16[320,384]{1,0:T(8,128)(2,1)}, bf16[320,384]{1,0:T(8,128)(2,1)S(1)}, u32[]{:S(2)}, u32[]{:S(2)}) collective-permute-start(bf16[320,384]{1,0:T(8,128)(2,1)} %collective-permute-done.15.refs_3_), channel_id=1, source_target_pairs={{0,4},{4,8},{8,12},{12,14},{14,10},{10,6},{6,2},{2,0},{1,5},{5,9},... | collective-permute-start | bytes 737288 | tf_op jit(solution)/shard_map/ppermute | solution.py:375
  75.8 1.9 %collective-permute-start.7 = (bf16[360,384]{1,0:T(8,128)(2,1)S(1)}, bf16[360,384]{1,0:T(8,128)(2,1)S(1)}, u32[]{:S(2)}, u32[]{:S(2)}) collective-permute-start(bf16[360,384]{1,0:T(8,128)(2,1)S(1)} %collective-permute-done.5.refs_5_), channel_id=1, source_target_pairs={{0,4},{4,8},{8,12},{12,14},{14,10},{10,6},{6,2},{2,0},{1,5},{5,9},... | collective-permute-start | bytes 829448 | tf_op jit(solution)/shard_map/ppermute | solution.py:375
  77.8 1.3 constant_dynamic-update-slice_fusion
  79.2 4.0 %prepare.3.refs_8_ = bf16[3072,384]{1,0:T(8,128)(2,1)S(1)} custom-call(s32[17]{0:T(128)S(1)} %get-tuple-element.19.index_ref, s32[48,48]{1,0:T(8,128)S(1)} %copy-done.27, bf16[384,1536]{1,0:T(8,128)(2,1)} %collective-permute-done.10.refs_0_, bf16[384,1536]{1,0:T(8,128)(2,1)} %collective-permute-done.11.refs_1_), custom_call_target="tpu_custom_call" | custom-call | bytes 4718592 | tf_op jit(solution)/shard_map/prepare/pallas_call | solution.py:103
  83.3 1.0 product.13
  84.3 2.0 %collective-permute-start.33 = (bf16[192,384]{1,0:T(8,128)(2,1)S(1)}, bf16[192,384]{1,0:T(8,128)(2,1)S(1)}, u32[]{:S(2)}, u32[]{:S(2)}) collective-permute-start(bf16[192,384]{1,0:T(8,128)(2,1)S(1)} %copy-done.24), channel_id=1, source_target_pairs={{0,4},{4,8},{8,12},{12,14},{14,10},{10,6},{6,2},{2,0},{1,5},{5,9},... | collective-permute-start | bytes 442376 | tf_op jit(solution)/shard_map/ppermute | solution.py:375
  87.0 2.6 %product.11 = f32[320,384]{1,0:T(8,128)S(1)} custom-call(bf16[320,384]{1,0:T(8,128)(2,1)S(1)} %copy-done.2, bf16[320,384]{1,0:T(8,128)(2,1)} %collective-permute-done.13.refs_1_, bf16[320,384]{1,0:T(8,128)(2,1)} %collective-permute-done.14.refs_2_, bf16[320,384]{1,0:T(8,128)(2,1)} %collective-permute-done.15.refs_3_, ...), custom_call_target="tpu_custom_call" | custom-call | flops 754974720 | bytes 4325376 | tf_op jit(solution)/shard_map/product/pallas_call | solution.py:130
  90.0 1.6 %collective-permute-start.20 = (f32[320,384]{1,0:T(8,128)S(1)}, f32[320,384]{1,0:T(8,128)S(1)}, u32[]{:S(2)}, u32[]{:S(2)}) collective-permute-start(f32[320,384]{1,0:T(8,128)S(1)} %product.11), channel_id=1, source_target_pairs={{0,1},{1,0},{2,3},{3,2},{4,5},{5,4},{6,7},{7,6},{8,9},{9,8},{10,11... | collective-permute-start | bytes 1474568 | tf_op jit(solution)/shard_map/ppermute | solution.py:380
  91.6 2.5 %product.9 = f32[360,384]{1,0:T(8,128)S(1)} custom-call(bf16[360,384]{1,0:T(8,128)(2,1)S(1)} %copy-done.1, bf16[360,384]{1,0:T(8,128)(2,1)} %collective-permute-done.1.refs_1_, bf16[360,384]{1,0:T(8,128)(2,1)} %collective-permute-done.2.refs_2_, bf16[360,384]{1,0:T(8,128)(2,1)} %collective-permute-done.3.refs_3_, ...), custom_call_target="tpu_custom_call" | custom-call | flops 849346560 | bytes 4571136 | tf_op jit(solution)/shard_map/product/pallas_call | solution.py:130
  94.7 2.9 %fusion.refs_9_ = f32[1128,384]{1,0:T(8,128)S(1)} fusion(bf16[2256,384]{1,0:T(8,128)(2,1)S(1)} %constant_dynamic-update-slice_fusion, bf16[1128,2256]{1,0:T(8,128)(2,1)S(1)} %bitcast.11, bf16[1128,384]{1,0:T(8,128)(2,1)S(1)} %copy-done.28, f32[1128]{0:T(1024)S(1)} %select_reduce_fusion), kind=kOutput, calls=%fused_computation.1 | convolution fusion | flops 1955681280 | bytes 9425568 | tf_op jit(solution)/shard_map/dot_general | solution.py:367
  97.6 2.9 %prepare.2.refs_8_ = bf16[3072,384]{1,0:T(8,128)(2,1)S(1)} custom-call(s32[17]{0:T(128)S(1)} %get-tuple-element.20.index_ref, s32[48,48]{1,0:T(8,128)S(1)} %copy-done.27, bf16[384,1536]{1,0:T(8,128)(2,1)S(1)} %parts.3.refs_0_, bf16[384,1536]{1,0:T(8,128)(2,1)S(1)} %collective-permute-done.8.refs_1_), custom_call_target="tpu_custom_call" | custom-call | bytes 4718592 | tf_op jit(solution)/shard_map/prepare/pallas_call | solution.py:103
  100.6 0.8 product.15
  101.4 1.7 %collective-permute-start.36 = (f32[192,384]{1,0:T(8,128)S(1)}, f32[192,384]{1,0:T(8,128)S(1)}, u32[]{:S(2)}, u32[]{:S(2)}) collective-permute-start(f32[192,384]{1,0:T(8,128)S(1)} %product.15), channel_id=1, source_target_pairs={{0,1},{1,0},{2,3},{3,2},{4,5},{5,4},{6,7},{7,6},{8,9},{9,8},{10,11... | collective-permute-start | bytes 884744 | tf_op jit(solution)/shard_map/ppermute | solution.py:380
  103.1 2.5 %product.8 = f32[360,384]{1,0:T(8,128)S(1)} custom-call(bf16[360,384]{1,0:T(8,128)(2,1)S(1)} %copy-done.1, bf16[360,384]{1,0:T(8,128)(2,1)} %collective-permute-done.1.refs_1_, bf16[360,384]{1,0:T(8,128)(2,1)} %collective-permute-done.2.refs_2_, bf16[360,384]{1,0:T(8,128)(2,1)} %collective-permute-done.3.refs_3_, ...), custom_call_target="tpu_custom_call" | custom-call | flops 849346560 | bytes 4571136 | tf_op jit(solution)/shard_map/product/pallas_call | solution.py:130
  105.6 15.5 %collective-permute-done.12 = f32[360,384]{1,0:T(8,128)S(1)} collective-permute-done((f32[360,384]{1,0:T(8,128)S(1)}, f32[360,384]{1,0:T(8,128)S(1)}, u32[]{:S(2)}, u32[]{:S(2)}) %collective-permute-start.12) | collective-permute-done | bytes 552992 | tf_op jit(solution)/shard_map/ppermute | solution.py:380
  121.3 2.6 %product.10 = f32[320,384]{1,0:T(8,128)S(1)} custom-call(bf16[320,384]{1,0:T(8,128)(2,1)S(1)} %copy-done.2, bf16[320,384]{1,0:T(8,128)(2,1)} %collective-permute-done.13.refs_1_, bf16[320,384]{1,0:T(8,128)(2,1)} %collective-permute-done.14.refs_2_, bf16[320,384]{1,0:T(8,128)(2,1)} %collective-permute-done.15.refs_3_, ...), custom_call_target="tpu_custom_call" | custom-call | flops 754974720 | bytes 4325376 | tf_op jit(solution)/shard_map/product/pallas_call | solution.py:130
  124.5 1.0 product.12
  126.1 0.8 product.14
  127.5 3.9 %mirror_early.1.refs_5_ = f32[1136,3,128]{2,1,0:T(4,128)S(1)} custom-call(s32[1128]{0:T(1024)S(1)} %maximum_select_fusion.index_ref, f32[360,384]{1,0:T(8,128)S(1)} %add.79.refs_0_, f32[320,384]{1,0:T(8,128)S(1)} %add.80.refs_1_, f32[256,384]{1,0:T(8,128)S(1)} %add.81.refs_2_, f32[360,384]{1,0:T(8,128)S(1)} %collective-permute-done.38.refs_3_, ...), custom_call_target="tpu_custom_call" | custom-call | flops 433152 | bytes 5197824 | tf_op jit(solution)/shard_map/mirror_early/pallas_call | solution.py:283
  131.5 3.3 %mirror_late.1 = (f32[1128,384]{1,0:T(8,128)}, f32[1136,3,128]{2,1,0:T(4,128)S(1)}) custom-call(s32[384]{0:T(512)S(1)} %and_select_fusion.2.target_ref, f32[360,384]{1,0:T(8,128)S(1)} %add.79.refs_0_, f32[320,384]{1,0:T(8,128)S(1)} %add.80.refs_1_, f32[256,384]{1,0:T(8,128)S(1)} %add.81.refs_2_, ...), custom_call_target="tpu_custom_call", output_to_operand_aliasing={{1}: (6, {})} | custom-call | flops 433152 | bytes 5197824 | tf_op jit(solution)/shard_map/mirror_late/pallas_call | solution.py:293
  (133 shorter events, 14.2 us)
Async XLA Ops:
  0.0 47.6 %copy-start = (bf16[384,3072]{1,0:T(8,128)(2,1)S(1)}, bf16[384,3072]{1,0:T(8,128)(2,1)}, u32[]{:S(2)}) copy-start(bf16[384,3072]{1,0:T(8,128)(2,1)} %refs_0_.3) | copy-start | bytes 7077892
  3.1 34.9 %collective-permute-start.10 = (bf16[384,1536]{1,0:T(8,128)(2,1)}, bf16[384,1536]{1,0:T(8,128)(2,1)}, u32[]{:S(2)}, u32[]{:S(2)}) collective-permute-start(bf16[384,1536]{1,0:T(8,128)(2,1)} %get-tuple-element.12), channel_id=1, source_target_pairs={{0,1},{1,0},{2,3},{3,2},{4,5},{5,4},{6,7},{7,6},{8,9},{9,8},{10,11... | collective-permute-start | bytes 3538952 | tf_op jit(solution)/shard_map/ppermute | solution.py:353
  6.1 12.7 %collective-permute-start.21 = (bf16[256,384]{1,0:T(8,128)(2,1)}, bf16[256,384]{1,0:T(8,128)(2,1)S(1)}, u32[]{:S(2)}, u32[]{:S(2)}) collective-permute-start(bf16[256,384]{1,0:T(8,128)(2,1)} %get-tuple-element.14.refs_0_), channel_id=1, source_target_pairs={{0,4},{4,8},{8,12},{12,14},{14,10},{10,6},{6,2},{2,0},{1,5},{5,9},... | collective-permute-start | bytes 589832 | tf_op jit(solution)/shard_map/ppermute | solution.py:375
  7.7 6.9 %collective-permute-start.30 = (bf16[192,384]{1,0:T(8,128)(2,1)}, bf16[192,384]{1,0:T(8,128)(2,1)S(1)}, u32[]{:S(2)}, u32[]{:S(2)}) collective-permute-start(bf16[192,384]{1,0:T(8,128)(2,1)} %get-tuple-element.15.refs_0_), channel_id=1, source_target_pairs={{4,0},{8,4},{12,8},{14,12},{10,14},{6,10},{2,6},{0,2},{5,1},{9,5},... | collective-permute-start | bytes 442376 | tf_op jit(solution)/shard_map/ppermute | solution.py:377
  8.2 9.1 %collective-permute-start.29 = (bf16[192,384]{1,0:T(8,128)(2,1)}, bf16[192,384]{1,0:T(8,128)(2,1)S(1)}, u32[]{:S(2)}, u32[]{:S(2)}) collective-permute-start(bf16[192,384]{1,0:T(8,128)(2,1)} %get-tuple-element.15.refs_0_), channel_id=1, source_target_pairs={{0,4},{4,8},{8,12},{12,14},{14,10},{10,6},{6,2},{2,0},{1,5},{5,9},... | collective-permute-start | bytes 442376 | tf_op jit(solution)/shard_map/ppermute | solution.py:375
  9.7 9.6 %collective-permute-start.22 = (bf16[256,384]{1,0:T(8,128)(2,1)}, bf16[256,384]{1,0:T(8,128)(2,1)S(1)}, u32[]{:S(2)}, u32[]{:S(2)}) collective-permute-start(bf16[256,384]{1,0:T(8,128)(2,1)} %get-tuple-element.14.refs_0_), channel_id=1, source_target_pairs={{4,0},{8,4},{12,8},{14,12},{10,14},{6,10},{2,6},{0,2},{5,1},{9,5},... | collective-permute-start | bytes 589832 | tf_op jit(solution)/shard_map/ppermute | solution.py:377
  14.7 16.2 %collective-permute-start.1 = (bf16[360,384]{1,0:T(8,128)(2,1)}, bf16[360,384]{1,0:T(8,128)(2,1)}, u32[]{:S(2)}, u32[]{:S(2)}) collective-permute-start(bf16[360,384]{1,0:T(8,128)(2,1)} %get-tuple-element.11.refs_0_), channel_id=1, source_target_pairs={{0,4},{4,8},{8,12},{12,14},{14,10},{10,6},{6,2},{2,0},{1,5},{5,9},... | collective-permute-start | bytes 829448 | tf_op jit(solution)/shard_map/ppermute | solution.py:375
  17.3 8.5 %collective-permute-start.14 = (bf16[320,384]{1,0:T(8,128)(2,1)}, bf16[320,384]{1,0:T(8,128)(2,1)}, u32[]{:S(2)}, u32[]{:S(2)}) collective-permute-start(bf16[320,384]{1,0:T(8,128)(2,1)} %get-tuple-element.13.refs_0_), channel_id=1, source_target_pairs={{4,0},{8,4},{12,8},{14,12},{10,14},{6,10},{2,6},{0,2},{5,1},{9,5},... | collective-permute-start | bytes 737288 | tf_op jit(solution)/shard_map/ppermute | solution.py:377
  18.8 10.5 %collective-permute-start.13 = (bf16[320,384]{1,0:T(8,128)(2,1)}, bf16[320,384]{1,0:T(8,128)(2,1)}, u32[]{:S(2)}, u32[]{:S(2)}) collective-permute-start(bf16[320,384]{1,0:T(8,128)(2,1)} %get-tuple-element.13.refs_0_), channel_id=1, source_target_pairs={{0,4},{4,8},{8,12},{12,14},{14,10},{10,6},{6,2},{2,0},{1,5},{5,9},... | collective-permute-start | bytes 737288 | tf_op jit(solution)/shard_map/ppermute | solution.py:375
  19.3 13.3 %collective-permute-start.2 = (bf16[360,384]{1,0:T(8,128)(2,1)}, bf16[360,384]{1,0:T(8,128)(2,1)}, u32[]{:S(2)}, u32[]{:S(2)}) collective-permute-start(bf16[360,384]{1,0:T(8,128)(2,1)} %get-tuple-element.11.refs_0_), channel_id=1, source_target_pairs={{4,0},{8,4},{12,8},{14,12},{10,14},{6,10},{2,6},{0,2},{5,1},{9,5},... | collective-permute-start | bytes 829448 | tf_op jit(solution)/shard_map/ppermute | solution.py:377
  25.8 12.2 %collective-permute-start.23 = (bf16[256,384]{1,0:T(8,128)(2,1)S(1)}, bf16[256,384]{1,0:T(8,128)(2,1)S(1)}, u32[]{:S(2)}, u32[]{:S(2)}) collective-permute-start(bf16[256,384]{1,0:T(8,128)(2,1)S(1)} %collective-permute-done.21.refs_1_), channel_id=1, source_target_pairs={{0,4},{4,8},{8,12},{12,14},{14,10},{10,6},{6,2},{2,0},{1,5},{5,9},... | collective-permute-start | bytes 589832 | tf_op jit(solution)/shard_map/ppermute | solution.py:375
  29.3 6.7 %collective-permute-start.32 = (bf16[192,384]{1,0:T(8,128)(2,1)S(1)}, bf16[192,384]{1,0:T(8,128)(2,1)S(1)}, u32[]{:S(2)}, u32[]{:S(2)}) collective-permute-start(bf16[192,384]{1,0:T(8,128)(2,1)S(1)} %collective-permute-done.30.refs_2_), channel_id=1, source_target_pairs={{4,0},{8,4},{12,8},{14,12},{10,14},{6,10},{2,6},{0,2},{5,1},{9,5},... | collective-permute-start | bytes 442376 | tf_op jit(solution)/shard_map/ppermute | solution.py:377
  30.8 6.1 %collective-permute-start.31 = (bf16[192,384]{1,0:T(8,128)(2,1)S(1)}, bf16[192,384]{1,0:T(8,128)(2,1)S(1)}, u32[]{:S(2)}, u32[]{:S(2)}) collective-permute-start(bf16[192,384]{1,0:T(8,128)(2,1)S(1)} %collective-permute-done.29.refs_1_), channel_id=1, source_target_pairs={{0,4},{4,8},{8,12},{12,14},{14,10},{10,6},{6,2},{2,0},{1,5},{5,9},... | collective-permute-start | bytes 442376 | tf_op jit(solution)/shard_map/ppermute | solution.py:375
  32.6 7.0 %collective-permute-start.24 = (bf16[256,384]{1,0:T(8,128)(2,1)S(1)}, bf16[256,384]{1,0:T(8,128)(2,1)S(1)}, u32[]{:S(2)}, u32[]{:S(2)}) collective-permute-start(bf16[256,384]{1,0:T(8,128)(2,1)S(1)} %collective-permute-done.22.refs_2_), channel_id=1, source_target_pairs={{4,0},{8,4},{12,8},{14,12},{10,14},{6,10},{2,6},{0,2},{5,1},{9,5},... | collective-permute-start | bytes 589832 | tf_op jit(solution)/shard_map/ppermute | solution.py:377
  36.0 11.8 %collective-permute-start.16 = (bf16[320,384]{1,0:T(8,128)(2,1)}, bf16[320,384]{1,0:T(8,128)(2,1)}, u32[]{:S(2)}, u32[]{:S(2)}) collective-permute-start(bf16[320,384]{1,0:T(8,128)(2,1)} %collective-permute-done.14.refs_2_), channel_id=1, source_target_pairs={{4,0},{8,4},{12,8},{14,12},{10,14},{6,10},{2,6},{0,2},{5,1},{9,5},... | collective-permute-start | bytes 737288 | tf_op jit(solution)/shard_map/ppermute | solution.py:377
  36.9 11.0 %collective-permute-start.15 = (bf16[320,384]{1,0:T(8,128)(2,1)}, bf16[320,384]{1,0:T(8,128)(2,1)}, u32[]{:S(2)}, u32[]{:S(2)}) collective-permute-start(bf16[320,384]{1,0:T(8,128)(2,1)} %collective-permute-done.13.refs_1_), channel_id=1, source_target_pairs={{0,4},{4,8},{8,12},{12,14},{14,10},{10,6},{6,2},{2,0},{1,5},{5,9},... | collective-permute-start | bytes 737288 | tf_op jit(solution)/shard_map/ppermute | solution.py:375
  38.0 37.8 %collective-permute-start.11 = (bf16[384,1536]{1,0:T(8,128)(2,1)}, bf16[384,1536]{1,0:T(8,128)(2,1)}, u32[]{:S(2)}, u32[]{:S(2)}) collective-permute-start(bf16[384,1536]{1,0:T(8,128)(2,1)} %collective-permute-done.10.refs_0_), channel_id=1, source_target_pairs={{0,16},{16,0},{1,17},{17,1},{2,18},{18,2},{3,19},{19,3},{4,20},{20... | collective-permute-start | bytes 3538952 | tf_op jit(solution)/shard_map/ppermute | solution.py:32
  38.0 7.5 %collective-permute-start.34 = (bf16[192,384]{1,0:T(8,128)(2,1)S(1)}, bf16[192,384]{1,0:T(8,128)(2,1)S(1)}, u32[]{:S(2)}, u32[]{:S(2)}) collective-permute-start(bf16[192,384]{1,0:T(8,128)(2,1)S(1)} %collective-permute-done.32.refs_4_), channel_id=1, source_target_pairs={{4,0},{8,4},{12,8},{14,12},{10,14},{6,10},{2,6},{0,2},{5,1},{9,5},... | collective-permute-start | bytes 442376 | tf_op jit(solution)/shard_map/ppermute | solution.py:377
  39.7 9.7 %collective-permute-start.3 = (bf16[360,384]{1,0:T(8,128)(2,1)}, bf16[360,384]{1,0:T(8,128)(2,1)}, u32[]{:S(2)}, u32[]{:S(2)}) collective-permute-start(bf16[360,384]{1,0:T(8,128)(2,1)} %collective-permute-done.1.refs_1_), channel_id=1, source_target_pairs={{0,4},{4,8},{8,12},{12,14},{14,10},{10,6},{6,2},{2,0},{1,5},{5,9},... | collective-permute-start | bytes 829448 | tf_op jit(solution)/shard_map/ppermute | solution.py:375
  46.2 8.0 %collective-permute-start.4 = (bf16[360,384]{1,0:T(8,128)(2,1)}, bf16[360,384]{1,0:T(8,128)(2,1)}, u32[]{:S(2)}, u32[]{:S(2)}) collective-permute-start(bf16[360,384]{1,0:T(8,128)(2,1)} %collective-permute-done.2.refs_2_), channel_id=1, source_target_pairs={{4,0},{8,4},{12,8},{14,12},{10,14},{6,10},{2,6},{0,2},{5,1},{9,5},... | collective-permute-start | bytes 829448 | tf_op jit(solution)/shard_map/ppermute | solution.py:377
  47.6 9.5 %copy-start.30 = (s32[1128,2]{0,1:T(2,128)S(1)}, s32[1128,2]{0,1:T(2,128)}, u32[]{:S(2)}) copy-start(s32[1128,2]{0,1:T(2,128)} %param.13) | copy-start | bytes 27076
  47.6 9.5 %copy-start.31 = (f32[48]{0:T(128)S(1)}, f32[48]{0:T(128)}, u32[]{:S(2)}) copy-start(f32[48]{0:T(128)} %param.12) | copy-start | bytes 580
  47.8 27.8 %collective-permute-start.9 = (bf16[1128,384]{1,0:T(8,128)(2,1)}, bf16[1128,384]{1,0:T(8,128)(2,1)}, u32[]{:S(2)}, u32[]{:S(2)}) collective-permute-start(bf16[1128,384]{1,0:T(8,128)(2,1)} %refs_1_.1), channel_id=1, source_target_pairs={{0,16},{16,0},{1,17},{17,1},{2,18},{18,2},{3,19},{19,3},{4,20},{20... | collective-permute-start | bytes 2598920 | tf_op jit(solution)/shard_map/ppermute | solution.py:32
  47.9 7.5 %collective-permute-start.25 = (bf16[256,384]{1,0:T(8,128)(2,1)}, bf16[256,384]{1,0:T(8,128)(2,1)S(1)}, u32[]{:S(2)}, u32[]{:S(2)}) collective-permute-start(bf16[256,384]{1,0:T(8,128)(2,1)} %copy-done.8), channel_id=1, source_target_pairs={{0,4},{4,8},{8,12},{12,14},{14,10},{10,6},{6,2},{2,0},{1,5},{5,9},... | collective-permute-start | bytes 589832 | tf_op jit(solution)/shard_map/ppermute | solution.py:375
  49.3 44.8 %collective-permute-start.8 = (bf16[384,1536]{1,0:T(8,128)(2,1)S(1)}, bf16[384,1536]{1,0:T(8,128)(2,1)S(1)}, u32[]{:S(2)}, u32[]{:S(2)}) collective-permute-start(bf16[384,1536]{1,0:T(8,128)(2,1)S(1)} %parts.3.refs_0_), channel_id=1, source_target_pairs={{0,16},{16,0},{1,17},{17,1},{2,18},{18,2},{3,19},{19,3},{4,20},{20... | collective-permute-start | bytes 3538952 | tf_op jit(solution)/shard_map/ppermute | solution.py:32
  54.2 8.0 %collective-permute-start.26 = (bf16[256,384]{1,0:T(8,128)(2,1)}, bf16[256,384]{1,0:T(8,128)(2,1)S(1)}, u32[]{:S(2)}, u32[]{:S(2)}) collective-permute-start(bf16[256,384]{1,0:T(8,128)(2,1)} %copy-done.10), channel_id=1, source_target_pairs={{4,0},{8,4},{12,8},{14,12},{10,14},{6,10},{2,6},{0,2},{5,1},{9,5},... | collective-permute-start | bytes 589832 | tf_op jit(solution)/shard_map/ppermute | solution.py:377
  55.4 11.8 %copy-start.12 = (bf16[256,384]{1,0:T(8,128)(2,1)}, bf16[256,384]{1,0:T(8,128)(2,1)S(1)}, u32[]{:S(2)}) copy-start(bf16[256,384]{1,0:T(8,128)(2,1)S(1)} %collective-permute-done.25.refs_5_) | copy-start | bytes 589828
  55.4 9.9 %collective-permute-start.18 = (bf16[320,384]{1,0:T(8,128)(2,1)}, bf16[320,384]{1,0:T(8,128)(2,1)}, u32[]{:S(2)}, u32[]{:S(2)}) collective-permute-start(bf16[320,384]{1,0:T(8,128)(2,1)} %collective-permute-done.16.refs_4_), channel_id=1, source_target_pairs={{4,0},{8,4},{12,8},{14,12},{10,14},{6,10},{2,6},{0,2},{5,1},{9,5},... | collective-permute-start | bytes 737288 | tf_op jit(solution)/shard_map/ppermute | solution.py:377
  62.9 12.7 %collective-permute-start.5 = (bf16[360,384]{1,0:T(8,128)(2,1)}, bf16[360,384]{1,0:T(8,128)(2,1)S(1)}, u32[]{:S(2)}, u32[]{:S(2)}) collective-permute-start(bf16[360,384]{1,0:T(8,128)(2,1)} %collective-permute-done.3.refs_3_), channel_id=1, source_target_pairs={{0,4},{4,8},{8,12},{12,14},{14,10},{10,6},{6,2},{2,0},{1,5},{5,9},... | collective-permute-start | bytes 829448 | tf_op jit(solution)/shard_map/ppermute | solution.py:375
  65.3 7.9 %collective-permute-start.27 = (bf16[256,384]{1,0:T(8,128)(2,1)S(1)}, bf16[256,384]{1,0:T(8,128)(2,1)S(1)}, u32[]{:S(2)}, u32[]{:S(2)}) collective-permute-start(bf16[256,384]{1,0:T(8,128)(2,1)S(1)} %collective-permute-done.25.refs_5_), channel_id=1, source_target_pairs={{0,4},{4,8},{8,12},{12,14},{14,10},{10,6},{6,2},{2,0},{1,5},{5,9},... | collective-permute-start | bytes 589832 | tf_op jit(solution)/shard_map/ppermute | solution.py:375
  67.0 12.1 %copy-start.27 = (s32[48,48]{1,0:T(8,128)S(1)}, s32[48,48]{1,0:T(8,128)}, u32[]{:S(2)}) copy-start(s32[48,48]{1,0:T(8,128)} %map_hbm.3) | copy-start | bytes 27652
  73.2 11.1 %collective-permute-start.17 = (bf16[320,384]{1,0:T(8,128)(2,1)}, bf16[320,384]{1,0:T(8,128)(2,1)S(1)}, u32[]{:S(2)}, u32[]{:S(2)}) collective-permute-start(bf16[320,384]{1,0:T(8,128)(2,1)} %collective-permute-done.15.refs_3_), channel_id=1, source_target_pairs={{0,4},{4,8},{8,12},{12,14},{14,10},{10,6},{6,2},{2,0},{1,5},{5,9},... | collective-permute-start | bytes 737288 | tf_op jit(solution)/shard_map/ppermute | solution.py:375
  75.7 13.9 %collective-permute-start.6 = (bf16[360,384]{1,0:T(8,128)(2,1)}, bf16[360,384]{1,0:T(8,128)(2,1)S(1)}, u32[]{:S(2)}, u32[]{:S(2)}) collective-permute-start(bf16[360,384]{1,0:T(8,128)(2,1)} %collective-permute-done.4.refs_4_), channel_id=1, source_target_pairs={{4,0},{8,4},{12,8},{14,12},{10,14},{6,10},{2,6},{0,2},{5,1},{9,5},... | collective-permute-start | bytes 829448 | tf_op jit(solution)/shard_map/ppermute | solution.py:377
  75.7 10.9 %collective-permute-start.19 = (bf16[320,384]{1,0:T(8,128)(2,1)}, bf16[320,384]{1,0:T(8,128)(2,1)S(1)}, u32[]{:S(2)}, u32[]{:S(2)}) collective-permute-start(bf16[320,384]{1,0:T(8,128)(2,1)} %collective-permute-done.18.refs_6_), channel_id=1, source_target_pairs={{4,0},{8,4},{12,8},{14,12},{10,14},{6,10},{2,6},{0,2},{5,1},{9,5},... | collective-permute-start | bytes 737288 | tf_op jit(solution)/shard_map/ppermute | solution.py:377
  75.8 14.2 %collective-permute-start.7 = (bf16[360,384]{1,0:T(8,128)(2,1)S(1)}, bf16[360,384]{1,0:T(8,128)(2,1)S(1)}, u32[]{:S(2)}, u32[]{:S(2)}) collective-permute-start(bf16[360,384]{1,0:T(8,128)(2,1)S(1)} %collective-permute-done.5.refs_5_), channel_id=1, source_target_pairs={{0,4},{4,8},{8,12},{12,14},{14,10},{10,6},{6,2},{2,0},{1,5},{5,9},... | collective-permute-start | bytes 829448 | tf_op jit(solution)/shard_map/ppermute | solution.py:375
  83.2 11.4 %slice-start = ((s8[5197824]{0:T(1024)(128)(4,1)}), s8[4194304]{0:T(1024)(128)(4,1)S(1)}, s32[]{:S(2)}) async-start(s8[5197824]{0:T(1024)(128)(4,1)} %bitcast.10), calls=%async_computation | async-start | bytes 8388608
  84.2 10.4 %slice-start.1 = ((s8[5197824]{0:T(1024)(128)(4,1)}), s8[1003520]{0:T(1024)(128)(4,1)S(1)}, s32[]{:S(2)}) async-start(s8[5197824]{0:T(1024)(128)(4,1)} %bitcast.10), calls=%async_computation.1 | async-start | bytes 2007040
  84.3 16.2 %collective-permute-start.33 = (bf16[192,384]{1,0:T(8,128)(2,1)S(1)}, bf16[192,384]{1,0:T(8,128)(2,1)S(1)}, u32[]{:S(2)}, u32[]{:S(2)}) collective-permute-start(bf16[192,384]{1,0:T(8,128)(2,1)S(1)} %copy-done.24), channel_id=1, source_target_pairs={{0,4},{4,8},{8,12},{12,14},{14,10},{10,6},{6,2},{2,0},{1,5},{5,9},... | collective-permute-start | bytes 442376 | tf_op jit(solution)/shard_map/ppermute | solution.py:375
  86.6 13.9 %collective-permute-start.35 = (bf16[192,384]{1,0:T(8,128)(2,1)S(1)}, bf16[192,384]{1,0:T(8,128)(2,1)S(1)}, u32[]{:S(2)}, u32[]{:S(2)}) collective-permute-start(bf16[192,384]{1,0:T(8,128)(2,1)S(1)} %copy-done.26), channel_id=1, source_target_pairs={{4,0},{8,4},{12,8},{14,12},{10,14},{6,10},{2,6},{0,2},{5,1},{9,5},... | collective-permute-start | bytes 442376 | tf_op jit(solution)/shard_map/ppermute | solution.py:377
  89.5 35.9 %collective-permute-start.28 = (f32[256,384]{1,0:T(8,128)S(1)}, f32[256,384]{1,0:T(8,128)S(1)}, u32[]{:S(2)}, u32[]{:S(2)}) collective-permute-start(f32[256,384]{1,0:T(8,128)S(1)} %product.13), channel_id=1, source_target_pairs={{0,1},{1,0},{2,3},{3,2},{4,5},{5,4},{6,7},{7,6},{8,9},{9,8},{10,11... | collective-permute-start | bytes 1179656 | tf_op jit(solution)/shard_map/ppermute | solution.py:380
  90.0 33.8 %collective-permute-start.20 = (f32[320,384]{1,0:T(8,128)S(1)}, f32[320,384]{1,0:T(8,128)S(1)}, u32[]{:S(2)}, u32[]{:S(2)}) collective-permute-start(f32[320,384]{1,0:T(8,128)S(1)} %product.11), channel_id=1, source_target_pairs={{0,1},{1,0},{2,3},{3,2},{4,5},{5,4},{6,7},{7,6},{8,9},{9,8},{10,11... | collective-permute-start | bytes 1474568 | tf_op jit(solution)/shard_map/ppermute | solution.py:380
  94.2 26.9 %collective-permute-start.12 = (f32[360,384]{1,0:T(8,128)S(1)}, f32[360,384]{1,0:T(8,128)S(1)}, u32[]{:S(2)}, u32[]{:S(2)}) collective-permute-start(f32[360,384]{1,0:T(8,128)S(1)} %product.9), channel_id=1, source_target_pairs={{0,1},{1,0},{2,3},{3,2},{4,5},{5,4},{6,7},{7,6},{8,9},{9,8},{10,11... | collective-permute-start | bytes 1658888 | tf_op jit(solution)/shard_map/ppermute | solution.py:380
  101.4 25.5 %collective-permute-start.36 = (f32[192,384]{1,0:T(8,128)S(1)}, f32[192,384]{1,0:T(8,128)S(1)}, u32[]{:S(2)}, u32[]{:S(2)}) collective-permute-start(f32[192,384]{1,0:T(8,128)S(1)} %product.15), channel_id=1, source_target_pairs={{0,1},{1,0},{2,3},{3,2},{4,5},{5,4},{6,7},{7,6},{8,9},{9,8},{10,11... | collective-permute-start | bytes 884744 | tf_op jit(solution)/shard_map/ppermute | solution.py:380
  121.2 6.3 %collective-permute-start.38 = (f32[360,384]{1,0:T(8,128)S(1)}, f32[360,384]{1,0:T(8,128)S(1)}, u32[]{:S(2)}, u32[]{:S(2)}) collective-permute-start(f32[360,384]{1,0:T(8,128)S(1)} %add.79.refs_0_), channel_id=1, source_target_pairs={{0,16},{16,0},{1,17},{17,1},{2,18},{18,2},{3,19},{19,3},{4,20},{20... | collective-permute-start | bytes 1658888 | tf_op jit(solution)/shard_map/ppermute | solution.py:32
  123.9 3.6 %collective-permute-start.39 = (f32[320,384]{1,0:T(8,128)S(1)}, f32[320,384]{1,0:T(8,128)S(1)}, u32[]{:S(2)}, u32[]{:S(2)}) collective-permute-start(f32[320,384]{1,0:T(8,128)S(1)} %add.80.refs_1_), channel_id=1, source_target_pairs={{0,16},{16,0},{1,17},{17,1},{2,18},{18,2},{3,19},{19,3},{4,20},{20... | collective-permute-start | bytes 1474568 | tf_op jit(solution)/shard_map/ppermute | solution.py:32
  125.5 2.0 %collective-permute-start.40 = (f32[256,384]{1,0:T(8,128)S(1)}, f32[256,384]{1,0:T(8,128)S(1)}, u32[]{:S(2)}, u32[]{:S(2)}) collective-permute-start(f32[256,384]{1,0:T(8,128)S(1)} %add.81.refs_2_), channel_id=1, source_target_pairs={{0,16},{16,0},{1,17},{17,1},{2,18},{18,2},{3,19},{19,3},{4,20},{20... | collective-permute-start | bytes 1179656 | tf_op jit(solution)/shard_map/ppermute | solution.py:32
  125.6 1.7 %collective-permute-start = (s32[1128]{0:T(1024)S(1)}, s32[1128]{0:T(1024)S(1)}, u32[]{:S(2)}, u32[]{:S(2)}) collective-permute-start(s32[1128]{0:T(1024)S(1)} %copy-done.29), channel_id=1, source_target_pairs={{0,16},{16,0},{1,17},{17,1},{2,18},{18,2},{3,19},{19,3},{4,20},{20... | collective-permute-start | bytes 13544 | tf_op jit(solution)/shard_map/ppermute | solution.py:32
  126.9 4.5 %collective-permute-start.37 = (f32[192,384]{1,0:T(8,128)S(1)}, f32[192,384]{1,0:T(8,128)S(1)}, u32[]{:S(2)}, u32[]{:S(2)}) collective-permute-start(f32[192,384]{1,0:T(8,128)S(1)} %add.82.refs_3_), channel_id=1, source_target_pairs={{0,16},{16,0},{1,17},{17,1},{2,18},{18,2},{3,19},{19,3},{4,20},{20... | collective-permute-start | bytes 884744 | tf_op jit(solution)/shard_map/ppermute | solution.py:32
  (27 other events, 76.1 us)
where the time goes:
time: 135 us
  waiting for transfers between devices  50.9 us (38%)
  starting transfers between devices  41.4 us (31%)
  Pallas kernels  31.1 us (23%)
  local copies, waits for them, and re-layouts  6.64 us (5%)
  matrix products  2.87 us (2%)
    ppermute x14, waiting for transfers between devices, shards(): blocks[-step] = lax.ppermute(blocks[1 - step], 'vir', backward)  26.4 us
    ppermute x14, starting transfers between devices, shards(): blocks[step] = lax.ppermute(blocks[step - 1], 'vir', forward)  20.7 us
    ppermute x4, waiting for transfers between devices, shards(): from_near = lax.ppermute(for_near, 'vir', across)  15.5 us
    pallas_call x8, Pallas kernels, product(): pl.pallas_call(functools.partial(product_kernel, len(blocks), start), out...  13.7 us
    ppermute x14, starting transfers between devices, shards(): blocks[-step] = lax.ppermute(blocks[1 - step], 'vir', backward)  11.8 us
    ppermute x14, waiting for transfers between devices, shards(): blocks[step] = lax.ppermute(blocks[step - 1], 'vir', forward)  8.78 us
    pallas_call x2, Pallas kernels, prepare(): pl.pallas_call(functools.partial(prepare_kernel, cols), out_shape=jax.Sha...  6.89 us
    unnamed x68, local copies, waits for them, and re-layouts  4.83 us
  transfers between devices with their start and end apart: 41, of which 14 were waited for; matrix products, arithmetic and copies ran while one was open for 4% of the time, Pallas kernels for 18%

commit v1 on v0

--- a/solution.py
+++ b/solution.py
@@ -18,6 +18,7 @@
 SMEM = pl.BlockSpec(memory_space=pltpu.SMEM)
 VMEM = pl.BlockSpec(memory_space=pltpu.VMEM)
 HBM = pl.BlockSpec(memory_space=pltpu.HBM)
+ANY = pl.BlockSpec(memory_space=pl.ANY)
 
 
 def row_chunks(rows, shares):
@@ -114,24 +115,43 @@
     )(index, tile_map, *pieces)
 
 
+FETCHED = 2
+
+
 def product_kernel(count, start, *refs):
-    integrals, out = refs[count], refs[-1]
-    row = jnp.concatenate([block[...] for block in refs[:count]], axis=1)
-    result = jnp.dot(row, integrals[...], preferred_element_type=jnp.float32)
+    blocks, integrals = refs[:count], refs[count]
+    out, fetched, sems = refs[-3:]
+    near = count - FETCHED
+    cols = out.shape[1]
+    copies = [
+        pltpu.make_async_copy(block, fetched.at[k], sems.at[k]) for k, block in enumerate(blocks[near:])
+    ]
+    for copy in copies:
+        copy.start()
+    row = jnp.concatenate([block[...] for block in blocks[:near]], axis=1)
+    first = jnp.dot(row, integrals[: near * cols, :], preferred_element_type=jnp.float32)
     if start is not None:
-        result = result + refs[count + 1][start : start + out.shape[0], :]
-    out[...] = result
+        first = first + refs[count + 1][start : start + out.shape[0], :]
+    out[...] = first
+    for copy in copies:
+        copy.wait()
+    row = jnp.concatenate([fetched[k] for k in range(FETCHED)], axis=1)
+    out[...] += jnp.dot(row, integrals[near * cols :, :], preferred_element_type=jnp.float32)
 
 
 def product(blocks, integrals, base=None, start=None):
-    length, _ = blocks[0].shape
+    length, cols = blocks[0].shape
     given = [] if base is None else [base]
     depth, width = integrals.shape
     return pl.pallas_call(
         functools.partial(product_kernel, len(blocks), start),
         out_shape=jax.ShapeDtypeStruct((length, width), jnp.float32),
-        in_specs=[VMEM] * (len(blocks) + 1 + len(given)),
+        in_specs=[VMEM] * (len(blocks) - FETCHED) + [ANY] * FETCHED + [VMEM] * (1 + len(given)),
         out_specs=VMEM,
+        scratch_shapes=[
+            pltpu.VMEM((FETCHED, length, cols), blocks[0].dtype),
+            pltpu.SemaphoreType.DMA((FETCHED,)),
+        ],
         compiler_params=pltpu.CompilerParams(vmem_limit_bytes=LIMIT),
         cost_estimate=pl.CostEstimate(
             flops=2 * length * depth * width,
@@ -329,7 +349,8 @@
     place = jnp.where(group % 2 == 0, group // 2, members - (group + 1) // 2)
     own_half = occ_place * half_blocks if cores == 2 else 0
 
-    ring_steps = sorted([*range((members + 1) // 2), *range(-(members // 2), 0)], key=abs)
+    ring_steps = [*range((members + 1) // 2), *range(-(members // 2), 0)]
+    ring_steps.sort(key=lambda step: (abs(step) == 1, abs(step)))
 
     ring_place = (place - jnp.array(ring_steps, jnp.int32)) % members
     ring_group = jnp.where(ring_place < evens, 2 * ring_place, 2 * (members - ring_place) - 1)

time: 135 us -> 137 us (1.015)
  Pallas kernels: 31.1 us -> 33.8 us
    pallas_call x8, Pallas kernels: 13.7 us -> 16.4 us  [product(): pl.pallas_call(functools.partial(product_kernel, len(blocks), start), out...]
  transfers between devices with their start and end apart: 41 -> 41, of which waited for: 14 -> 12; matrix products, arithmetic and copies ran while one was open for 4% -> 4% of each run, Pallas kernels for 18% -> 20%
where the time goes in v1:
time: 137 us; the launch traced here: 136 us
  waiting for transfers between devices  49.9 us (36%)
  starting transfers between devices  41.1 us (30%)
  Pallas kernels  33.8 us (25%)
  local copies, waits for them, and re-layouts  6.64 us (5%)
  matrix products  2.87 us (2%)
    ppermute x14, waiting for transfers between devices, shards(): blocks[-step] = lax.ppermute(blocks[1 - step], 'vir', backward)  26.1 us
    ppermute x14, starting transfers between devices, shards(): blocks[step] = lax.ppermute(blocks[step - 1], 'vir', forward)  20.7 us
    pallas_call x8, Pallas kernels, product(): pl.pallas_call(functools.partial(product_kernel, len(blocks), start), out...  16.4 us
    ppermute x4, waiting for transfers between devices, shards(): from_near = lax.ppermute(for_near, 'vir', across)  15 us
    ppermute x14, starting transfers between devices, shards(): blocks[-step] = lax.ppermute(blocks[1 - step], 'vir', backward)  11.5 us
    ppermute x14, waiting for transfers between devices, shards(): blocks[step] = lax.ppermute(blocks[step - 1], 'vir', forward)  8.78 us
    pallas_call x2, Pallas kernels, prepare(): pl.pallas_call(functools.partial(prepare_kernel, cols), out_shape=jax.Sha...  6.91 us
    unnamed x68, local copies, waits for them, and re-layouts  4.83 us
  transfers between devices with their start and end apart: 41, of which 12 were waited for; matrix products, arithmetic and copies ran while one was open for 4% of the time, Pallas kernels for 20%

profile of v1, /device:TPU:0, one launch (start us, length us, event | category | flops | bytes accessed | tf_op | source)
XLA Modules:
  0.0 136.4 jit_solution(7515352003170627541)
XLA Ops:
  0.0 3.1 %parts.2 = (bf16[384,1536]{1,0:T(8,128)(2,1)}, bf16[360,384]{1,0:T(8,128)(2,1)}, bf16[320,384]{1,0:T(8,128)(2,1)}, bf16[256,384]{1,0:T(8,128)(2,1)}, bf16[192,384]{1,0:T(8,128)(2,1)}) custom-call(s32[1]{0:T(128)} %bitcast.side_ref, bf16[384,3072]{1,0:T(8,128)(2,1)} %refs_0_.3, bf16[1128,384]{1,0:T(8,128)(2,1)} %refs_1_.1), custom_call_target="tpu_custom_call" | custom-call | bytes 4718592 | tf_op jit(solution)/shard_map/parts/pallas_call | solution.py:64
  3.1 3.0 %collective-permute-start.10 = (bf16[384,1536]{1,0:T(8,128)(2,1)}, bf16[384,1536]{1,0:T(8,128)(2,1)}, u32[]{:S(2)}, u32[]{:S(2)}) collective-permute-start(bf16[384,1536]{1,0:T(8,128)(2,1)} %get-tuple-element.12), channel_id=1, source_target_pairs={{0,1},{1,0},{2,3},{3,2},{4,5},{5,4},{6,7},{7,6},{8,9},{9,8},{10,11... | collective-permute-start | bytes 3538952 | tf_op jit(solution)/shard_map/ppermute | solution.py:374
  6.1 1.6 %collective-permute-start.21 = (bf16[256,384]{1,0:T(8,128)(2,1)}, bf16[256,384]{1,0:T(8,128)(2,1)S(1)}, u32[]{:S(2)}, u32[]{:S(2)}) collective-permute-start(bf16[256,384]{1,0:T(8,128)(2,1)} %get-tuple-element.14.refs_0_), channel_id=1, source_target_pairs={{0,4},{4,8},{8,12},{12,14},{14,10},{10,6},{6,2},{2,0},{1,5},{5,9},... | collective-permute-start | bytes 589832 | tf_op jit(solution)/shard_map/ppermute | solution.py:396
  8.2 1.6 %collective-permute-start.29 = (bf16[192,384]{1,0:T(8,128)(2,1)}, bf16[192,384]{1,0:T(8,128)(2,1)S(1)}, u32[]{:S(2)}, u32[]{:S(2)}) collective-permute-start(bf16[192,384]{1,0:T(8,128)(2,1)} %get-tuple-element.15.refs_0_), channel_id=1, source_target_pairs={{0,4},{4,8},{8,12},{12,14},{14,10},{10,6},{6,2},{2,0},{1,5},{5,9},... | collective-permute-start | bytes 442376 | tf_op jit(solution)/shard_map/ppermute | solution.py:396
  10.2 4.5 %collective-permute-done.31.refs_7_ = bf16[192,384]{1,0:T(8,128)(2,1)S(1)} collective-permute-done((bf16[192,384]{1,0:T(8,128)(2,1)}, bf16[192,384]{1,0:T(8,128)(2,1)S(1)}, u32[]{:S(2)}, u32[]{:S(2)}) %collective-permute-start.31) | collective-permute-done | bytes 147488 | tf_op jit(solution)/shard_map/ppermute | solution.py:398
  14.7 1.6 %collective-permute-start.1 = (bf16[360,384]{1,0:T(8,128)(2,1)}, bf16[360,384]{1,0:T(8,128)(2,1)}, u32[]{:S(2)}, u32[]{:S(2)}) collective-permute-start(bf16[360,384]{1,0:T(8,128)(2,1)} %get-tuple-element.11.refs_0_), channel_id=1, source_target_pairs={{0,4},{4,8},{8,12},{12,14},{14,10},{10,6},{6,2},{2,0},{1,5},{5,9},... | collective-permute-start | bytes 829448 | tf_op jit(solution)/shard_map/ppermute | solution.py:396
  16.2 1.1 collective-permute-done.29.refs_6_
  17.3 1.5 %collective-permute-start.15 = (bf16[320,384]{1,0:T(8,128)(2,1)}, bf16[320,384]{1,0:T(8,128)(2,1)}, u32[]{:S(2)}, u32[]{:S(2)}) collective-permute-start(bf16[320,384]{1,0:T(8,128)(2,1)} %get-tuple-element.13.refs_0_), channel_id=1, source_target_pairs={{4,0},{8,4},{12,8},{14,12},{10,14},{6,10},{2,6},{0,2},{5,1},{9,5},... | collective-permute-start | bytes 737288 | tf_op jit(solution)/shard_map/ppermute | solution.py:398
  19.3 1.5 %collective-permute-start.3 = (bf16[360,384]{1,0:T(8,128)(2,1)}, bf16[360,384]{1,0:T(8,128)(2,1)}, u32[]{:S(2)}, u32[]{:S(2)}) collective-permute-start(bf16[360,384]{1,0:T(8,128)(2,1)} %get-tuple-element.11.refs_0_), channel_id=1, source_target_pairs={{4,0},{8,4},{12,8},{14,12},{10,14},{6,10},{2,6},{0,2},{5,1},{9,5},... | collective-permute-start | bytes 829448 | tf_op jit(solution)/shard_map/ppermute | solution.py:398
  20.8 5.0 %collective-permute-done.15.refs_7_ = bf16[320,384]{1,0:T(8,128)(2,1)} collective-permute-done((bf16[320,384]{1,0:T(8,128)(2,1)}, bf16[320,384]{1,0:T(8,128)(2,1)}, u32[]{:S(2)}, u32[]{:S(2)}) %collective-permute-start.15) | collective-permute-done | bytes 245792 | tf_op jit(solution)/shard_map/ppermute | solution.py:398
  25.8 1.6 %collective-permute-start.22 = (bf16[256,384]{1,0:T(8,128)(2,1)S(1)}, bf16[256,384]{1,0:T(8,128)(2,1)S(1)}, u32[]{:S(2)}, u32[]{:S(2)}) collective-permute-start(bf16[256,384]{1,0:T(8,128)(2,1)S(1)} %collective-permute-done.21.refs_6_), channel_id=1, source_target_pairs={{0,4},{4,8},{8,12},{12,14},{14,10},{10,6},{6,2},{2,0},{1,5},{5,9},... | collective-permute-start | bytes 589832 | tf_op jit(solution)/shard_map/ppermute | solution.py:396
  28.1 1.2 collective-permute-done.13.refs_6_
  29.3 0.9 collective-permute-start.32
  30.8 1.1 collective-permute-start.30
  32.6 0.9 collective-permute-start.24
  34.2 1.8 %collective-permute-done.32.refs_2_ = bf16[192,384]{1,0:T(8,128)(2,1)S(1)} collective-permute-done((bf16[192,384]{1,0:T(8,128)(2,1)S(1)}, bf16[192,384]{1,0:T(8,128)(2,1)S(1)}, u32[]{:S(2)}, u32[]{:S(2)}) %collective-permute-start.32) | collective-permute-done | bytes 147488 | tf_op jit(solution)/shard_map/ppermute | solution.py:398
  36.0 0.9 collective-permute-start.16
  36.9 1.1 collective-permute-start.14
  38.0 1.0 collective-permute-start.34
  39.7 1.2 collective-permute-start.2
  40.9 4.7 %collective-permute-done.34.refs_4_ = bf16[192,384]{1,0:T(8,128)(2,1)S(1)} collective-permute-done((bf16[192,384]{1,0:T(8,128)(2,1)S(1)}, bf16[192,384]{1,0:T(8,128)(2,1)S(1)}, u32[]{:S(2)}, u32[]{:S(2)}) %collective-permute-start.34) | collective-permute-done | bytes 147488 | tf_op jit(solution)/shard_map/ppermute | solution.py:398
  46.2 1.4 %collective-permute-start.4 = (bf16[360,384]{1,0:T(8,128)(2,1)}, bf16[360,384]{1,0:T(8,128)(2,1)}, u32[]{:S(2)}, u32[]{:S(2)}) collective-permute-start(bf16[360,384]{1,0:T(8,128)(2,1)} %collective-permute-done.3.refs_7_), channel_id=1, source_target_pairs={{4,0},{8,4},{12,8},{14,12},{10,14},{6,10},{2,6},{0,2},{5,1},{9,5},... | collective-permute-start | bytes 829448 | tf_op jit(solution)/shard_map/ppermute | solution.py:398
  49.5 4.7 %collective-permute-done.4.refs_2_ = bf16[360,384]{1,0:T(8,128)(2,1)} collective-permute-done((bf16[360,384]{1,0:T(8,128)(2,1)}, bf16[360,384]{1,0:T(8,128)(2,1)}, u32[]{:S(2)}, u32[]{:S(2)}) %collective-permute-start.4) | collective-permute-done | bytes 276512 | tf_op jit(solution)/shard_map/ppermute | solution.py:398
  55.4 1.6 %collective-permute-start.18 = (bf16[320,384]{1,0:T(8,128)(2,1)}, bf16[320,384]{1,0:T(8,128)(2,1)}, u32[]{:S(2)}, u32[]{:S(2)}) collective-permute-start(bf16[320,384]{1,0:T(8,128)(2,1)} %collective-permute-done.16.refs_2_), channel_id=1, source_target_pairs={{4,0},{8,4},{12,8},{14,12},{10,14},{6,10},{2,6},{0,2},{5,1},{9,5},... | collective-permute-start | bytes 737288 | tf_op jit(solution)/shard_map/ppermute | solution.py:398
  57.2 5.0 %collective-permute-done.26.refs_4_ = bf16[256,384]{1,0:T(8,128)(2,1)S(1)} collective-permute-done((bf16[256,384]{1,0:T(8,128)(2,1)}, bf16[256,384]{1,0:T(8,128)(2,1)S(1)}, u32[]{:S(2)}, u32[]{:S(2)}) %collective-permute-start.26) | collective-permute-done | bytes 196640 | tf_op jit(solution)/shard_map/ppermute | solution.py:398
  62.9 1.7 %collective-permute-start.5 = (bf16[360,384]{1,0:T(8,128)(2,1)}, bf16[360,384]{1,0:T(8,128)(2,1)S(1)}, u32[]{:S(2)}, u32[]{:S(2)}) collective-permute-start(bf16[360,384]{1,0:T(8,128)(2,1)} %collective-permute-done.2.refs_1_), channel_id=1, source_target_pairs={{0,4},{4,8},{8,12},{12,14},{14,10},{10,6},{6,2},{2,0},{1,5},{5,9},... | collective-permute-start | bytes 829448 | tf_op jit(solution)/shard_map/ppermute | solution.py:396
  65.3 1.6 %collective-permute-start.27 = (bf16[256,384]{1,0:T(8,128)(2,1)S(1)}, bf16[256,384]{1,0:T(8,128)(2,1)S(1)}, u32[]{:S(2)}, u32[]{:S(2)}) collective-permute-start(bf16[256,384]{1,0:T(8,128)(2,1)S(1)} %collective-permute-done.25.refs_3_), channel_id=1, source_target_pairs={{0,4},{4,8},{8,12},{12,14},{14,10},{10,6},{6,2},{2,0},{1,5},{5,9},... | collective-permute-start | bytes 589832 | tf_op jit(solution)/shard_map/ppermute | solution.py:396
  67.2 6.0 %collective-permute-done.27.refs_5_ = bf16[256,384]{1,0:T(8,128)(2,1)S(1)} collective-permute-done((bf16[256,384]{1,0:T(8,128)(2,1)S(1)}, bf16[256,384]{1,0:T(8,128)(2,1)S(1)}, u32[]{:S(2)}, u32[]{:S(2)}) %collective-permute-start.27) | collective-permute-done | bytes 196640 | tf_op jit(solution)/shard_map/ppermute | solution.py:396
  73.2 2.5 %collective-permute-start.17 = (bf16[320,384]{1,0:T(8,128)(2,1)}, bf16[320,384]{1,0:T(8,128)(2,1)S(1)}, u32[]{:S(2)}, u32[]{:S(2)}) collective-permute-start(bf16[320,384]{1,0:T(8,128)(2,1)} %collective-permute-done.14.refs_1_), channel_id=1, source_target_pairs={{0,4},{4,8},{8,12},{12,14},{14,10},{10,6},{6,2},{2,0},{1,5},{5,9},... | collective-permute-start | bytes 737288 | tf_op jit(solution)/shard_map/ppermute | solution.py:396
  75.8 1.9 %collective-permute-start.7 = (bf16[360,384]{1,0:T(8,128)(2,1)S(1)}, bf16[360,384]{1,0:T(8,128)(2,1)S(1)}, u32[]{:S(2)}, u32[]{:S(2)}) collective-permute-start(bf16[360,384]{1,0:T(8,128)(2,1)S(1)} %collective-permute-done.5.refs_3_), channel_id=1, source_target_pairs={{0,4},{4,8},{8,12},{12,14},{14,10},{10,6},{6,2},{2,0},{1,5},{5,9},... | collective-permute-start | bytes 829448 | tf_op jit(solution)/shard_map/ppermute | solution.py:396
  77.8 1.3 constant_dynamic-update-slice_fusion
  79.2 3.9 %prepare.3.refs_8_ = bf16[3072,384]{1,0:T(8,128)(2,1)S(1)} custom-call(s32[17]{0:T(128)S(1)} %get-tuple-element.19.index_ref, s32[48,48]{1,0:T(8,128)S(1)} %copy-done.27, bf16[384,1536]{1,0:T(8,128)(2,1)} %collective-permute-done.10.refs_0_, bf16[384,1536]{1,0:T(8,128)(2,1)} %collective-permute-done.11.refs_1_), custom_call_target="tpu_custom_call" | custom-call | bytes 4718592 | tf_op jit(solution)/shard_map/prepare/pallas_call | solution.py:104
  83.2 1.6 %product.13 = f32[256,384]{1,0:T(8,128)S(1)} custom-call(bf16[256,384]{1,0:T(8,128)(2,1)S(1)} %copy-done.3, bf16[256,384]{1,0:T(8,128)(2,1)S(1)} %copy-done.9, bf16[256,384]{1,0:T(8,128)(2,1)S(1)} %copy-done.11, bf16[256,384]{1,0:T(8,128)(2,1)S(1)} %copy-done.13, bf16[256,384]{1,0:T(8,128)(2,1)S(1)} %copy-done.15, ...), custom_call_target="tpu_custom_call" | custom-call | flops 603979776 | bytes 3932160 | tf_op jit(solution)/shard_map/product/pallas_call | solution.py:146
  84.9 2.0 %collective-permute-start.33 = (bf16[192,384]{1,0:T(8,128)(2,1)S(1)}, bf16[192,384]{1,0:T(8,128)(2,1)S(1)}, u32[]{:S(2)}, u32[]{:S(2)}) collective-permute-start(bf16[192,384]{1,0:T(8,128)(2,1)S(1)} %copy-done.24), channel_id=1, source_target_pairs={{0,4},{4,8},{8,12},{12,14},{14,10},{10,6},{6,2},{2,0},{1,5},{5,9},... | collective-permute-start | bytes 442376 | tf_op jit(solution)/shard_map/ppermute | solution.py:396
  87.0 2.7 %product.11 = f32[320,384]{1,0:T(8,128)S(1)} custom-call(bf16[320,384]{1,0:T(8,128)(2,1)S(1)} %copy-done.2, bf16[320,384]{1,0:T(8,128)(2,1)} %collective-permute-done.14.refs_1_, bf16[320,384]{1,0:T(8,128)(2,1)} %collective-permute-done.16.refs_2_, bf16[320,384]{1,0:T(8,128)(2,1)S(1)} %collective-permute-done.17.refs_3_, ...), custom_call_target="tpu_custom_call" | custom-call | flops 754974720 | bytes 4325376 | tf_op jit(solution)/shard_map/product/pallas_call | solution.py:146
  90.4 1.5 %collective-permute-start.20 = (f32[320,384]{1,0:T(8,128)S(1)}, f32[320,384]{1,0:T(8,128)S(1)}, u32[]{:S(2)}, u32[]{:S(2)}) collective-permute-start(f32[320,384]{1,0:T(8,128)S(1)} %product.11), channel_id=1, source_target_pairs={{0,1},{1,0},{2,3},{3,2},{4,5},{5,4},{6,7},{7,6},{8,9},{9,8},{10,11... | collective-permute-start | bytes 1474568 | tf_op jit(solution)/shard_map/ppermute | solution.py:401
  91.9 2.6 %product.9 = f32[360,384]{1,0:T(8,128)S(1)} custom-call(bf16[360,384]{1,0:T(8,128)(2,1)S(1)} %copy-done.1, bf16[360,384]{1,0:T(8,128)(2,1)} %collective-permute-done.2.refs_1_, bf16[360,384]{1,0:T(8,128)(2,1)} %collective-permute-done.4.refs_2_, bf16[360,384]{1,0:T(8,128)(2,1)S(1)} %collective-permute-done.5.refs_3_, ...), custom_call_target="tpu_custom_call" | custom-call | flops 849346560 | bytes 4571136 | tf_op jit(solution)/shard_map/product/pallas_call | solution.py:146
  95.1 2.9 %fusion.refs_9_ = f32[1128,384]{1,0:T(8,128)S(1)} fusion(bf16[2256,384]{1,0:T(8,128)(2,1)S(1)} %constant_dynamic-update-slice_fusion, bf16[1128,2256]{1,0:T(8,128)(2,1)S(1)} %bitcast.11, bf16[1128,384]{1,0:T(8,128)(2,1)S(1)} %copy-done.28, f32[1128]{0:T(1024)S(1)} %select_reduce_fusion), kind=kOutput, calls=%fused_computation.1 | convolution fusion | flops 1955681280 | bytes 9425568 | tf_op jit(solution)/shard_map/dot_general | solution.py:388
  98.0 3.0 %prepare.2.refs_8_ = bf16[3072,384]{1,0:T(8,128)(2,1)S(1)} custom-call(s32[17]{0:T(128)S(1)} %get-tuple-element.20.index_ref, s32[48,48]{1,0:T(8,128)S(1)} %copy-done.27, bf16[384,1536]{1,0:T(8,128)(2,1)S(1)} %parts.3.refs_0_, bf16[384,1536]{1,0:T(8,128)(2,1)S(1)} %collective-permute-done.8.refs_1_), custom_call_target="tpu_custom_call" | custom-call | bytes 4718592 | tf_op jit(solution)/shard_map/prepare/pallas_call | solution.py:104
  101.0 1.3 product.15
  102.3 1.5 %collective-permute-start.36 = (f32[192,384]{1,0:T(8,128)S(1)}, f32[192,384]{1,0:T(8,128)S(1)}, u32[]{:S(2)}, u32[]{:S(2)}) collective-permute-start(f32[192,384]{1,0:T(8,128)S(1)} %product.15), channel_id=1, source_target_pairs={{0,1},{1,0},{2,3},{3,2},{4,5},{5,4},{6,7},{7,6},{8,9},{9,8},{10,11... | collective-permute-start | bytes 884744 | tf_op jit(solution)/shard_map/ppermute | solution.py:401
  103.9 2.6 %product.8 = f32[360,384]{1,0:T(8,128)S(1)} custom-call(bf16[360,384]{1,0:T(8,128)(2,1)S(1)} %copy-done.1, bf16[360,384]{1,0:T(8,128)(2,1)} %collective-permute-done.2.refs_1_, bf16[360,384]{1,0:T(8,128)(2,1)} %collective-permute-done.4.refs_2_, bf16[360,384]{1,0:T(8,128)(2,1)S(1)} %collective-permute-done.5.refs_3_, ...), custom_call_target="tpu_custom_call" | custom-call | flops 849346560 | bytes 4571136 | tf_op jit(solution)/shard_map/product/pallas_call | solution.py:146
  106.4 14.9 %collective-permute-done.12 = f32[360,384]{1,0:T(8,128)S(1)} collective-permute-done((f32[360,384]{1,0:T(8,128)S(1)}, f32[360,384]{1,0:T(8,128)S(1)}, u32[]{:S(2)}, u32[]{:S(2)}) %collective-permute-start.12) | collective-permute-done | bytes 552992 | tf_op jit(solution)/shard_map/ppermute | solution.py:401
  121.6 2.7 %product.10 = f32[320,384]{1,0:T(8,128)S(1)} custom-call(bf16[320,384]{1,0:T(8,128)(2,1)S(1)} %copy-done.2, bf16[320,384]{1,0:T(8,128)(2,1)} %collective-permute-done.14.refs_1_, bf16[320,384]{1,0:T(8,128)(2,1)} %collective-permute-done.16.refs_2_, bf16[320,384]{1,0:T(8,128)(2,1)S(1)} %collective-permute-done.17.refs_3_, ...), custom_call_target="tpu_custom_call" | custom-call | flops 754974720 | bytes 4325376 | tf_op jit(solution)/shard_map/product/pallas_call | solution.py:146
  124.9 1.6 %product.12 = f32[256,384]{1,0:T(8,128)S(1)} custom-call(bf16[256,384]{1,0:T(8,128)(2,1)S(1)} %copy-done.3, bf16[256,384]{1,0:T(8,128)(2,1)S(1)} %copy-done.9, bf16[256,384]{1,0:T(8,128)(2,1)S(1)} %copy-done.11, bf16[256,384]{1,0:T(8,128)(2,1)S(1)} %copy-done.13, bf16[256,384]{1,0:T(8,128)(2,1)S(1)} %copy-done.15, ...), custom_call_target="tpu_custom_call" | custom-call | flops 603979776 | bytes 3932160 | tf_op jit(solution)/shard_map/product/pallas_call | solution.py:146
  127.2 1.3 product.14
  128.9 3.9 %mirror_early.1.refs_5_ = f32[1136,3,128]{2,1,0:T(4,128)S(1)} custom-call(s32[1128]{0:T(1024)S(1)} %maximum_select_fusion.index_ref, f32[360,384]{1,0:T(8,128)S(1)} %add.79.refs_0_, f32[320,384]{1,0:T(8,128)S(1)} %add.80.refs_1_, f32[256,384]{1,0:T(8,128)S(1)} %add.81.refs_2_, f32[360,384]{1,0:T(8,128)S(1)} %collective-permute-done.38.refs_3_, ...), custom_call_target="tpu_custom_call" | custom-call | flops 433152 | bytes 5197824 | tf_op jit(solution)/shard_map/mirror_early/pallas_call | solution.py:303
  132.9 3.3 %mirror_late.1 = (f32[1128,384]{1,0:T(8,128)}, f32[1136,3,128]{2,1,0:T(4,128)S(1)}) custom-call(s32[384]{0:T(512)S(1)} %and_select_fusion.2.target_ref, f32[360,384]{1,0:T(8,128)S(1)} %add.79.refs_0_, f32[320,384]{1,0:T(8,128)S(1)} %add.80.refs_1_, f32[256,384]{1,0:T(8,128)S(1)} %add.81.refs_2_, ...), custom_call_target="tpu_custom_call", output_to_operand_aliasing={{1}: (6, {})} | custom-call | flops 433152 | bytes 5197824 | tf_op jit(solution)/shard_map/mirror_late/pallas_call | solution.py:313
  (133 shorter events, 13.7 us)
Async XLA Ops:
  0.0 47.6 %copy-start = (bf16[384,3072]{1,0:T(8,128)(2,1)S(1)}, bf16[384,3072]{1,0:T(8,128)(2,1)}, u32[]{:S(2)}) copy-start(bf16[384,3072]{1,0:T(8,128)(2,1)} %refs_0_.3) | copy-start | bytes 7077892
  3.1 34.9 %collective-permute-start.10 = (bf16[384,1536]{1,0:T(8,128)(2,1)}, bf16[384,1536]{1,0:T(8,128)(2,1)}, u32[]{:S(2)}, u32[]{:S(2)}) collective-permute-start(bf16[384,1536]{1,0:T(8,128)(2,1)} %get-tuple-element.12), channel_id=1, source_target_pairs={{0,1},{1,0},{2,3},{3,2},{4,5},{5,4},{6,7},{7,6},{8,9},{9,8},{10,11... | collective-permute-start | bytes 3538952 | tf_op jit(solution)/shard_map/ppermute | solution.py:374
  6.1 12.7 %collective-permute-start.21 = (bf16[256,384]{1,0:T(8,128)(2,1)}, bf16[256,384]{1,0:T(8,128)(2,1)S(1)}, u32[]{:S(2)}, u32[]{:S(2)}) collective-permute-start(bf16[256,384]{1,0:T(8,128)(2,1)} %get-tuple-element.14.refs_0_), channel_id=1, source_target_pairs={{0,4},{4,8},{8,12},{12,14},{14,10},{10,6},{6,2},{2,0},{1,5},{5,9},... | collective-permute-start | bytes 589832 | tf_op jit(solution)/shard_map/ppermute | solution.py:396
  7.7 6.9 %collective-permute-start.31 = (bf16[192,384]{1,0:T(8,128)(2,1)}, bf16[192,384]{1,0:T(8,128)(2,1)S(1)}, u32[]{:S(2)}, u32[]{:S(2)}) collective-permute-start(bf16[192,384]{1,0:T(8,128)(2,1)} %get-tuple-element.15.refs_0_), channel_id=1, source_target_pairs={{4,0},{8,4},{12,8},{14,12},{10,14},{6,10},{2,6},{0,2},{5,1},{9,5},... | collective-permute-start | bytes 442376 | tf_op jit(solution)/shard_map/ppermute | solution.py:398
  8.2 9.1 %collective-permute-start.29 = (bf16[192,384]{1,0:T(8,128)(2,1)}, bf16[192,384]{1,0:T(8,128)(2,1)S(1)}, u32[]{:S(2)}, u32[]{:S(2)}) collective-permute-start(bf16[192,384]{1,0:T(8,128)(2,1)} %get-tuple-element.15.refs_0_), channel_id=1, source_target_pairs={{0,4},{4,8},{8,12},{12,14},{14,10},{10,6},{6,2},{2,0},{1,5},{5,9},... | collective-permute-start | bytes 442376 | tf_op jit(solution)/shard_map/ppermute | solution.py:396
  9.7 9.6 %collective-permute-start.23 = (bf16[256,384]{1,0:T(8,128)(2,1)}, bf16[256,384]{1,0:T(8,128)(2,1)S(1)}, u32[]{:S(2)}, u32[]{:S(2)}) collective-permute-start(bf16[256,384]{1,0:T(8,128)(2,1)} %get-tuple-element.14.refs_0_), channel_id=1, source_target_pairs={{4,0},{8,4},{12,8},{14,12},{10,14},{6,10},{2,6},{0,2},{5,1},{9,5},... | collective-permute-start | bytes 589832 | tf_op jit(solution)/shard_map/ppermute | solution.py:398
  14.7 16.2 %collective-permute-start.1 = (bf16[360,384]{1,0:T(8,128)(2,1)}, bf16[360,384]{1,0:T(8,128)(2,1)}, u32[]{:S(2)}, u32[]{:S(2)}) collective-permute-start(bf16[360,384]{1,0:T(8,128)(2,1)} %get-tuple-element.11.refs_0_), channel_id=1, source_target_pairs={{0,4},{4,8},{8,12},{12,14},{14,10},{10,6},{6,2},{2,0},{1,5},{5,9},... | collective-permute-start | bytes 829448 | tf_op jit(solution)/shard_map/ppermute | solution.py:396
  17.3 8.5 %collective-permute-start.15 = (bf16[320,384]{1,0:T(8,128)(2,1)}, bf16[320,384]{1,0:T(8,128)(2,1)}, u32[]{:S(2)}, u32[]{:S(2)}) collective-permute-start(bf16[320,384]{1,0:T(8,128)(2,1)} %get-tuple-element.13.refs_0_), channel_id=1, source_target_pairs={{4,0},{8,4},{12,8},{14,12},{10,14},{6,10},{2,6},{0,2},{5,1},{9,5},... | collective-permute-start | bytes 737288 | tf_op jit(solution)/shard_map/ppermute | solution.py:398
  18.8 10.5 %collective-permute-start.13 = (bf16[320,384]{1,0:T(8,128)(2,1)}, bf16[320,384]{1,0:T(8,128)(2,1)}, u32[]{:S(2)}, u32[]{:S(2)}) collective-permute-start(bf16[320,384]{1,0:T(8,128)(2,1)} %get-tuple-element.13.refs_0_), channel_id=1, source_target_pairs={{0,4},{4,8},{8,12},{12,14},{14,10},{10,6},{6,2},{2,0},{1,5},{5,9},... | collective-permute-start | bytes 737288 | tf_op jit(solution)/shard_map/ppermute | solution.py:396
  19.3 13.3 %collective-permute-start.3 = (bf16[360,384]{1,0:T(8,128)(2,1)}, bf16[360,384]{1,0:T(8,128)(2,1)}, u32[]{:S(2)}, u32[]{:S(2)}) collective-permute-start(bf16[360,384]{1,0:T(8,128)(2,1)} %get-tuple-element.11.refs_0_), channel_id=1, source_target_pairs={{4,0},{8,4},{12,8},{14,12},{10,14},{6,10},{2,6},{0,2},{5,1},{9,5},... | collective-permute-start | bytes 829448 | tf_op jit(solution)/shard_map/ppermute | solution.py:398
  25.8 12.2 %collective-permute-start.22 = (bf16[256,384]{1,0:T(8,128)(2,1)S(1)}, bf16[256,384]{1,0:T(8,128)(2,1)S(1)}, u32[]{:S(2)}, u32[]{:S(2)}) collective-permute-start(bf16[256,384]{1,0:T(8,128)(2,1)S(1)} %collective-permute-done.21.refs_6_), channel_id=1, source_target_pairs={{0,4},{4,8},{8,12},{12,14},{14,10},{10,6},{6,2},{2,0},{1,5},{5,9},... | collective-permute-start | bytes 589832 | tf_op jit(solution)/shard_map/ppermute | solution.py:396
  29.3 6.7 %collective-permute-start.32 = (bf16[192,384]{1,0:T(8,128)(2,1)S(1)}, bf16[192,384]{1,0:T(8,128)(2,1)S(1)}, u32[]{:S(2)}, u32[]{:S(2)}) collective-permute-start(bf16[192,384]{1,0:T(8,128)(2,1)S(1)} %collective-permute-done.31.refs_7_), channel_id=1, source_target_pairs={{4,0},{8,4},{12,8},{14,12},{10,14},{6,10},{2,6},{0,2},{5,1},{9,5},... | collective-permute-start | bytes 442376 | tf_op jit(solution)/shard_map/ppermute | solution.py:398
  30.8 6.1 %collective-permute-start.30 = (bf16[192,384]{1,0:T(8,128)(2,1)S(1)}, bf16[192,384]{1,0:T(8,128)(2,1)S(1)}, u32[]{:S(2)}, u32[]{:S(2)}) collective-permute-start(bf16[192,384]{1,0:T(8,128)(2,1)S(1)} %collective-permute-done.29.refs_6_), channel_id=1, source_target_pairs={{0,4},{4,8},{8,12},{12,14},{14,10},{10,6},{6,2},{2,0},{1,5},{5,9},... | collective-permute-start | bytes 442376 | tf_op jit(solution)/shard_map/ppermute | solution.py:396
  32.6 7.0 %collective-permute-start.24 = (bf16[256,384]{1,0:T(8,128)(2,1)S(1)}, bf16[256,384]{1,0:T(8,128)(2,1)S(1)}, u32[]{:S(2)}, u32[]{:S(2)}) collective-permute-start(bf16[256,384]{1,0:T(8,128)(2,1)S(1)} %collective-permute-done.23.refs_7_), channel_id=1, source_target_pairs={{4,0},{8,4},{12,8},{14,12},{10,14},{6,10},{2,6},{0,2},{5,1},{9,5},... | collective-permute-start | bytes 589832 | tf_op jit(solution)/shard_map/ppermute | solution.py:398
  36.0 11.8 %collective-permute-start.16 = (bf16[320,384]{1,0:T(8,128)(2,1)}, bf16[320,384]{1,0:T(8,128)(2,1)}, u32[]{:S(2)}, u32[]{:S(2)}) collective-permute-start(bf16[320,384]{1,0:T(8,128)(2,1)} %collective-permute-done.15.refs_7_), channel_id=1, source_target_pairs={{4,0},{8,4},{12,8},{14,12},{10,14},{6,10},{2,6},{0,2},{5,1},{9,5},... | collective-permute-start | bytes 737288 | tf_op jit(solution)/shard_map/ppermute | solution.py:398
  36.9 11.0 %collective-permute-start.14 = (bf16[320,384]{1,0:T(8,128)(2,1)}, bf16[320,384]{1,0:T(8,128)(2,1)}, u32[]{:S(2)}, u32[]{:S(2)}) collective-permute-start(bf16[320,384]{1,0:T(8,128)(2,1)} %collective-permute-done.13.refs_6_), channel_id=1, source_target_pairs={{0,4},{4,8},{8,12},{12,14},{14,10},{10,6},{6,2},{2,0},{1,5},{5,9},... | collective-permute-start | bytes 737288 | tf_op jit(solution)/shard_map/ppermute | solution.py:396
  38.0 37.8 %collective-permute-start.11 = (bf16[384,1536]{1,0:T(8,128)(2,1)}, bf16[384,1536]{1,0:T(8,128)(2,1)}, u32[]{:S(2)}, u32[]{:S(2)}) collective-permute-start(bf16[384,1536]{1,0:T(8,128)(2,1)} %collective-permute-done.10.refs_0_), channel_id=1, source_target_pairs={{0,16},{16,0},{1,17},{17,1},{2,18},{18,2},{3,19},{19,3},{4,20},{20... | collective-permute-start | bytes 3538952 | tf_op jit(solution)/shard_map/ppermute | solution.py:33
  38.0 7.5 %collective-permute-start.34 = (bf16[192,384]{1,0:T(8,128)(2,1)S(1)}, bf16[192,384]{1,0:T(8,128)(2,1)S(1)}, u32[]{:S(2)}, u32[]{:S(2)}) collective-permute-start(bf16[192,384]{1,0:T(8,128)(2,1)S(1)} %collective-permute-done.32.refs_2_), channel_id=1, source_target_pairs={{4,0},{8,4},{12,8},{14,12},{10,14},{6,10},{2,6},{0,2},{5,1},{9,5},... | collective-permute-start | bytes 442376 | tf_op jit(solution)/shard_map/ppermute | solution.py:398
  39.7 9.7 %collective-permute-start.2 = (bf16[360,384]{1,0:T(8,128)(2,1)}, bf16[360,384]{1,0:T(8,128)(2,1)}, u32[]{:S(2)}, u32[]{:S(2)}) collective-permute-start(bf16[360,384]{1,0:T(8,128)(2,1)} %collective-permute-done.1.refs_6_), channel_id=1, source_target_pairs={{0,4},{4,8},{8,12},{12,14},{14,10},{10,6},{6,2},{2,0},{1,5},{5,9},... | collective-permute-start | bytes 829448 | tf_op jit(solution)/shard_map/ppermute | solution.py:396
  46.2 8.0 %collective-permute-start.4 = (bf16[360,384]{1,0:T(8,128)(2,1)}, bf16[360,384]{1,0:T(8,128)(2,1)}, u32[]{:S(2)}, u32[]{:S(2)}) collective-permute-start(bf16[360,384]{1,0:T(8,128)(2,1)} %collective-permute-done.3.refs_7_), channel_id=1, source_target_pairs={{4,0},{8,4},{12,8},{14,12},{10,14},{6,10},{2,6},{0,2},{5,1},{9,5},... | collective-permute-start | bytes 829448 | tf_op jit(solution)/shard_map/ppermute | solution.py:398
  47.6 9.5 %copy-start.30 = (s32[1128,2]{0,1:T(2,128)S(1)}, s32[1128,2]{0,1:T(2,128)}, u32[]{:S(2)}) copy-start(s32[1128,2]{0,1:T(2,128)} %param.13) | copy-start | bytes 27076
  47.6 9.5 %copy-start.31 = (f32[48]{0:T(128)S(1)}, f32[48]{0:T(128)}, u32[]{:S(2)}) copy-start(f32[48]{0:T(128)} %param.12) | copy-start | bytes 580
  47.8 27.8 %collective-permute-start.9 = (bf16[1128,384]{1,0:T(8,128)(2,1)}, bf16[1128,384]{1,0:T(8,128)(2,1)}, u32[]{:S(2)}, u32[]{:S(2)}) collective-permute-start(bf16[1128,384]{1,0:T(8,128)(2,1)} %refs_1_.1), channel_id=1, source_target_pairs={{0,16},{16,0},{1,17},{17,1},{2,18},{18,2},{3,19},{19,3},{4,20},{20... | collective-permute-start | bytes 2598920 | tf_op jit(solution)/shard_map/ppermute | solution.py:33
  47.9 7.5 %collective-permute-start.25 = (bf16[256,384]{1,0:T(8,128)(2,1)}, bf16[256,384]{1,0:T(8,128)(2,1)S(1)}, u32[]{:S(2)}, u32[]{:S(2)}) collective-permute-start(bf16[256,384]{1,0:T(8,128)(2,1)} %copy-done.8), channel_id=1, source_target_pairs={{0,4},{4,8},{8,12},{12,14},{14,10},{10,6},{6,2},{2,0},{1,5},{5,9},... | collective-permute-start | bytes 589832 | tf_op jit(solution)/shard_map/ppermute | solution.py:396
  49.3 45.1 %collective-permute-start.8 = (bf16[384,1536]{1,0:T(8,128)(2,1)S(1)}, bf16[384,1536]{1,0:T(8,128)(2,1)S(1)}, u32[]{:S(2)}, u32[]{:S(2)}) collective-permute-start(bf16[384,1536]{1,0:T(8,128)(2,1)S(1)} %parts.3.refs_0_), channel_id=1, source_target_pairs={{0,16},{16,0},{1,17},{17,1},{2,18},{18,2},{3,19},{19,3},{4,20},{20... | collective-permute-start | bytes 3538952 | tf_op jit(solution)/shard_map/ppermute | solution.py:33
  54.2 8.0 %collective-permute-start.26 = (bf16[256,384]{1,0:T(8,128)(2,1)}, bf16[256,384]{1,0:T(8,128)(2,1)S(1)}, u32[]{:S(2)}, u32[]{:S(2)}) collective-permute-start(bf16[256,384]{1,0:T(8,128)(2,1)} %copy-done.10), channel_id=1, source_target_pairs={{4,0},{8,4},{12,8},{14,12},{10,14},{6,10},{2,6},{0,2},{5,1},{9,5},... | collective-permute-start | bytes 589832 | tf_op jit(solution)/shard_map/ppermute | solution.py:398
  55.4 11.8 %copy-start.12 = (bf16[256,384]{1,0:T(8,128)(2,1)}, bf16[256,384]{1,0:T(8,128)(2,1)S(1)}, u32[]{:S(2)}) copy-start(bf16[256,384]{1,0:T(8,128)(2,1)S(1)} %collective-permute-done.25.refs_3_) | copy-start | bytes 589828
  55.4 9.9 %collective-permute-start.18 = (bf16[320,384]{1,0:T(8,128)(2,1)}, bf16[320,384]{1,0:T(8,128)(2,1)}, u32[]{:S(2)}, u32[]{:S(2)}) collective-permute-start(bf16[320,384]{1,0:T(8,128)(2,1)} %collective-permute-done.16.refs_2_), channel_id=1, source_target_pairs={{4,0},{8,4},{12,8},{14,12},{10,14},{6,10},{2,6},{0,2},{5,1},{9,5},... | collective-permute-start | bytes 737288 | tf_op jit(solution)/shard_map/ppermute | solution.py:398
  62.9 12.7 %collective-permute-start.5 = (bf16[360,384]{1,0:T(8,128)(2,1)}, bf16[360,384]{1,0:T(8,128)(2,1)S(1)}, u32[]{:S(2)}, u32[]{:S(2)}) collective-permute-start(bf16[360,384]{1,0:T(8,128)(2,1)} %collective-permute-done.2.refs_1_), channel_id=1, source_target_pairs={{0,4},{4,8},{8,12},{12,14},{14,10},{10,6},{6,2},{2,0},{1,5},{5,9},... | collective-permute-start | bytes 829448 | tf_op jit(solution)/shard_map/ppermute | solution.py:396
  65.3 7.9 %collective-permute-start.27 = (bf16[256,384]{1,0:T(8,128)(2,1)S(1)}, bf16[256,384]{1,0:T(8,128)(2,1)S(1)}, u32[]{:S(2)}, u32[]{:S(2)}) collective-permute-start(bf16[256,384]{1,0:T(8,128)(2,1)S(1)} %collective-permute-done.25.refs_3_), channel_id=1, source_target_pairs={{0,4},{4,8},{8,12},{12,14},{14,10},{10,6},{6,2},{2,0},{1,5},{5,9},... | collective-permute-start | bytes 589832 | tf_op jit(solution)/shard_map/ppermute | solution.py:396
  67.0 12.1 %copy-start.27 = (s32[48,48]{1,0:T(8,128)S(1)}, s32[48,48]{1,0:T(8,128)}, u32[]{:S(2)}) copy-start(s32[48,48]{1,0:T(8,128)} %map_hbm.3) | copy-start | bytes 27652
  73.2 11.7 %collective-permute-start.17 = (bf16[320,384]{1,0:T(8,128)(2,1)}, bf16[320,384]{1,0:T(8,128)(2,1)S(1)}, u32[]{:S(2)}, u32[]{:S(2)}) collective-permute-start(bf16[320,384]{1,0:T(8,128)(2,1)} %collective-permute-done.14.refs_1_), channel_id=1, source_target_pairs={{0,4},{4,8},{8,12},{12,14},{14,10},{10,6},{6,2},{2,0},{1,5},{5,9},... | collective-permute-start | bytes 737288 | tf_op jit(solution)/shard_map/ppermute | solution.py:396
  75.7 14.1 %collective-permute-start.6 = (bf16[360,384]{1,0:T(8,128)(2,1)}, bf16[360,384]{1,0:T(8,128)(2,1)S(1)}, u32[]{:S(2)}, u32[]{:S(2)}) collective-permute-start(bf16[360,384]{1,0:T(8,128)(2,1)} %collective-permute-done.4.refs_2_), channel_id=1, source_target_pairs={{4,0},{8,4},{12,8},{14,12},{10,14},{6,10},{2,6},{0,2},{5,1},{9,5},... | collective-permute-start | bytes 829448 | tf_op jit(solution)/shard_map/ppermute | solution.py:398
  75.7 11.3 %collective-permute-start.19 = (bf16[320,384]{1,0:T(8,128)(2,1)}, bf16[320,384]{1,0:T(8,128)(2,1)S(1)}, u32[]{:S(2)}, u32[]{:S(2)}) collective-permute-start(bf16[320,384]{1,0:T(8,128)(2,1)} %collective-permute-done.18.refs_4_), channel_id=1, source_target_pairs={{4,0},{8,4},{12,8},{14,12},{10,14},{6,10},{2,6},{0,2},{5,1},{9,5},... | collective-permute-start | bytes 737288 | tf_op jit(solution)/shard_map/ppermute | solution.py:398
  75.8 14.5 %collective-permute-start.7 = (bf16[360,384]{1,0:T(8,128)(2,1)S(1)}, bf16[360,384]{1,0:T(8,128)(2,1)S(1)}, u32[]{:S(2)}, u32[]{:S(2)}) collective-permute-start(bf16[360,384]{1,0:T(8,128)(2,1)S(1)} %collective-permute-done.5.refs_3_), channel_id=1, source_target_pairs={{0,4},{4,8},{8,12},{12,14},{14,10},{10,6},{6,2},{2,0},{1,5},{5,9},... | collective-permute-start | bytes 829448 | tf_op jit(solution)/shard_map/ppermute | solution.py:396
  83.2 11.8 %slice-start = ((s8[5197824]{0:T(1024)(128)(4,1)}), s8[4194304]{0:T(1024)(128)(4,1)S(1)}, s32[]{:S(2)}) async-start(s8[5197824]{0:T(1024)(128)(4,1)} %bitcast.10), calls=%async_computation | async-start | bytes 8388608
  84.9 10.1 %slice-start.1 = ((s8[5197824]{0:T(1024)(128)(4,1)}), s8[1003520]{0:T(1024)(128)(4,1)S(1)}, s32[]{:S(2)}) async-start(s8[5197824]{0:T(1024)(128)(4,1)} %bitcast.10), calls=%async_computation.1 | async-start | bytes 2007040
  84.9 16.0 %collective-permute-start.33 = (bf16[192,384]{1,0:T(8,128)(2,1)S(1)}, bf16[192,384]{1,0:T(8,128)(2,1)S(1)}, u32[]{:S(2)}, u32[]{:S(2)}) collective-permute-start(bf16[192,384]{1,0:T(8,128)(2,1)S(1)} %copy-done.24), channel_id=1, source_target_pairs={{0,4},{4,8},{8,12},{12,14},{14,10},{10,6},{6,2},{2,0},{1,5},{5,9},... | collective-permute-start | bytes 442376 | tf_op jit(solution)/shard_map/ppermute | solution.py:396
  87.0 14.0 %collective-permute-start.35 = (bf16[192,384]{1,0:T(8,128)(2,1)S(1)}, bf16[192,384]{1,0:T(8,128)(2,1)S(1)}, u32[]{:S(2)}, u32[]{:S(2)}) collective-permute-start(bf16[192,384]{1,0:T(8,128)(2,1)S(1)} %copy-done.26), channel_id=1, source_target_pairs={{4,0},{8,4},{12,8},{14,12},{10,14},{6,10},{2,6},{0,2},{5,1},{9,5},... | collective-permute-start | bytes 442376 | tf_op jit(solution)/shard_map/ppermute | solution.py:398
  89.8 36.8 %collective-permute-start.28 = (f32[256,384]{1,0:T(8,128)S(1)}, f32[256,384]{1,0:T(8,128)S(1)}, u32[]{:S(2)}, u32[]{:S(2)}) collective-permute-start(f32[256,384]{1,0:T(8,128)S(1)} %product.13), channel_id=1, source_target_pairs={{0,1},{1,0},{2,3},{3,2},{4,5},{5,4},{6,7},{7,6},{8,9},{9,8},{10,11... | collective-permute-start | bytes 1179656 | tf_op jit(solution)/shard_map/ppermute | solution.py:401
  90.4 33.9 %collective-permute-start.20 = (f32[320,384]{1,0:T(8,128)S(1)}, f32[320,384]{1,0:T(8,128)S(1)}, u32[]{:S(2)}, u32[]{:S(2)}) collective-permute-start(f32[320,384]{1,0:T(8,128)S(1)} %product.11), channel_id=1, source_target_pairs={{0,1},{1,0},{2,3},{3,2},{4,5},{5,4},{6,7},{7,6},{8,9},{9,8},{10,11... | collective-permute-start | bytes 1474568 | tf_op jit(solution)/shard_map/ppermute | solution.py:401
  94.4 27.0 %collective-permute-start.12 = (f32[360,384]{1,0:T(8,128)S(1)}, f32[360,384]{1,0:T(8,128)S(1)}, u32[]{:S(2)}, u32[]{:S(2)}) collective-permute-start(f32[360,384]{1,0:T(8,128)S(1)} %product.9), channel_id=1, source_target_pairs={{0,1},{1,0},{2,3},{3,2},{4,5},{5,4},{6,7},{7,6},{8,9},{9,8},{10,11... | collective-permute-start | bytes 1658888 | tf_op jit(solution)/shard_map/ppermute | solution.py:401
  102.3 26.1 %collective-permute-start.36 = (f32[192,384]{1,0:T(8,128)S(1)}, f32[192,384]{1,0:T(8,128)S(1)}, u32[]{:S(2)}, u32[]{:S(2)}) collective-permute-start(f32[192,384]{1,0:T(8,128)S(1)} %product.15), channel_id=1, source_target_pairs={{0,1},{1,0},{2,3},{3,2},{4,5},{5,4},{6,7},{7,6},{8,9},{9,8},{10,11... | collective-permute-start | bytes 884744 | tf_op jit(solution)/shard_map/ppermute | solution.py:401
  121.5 7.4 %collective-permute-start.38 = (f32[360,384]{1,0:T(8,128)S(1)}, f32[360,384]{1,0:T(8,128)S(1)}, u32[]{:S(2)}, u32[]{:S(2)}) collective-permute-start(f32[360,384]{1,0:T(8,128)S(1)} %add.79.refs_0_), channel_id=1, source_target_pairs={{0,16},{16,0},{1,17},{17,1},{2,18},{18,2},{3,19},{19,3},{4,20},{20... | collective-permute-start | bytes 1658888 | tf_op jit(solution)/shard_map/ppermute | solution.py:33
  124.3 4.6 %collective-permute-start.39 = (f32[320,384]{1,0:T(8,128)S(1)}, f32[320,384]{1,0:T(8,128)S(1)}, u32[]{:S(2)}, u32[]{:S(2)}) collective-permute-start(f32[320,384]{1,0:T(8,128)S(1)} %add.80.refs_1_), channel_id=1, source_target_pairs={{0,16},{16,0},{1,17},{17,1},{2,18},{18,2},{3,19},{19,3},{4,20},{20... | collective-permute-start | bytes 1474568 | tf_op jit(solution)/shard_map/ppermute | solution.py:33
  126.6 2.3 %collective-permute-start.40 = (f32[256,384]{1,0:T(8,128)S(1)}, f32[256,384]{1,0:T(8,128)S(1)}, u32[]{:S(2)}, u32[]{:S(2)}) collective-permute-start(f32[256,384]{1,0:T(8,128)S(1)} %add.81.refs_2_), channel_id=1, source_target_pairs={{0,16},{16,0},{1,17},{17,1},{2,18},{18,2},{3,19},{19,3},{4,20},{20... | collective-permute-start | bytes 1179656 | tf_op jit(solution)/shard_map/ppermute | solution.py:33
  126.7 2.1 %collective-permute-start = (s32[1128]{0:T(1024)S(1)}, s32[1128]{0:T(1024)S(1)}, u32[]{:S(2)}, u32[]{:S(2)}) collective-permute-start(s32[1128]{0:T(1024)S(1)} %copy-done.29), channel_id=1, source_target_pairs={{0,16},{16,0},{1,17},{17,1},{2,18},{18,2},{3,19},{19,3},{4,20},{20... | collective-permute-start | bytes 13544 | tf_op jit(solution)/shard_map/ppermute | solution.py:33
  128.5 4.4 %collective-permute-start.37 = (f32[192,384]{1,0:T(8,128)S(1)}, f32[192,384]{1,0:T(8,128)S(1)}, u32[]{:S(2)}, u32[]{:S(2)}) collective-permute-start(f32[192,384]{1,0:T(8,128)S(1)} %add.82.refs_3_), channel_id=1, source_target_pairs={{0,16},{16,0},{1,17},{17,1},{2,18},{18,2},{3,19},{19,3},{4,20},{20... | collective-permute-start | bytes 884744 | tf_op jit(solution)/shard_map/ppermute | solution.py:33
  (27 other events, 77.5 us)

commit v2 on v0

--- a/solution.py
+++ b/solution.py
@@ -11,6 +11,8 @@
 TILE = 128
 SHARES = (360, 320, 256, 192)
 
+FETCHED = {0: (0,), 1: (1, -1)}
+
 
 LIMIT = 16 * 1024 * 1024
 MIRROR_LIMIT = 24 * 1024 * 1024
@@ -18,6 +20,7 @@
 SMEM = pl.BlockSpec(memory_space=pltpu.SMEM)
 VMEM = pl.BlockSpec(memory_space=pltpu.VMEM)
 HBM = pl.BlockSpec(memory_space=pltpu.HBM)
+ANY = pl.BlockSpec(memory_space=pl.ANY)
 
 
 def row_chunks(rows, shares):
@@ -114,24 +117,45 @@
     )(index, tile_map, *pieces)
 
 
-def product_kernel(count, start, *refs):
-    integrals, out = refs[count], refs[-1]
-    row = jnp.concatenate([block[...] for block in refs[:count]], axis=1)
-    result = jnp.dot(row, integrals[...], preferred_element_type=jnp.float32)
+def product_kernel(count, fetched, start, *refs):
+    blocks, integrals = refs[:count], refs[count]
+    out = refs[count + 1 + (start is not None)]
+    cols = blocks[0].shape[1]
+
+    def some(values, places):
+        row = jnp.concatenate(values, axis=1)
+        parts = [integrals[k * cols : (k + 1) * cols, :] for k in places]
+        return jnp.dot(row, jnp.concatenate(parts, axis=0), preferred_element_type=jnp.float32)
+
+    copies = []
+    for n, k in enumerate(fetched):
+        copies.append(pltpu.make_async_copy(blocks[k], refs[-2].at[n], refs[-1].at[n]))
+        copies[-1].start()
+    here = [k for k in range(count) if k not in fetched]
+    first = some([blocks[k][...] for k in here], here)
     if start is not None:
-        result = result + refs[count + 1][start : start + out.shape[0], :]
-    out[...] = result
-
-
-def product(blocks, integrals, base=None, start=None):
-    length, _ = blocks[0].shape
+        first = first + refs[count + 1][start : start + out.shape[0], :]
+    out[...] = first
+    if fetched:
+        for copy in copies:
+            copy.wait()
+        out[...] += some([refs[-2][n] for n in range(len(fetched))], fetched)
+
+
+def product(blocks, integrals, fetched=(), base=None, start=None):
+    length, cols = blocks[0].shape
     given = [] if base is None else [base]
     depth, width = integrals.shape
+    scratch = [
+        pltpu.VMEM((len(fetched), length, cols), blocks[0].dtype),
+        pltpu.SemaphoreType.DMA((len(fetched),)),
+    ]
     return pl.pallas_call(
-        functools.partial(product_kernel, len(blocks), start),
+        functools.partial(product_kernel, len(blocks), fetched, start),
         out_shape=jax.ShapeDtypeStruct((length, width), jnp.float32),
-        in_specs=[VMEM] * (len(blocks) + 1 + len(given)),
+        in_specs=[ANY if k in fetched else VMEM for k in range(len(blocks))] + [VMEM] * (1 + len(given)),
         out_specs=VMEM,
+        scratch_shapes=scratch if fetched else [],
         compiler_params=pltpu.CompilerParams(vmem_limit_bytes=LIMIT),
         cost_estimate=pl.CostEstimate(
             flops=2 * length * depth * width,
@@ -329,7 +353,8 @@
     place = jnp.where(group % 2 == 0, group // 2, members - (group + 1) // 2)
     own_half = occ_place * half_blocks if cores == 2 else 0
 
-    ring_steps = sorted([*range((members + 1) // 2), *range(-(members // 2), 0)], key=abs)
+    ring_steps = [*range((members + 1) // 2), *range(-(members // 2), 0)]
+    ring_steps.sort(key=lambda step: (abs(step) == 1, abs(step)))
 
     ring_place = (place - jnp.array(ring_steps, jnp.int32)) % members
     ring_group = jnp.where(ring_place < evens, 2 * ring_place, 2 * (members - ring_place) - 1)
@@ -376,9 +401,10 @@
         for step in range(1, members - ups):
             blocks[-step] = lax.ppermute(blocks[1 - step], "vir", backward)
         arrived = [blocks[step] if step in blocks else blocks[step + members] for step in ring_steps]
-        for_near = product(arrived, near_all)
+        fetched = tuple(k for k, step in enumerate(ring_steps) if step in FETCHED.get(index, ()))
+        for_near = product(arrived, near_all, fetched)
         from_near = lax.ppermute(for_near, "vir", across)
-        rest = product(arrived, kept_all, base, start)
+        rest = product(arrived, kept_all, fetched, base, start)
         raws.append(rest + from_near)
 
     if cores == 2:

time: 135 us -> 136 us (level)
  transfers between devices with their start and end apart: 41 -> 41, of which waited for: 14 -> 14; matrix products, arithmetic and copies ran while one was open for 4% -> 4% of each run, Pallas kernels for 18% -> 19%
where the time goes in v2:
time: 136 us; the launch traced here: 135 us
  waiting for transfers between devices  50.4 us (37%)
  starting transfers between devices  41.4 us (30%)
  Pallas kernels  31.9 us (23%)
  local copies, waits for them, and re-layouts  6.64 us (5%)
  matrix products  2.87 us (2%)
    ppermute x14, waiting for transfers between devices, shards(): blocks[-step] = lax.ppermute(blocks[1 - step], 'vir', backward)  26.4 us
    ppermute x14, starting transfers between devices, shards(): blocks[step] = lax.ppermute(blocks[step - 1], 'vir', forward)  20.7 us
    ppermute x4, waiting for transfers between devices, shards(): from_near = lax.ppermute(for_near, 'vir', across)  15.1 us
    pallas_call x8, Pallas kernels, product(): pl.pallas_call(functools.partial(product_kernel, len(blocks), fetched, st...  14.4 us
    ppermute x14, starting transfers between devices, shards(): blocks[-step] = lax.ppermute(blocks[1 - step], 'vir', backward)  11.8 us
    ppermute x14, waiting for transfers between devices, shards(): blocks[step] = lax.ppermute(blocks[step - 1], 'vir', forward)  8.78 us
    pallas_call x2, Pallas kernels, prepare(): pl.pallas_call(functools.partial(prepare_kernel, cols), out_shape=jax.Sha...  6.91 us
    unnamed x68, local copies, waits for them, and re-layouts  4.83 us
  transfers between devices with their start and end apart: 41, of which 14 were waited for; matrix products, arithmetic and copies ran while one was open for 4% of the time, Pallas kernels for 19%

profile of v2, /device:TPU:0, one launch (start us, length us, event | category | flops | bytes accessed | tf_op | source)
XLA Modules:
  0.0 135.2 jit_solution(4598601701775375672)
XLA Ops:
  0.0 3.1 %parts.2 = (bf16[384,1536]{1,0:T(8,128)(2,1)}, bf16[360,384]{1,0:T(8,128)(2,1)}, bf16[320,384]{1,0:T(8,128)(2,1)}, bf16[256,384]{1,0:T(8,128)(2,1)}, bf16[192,384]{1,0:T(8,128)(2,1)}) custom-call(s32[1]{0:T(128)} %bitcast.side_ref, bf16[384,3072]{1,0:T(8,128)(2,1)} %refs_0_.3, bf16[1128,384]{1,0:T(8,128)(2,1)} %refs_1_.1), custom_call_target="tpu_custom_call" | custom-call | bytes 4718592 | tf_op jit(solution)/shard_map/parts/pallas_call | solution.py:66
  3.1 3.0 %collective-permute-start.10 = (bf16[384,1536]{1,0:T(8,128)(2,1)}, bf16[384,1536]{1,0:T(8,128)(2,1)}, u32[]{:S(2)}, u32[]{:S(2)}) collective-permute-start(bf16[384,1536]{1,0:T(8,128)(2,1)} %get-tuple-element.12), channel_id=1, source_target_pairs={{0,1},{1,0},{2,3},{3,2},{4,5},{5,4},{6,7},{7,6},{8,9},{9,8},{10,11... | collective-permute-start | bytes 3538952 | tf_op jit(solution)/shard_map/ppermute | solution.py:378
  6.1 1.6 %collective-permute-start.21 = (bf16[256,384]{1,0:T(8,128)(2,1)}, bf16[256,384]{1,0:T(8,128)(2,1)S(1)}, u32[]{:S(2)}, u32[]{:S(2)}) collective-permute-start(bf16[256,384]{1,0:T(8,128)(2,1)} %get-tuple-element.14.refs_0_), channel_id=1, source_target_pairs={{0,4},{4,8},{8,12},{12,14},{14,10},{10,6},{6,2},{2,0},{1,5},{5,9},... | collective-permute-start | bytes 589832 | tf_op jit(solution)/shard_map/ppermute | solution.py:400
  8.2 1.6 %collective-permute-start.29 = (bf16[192,384]{1,0:T(8,128)(2,1)}, bf16[192,384]{1,0:T(8,128)(2,1)S(1)}, u32[]{:S(2)}, u32[]{:S(2)}) collective-permute-start(bf16[192,384]{1,0:T(8,128)(2,1)} %get-tuple-element.15.refs_0_), channel_id=1, source_target_pairs={{0,4},{4,8},{8,12},{12,14},{14,10},{10,6},{6,2},{2,0},{1,5},{5,9},... | collective-permute-start | bytes 442376 | tf_op jit(solution)/shard_map/ppermute | solution.py:400
  10.2 4.5 %collective-permute-done.31.refs_7_ = bf16[192,384]{1,0:T(8,128)(2,1)S(1)} collective-permute-done((bf16[192,384]{1,0:T(8,128)(2,1)}, bf16[192,384]{1,0:T(8,128)(2,1)S(1)}, u32[]{:S(2)}, u32[]{:S(2)}) %collective-permute-start.31) | collective-permute-done | bytes 147488 | tf_op jit(solution)/shard_map/ppermute | solution.py:402
  14.7 1.6 %collective-permute-start.1 = (bf16[360,384]{1,0:T(8,128)(2,1)}, bf16[360,384]{1,0:T(8,128)(2,1)}, u32[]{:S(2)}, u32[]{:S(2)}) collective-permute-start(bf16[360,384]{1,0:T(8,128)(2,1)} %get-tuple-element.11.refs_0_), channel_id=1, source_target_pairs={{0,4},{4,8},{8,12},{12,14},{14,10},{10,6},{6,2},{2,0},{1,5},{5,9},... | collective-permute-start | bytes 829448 | tf_op jit(solution)/shard_map/ppermute | solution.py:400
  16.2 1.1 collective-permute-done.29.refs_6_
  17.3 1.5 %collective-permute-start.15 = (bf16[320,384]{1,0:T(8,128)(2,1)}, bf16[320,384]{1,0:T(8,128)(2,1)}, u32[]{:S(2)}, u32[]{:S(2)}) collective-permute-start(bf16[320,384]{1,0:T(8,128)(2,1)} %get-tuple-element.13.refs_0_), channel_id=1, source_target_pairs={{4,0},{8,4},{12,8},{14,12},{10,14},{6,10},{2,6},{0,2},{5,1},{9,5},... | collective-permute-start | bytes 737288 | tf_op jit(solution)/shard_map/ppermute | solution.py:402
  19.3 1.5 %collective-permute-start.3 = (bf16[360,384]{1,0:T(8,128)(2,1)}, bf16[360,384]{1,0:T(8,128)(2,1)}, u32[]{:S(2)}, u32[]{:S(2)}) collective-permute-start(bf16[360,384]{1,0:T(8,128)(2,1)} %get-tuple-element.11.refs_0_), channel_id=1, source_target_pairs={{4,0},{8,4},{12,8},{14,12},{10,14},{6,10},{2,6},{0,2},{5,1},{9,5},... | collective-permute-start | bytes 829448 | tf_op jit(solution)/shard_map/ppermute | solution.py:402
  20.8 5.0 %collective-permute-done.15.refs_7_ = bf16[320,384]{1,0:T(8,128)(2,1)} collective-permute-done((bf16[320,384]{1,0:T(8,128)(2,1)}, bf16[320,384]{1,0:T(8,128)(2,1)}, u32[]{:S(2)}, u32[]{:S(2)}) %collective-permute-start.15) | collective-permute-done | bytes 245792 | tf_op jit(solution)/shard_map/ppermute | solution.py:402
  25.8 1.6 %collective-permute-start.22 = (bf16[256,384]{1,0:T(8,128)(2,1)S(1)}, bf16[256,384]{1,0:T(8,128)(2,1)S(1)}, u32[]{:S(2)}, u32[]{:S(2)}) collective-permute-start(bf16[256,384]{1,0:T(8,128)(2,1)S(1)} %collective-permute-done.21.refs_6_), channel_id=1, source_target_pairs={{0,4},{4,8},{8,12},{12,14},{14,10},{10,6},{6,2},{2,0},{1,5},{5,9},... | collective-permute-start | bytes 589832 | tf_op jit(solution)/shard_map/ppermute | solution.py:400
  28.1 1.2 collective-permute-done.13.refs_6_
  29.3 0.9 collective-permute-start.32
  30.8 1.1 collective-permute-start.30
  32.6 0.9 collective-permute-start.24
  34.2 1.8 %collective-permute-done.32.refs_2_ = bf16[192,384]{1,0:T(8,128)(2,1)S(1)} collective-permute-done((bf16[192,384]{1,0:T(8,128)(2,1)S(1)}, bf16[192,384]{1,0:T(8,128)(2,1)S(1)}, u32[]{:S(2)}, u32[]{:S(2)}) %collective-permute-start.32) | collective-permute-done | bytes 147488 | tf_op jit(solution)/shard_map/ppermute | solution.py:402
  36.0 0.9 collective-permute-start.16
  36.9 1.1 collective-permute-start.14
  38.0 1.0 collective-permute-start.34
  39.7 1.2 collective-permute-start.2
  40.9 4.7 %collective-permute-done.34.refs_4_ = bf16[192,384]{1,0:T(8,128)(2,1)S(1)} collective-permute-done((bf16[192,384]{1,0:T(8,128)(2,1)S(1)}, bf16[192,384]{1,0:T(8,128)(2,1)S(1)}, u32[]{:S(2)}, u32[]{:S(2)}) %collective-permute-start.34) | collective-permute-done | bytes 147488 | tf_op jit(solution)/shard_map/ppermute | solution.py:402
  46.2 1.4 %collective-permute-start.4 = (bf16[360,384]{1,0:T(8,128)(2,1)}, bf16[360,384]{1,0:T(8,128)(2,1)}, u32[]{:S(2)}, u32[]{:S(2)}) collective-permute-start(bf16[360,384]{1,0:T(8,128)(2,1)} %collective-permute-done.3.refs_7_), channel_id=1, source_target_pairs={{4,0},{8,4},{12,8},{14,12},{10,14},{6,10},{2,6},{0,2},{5,1},{9,5},... | collective-permute-start | bytes 829448 | tf_op jit(solution)/shard_map/ppermute | solution.py:402
  49.5 4.7 %collective-permute-done.4.refs_2_ = bf16[360,384]{1,0:T(8,128)(2,1)} collective-permute-done((bf16[360,384]{1,0:T(8,128)(2,1)}, bf16[360,384]{1,0:T(8,128)(2,1)}, u32[]{:S(2)}, u32[]{:S(2)}) %collective-permute-start.4) | collective-permute-done | bytes 276512 | tf_op jit(solution)/shard_map/ppermute | solution.py:402
  55.4 1.6 %collective-permute-start.18 = (bf16[320,384]{1,0:T(8,128)(2,1)}, bf16[320,384]{1,0:T(8,128)(2,1)}, u32[]{:S(2)}, u32[]{:S(2)}) collective-permute-start(bf16[320,384]{1,0:T(8,128)(2,1)} %collective-permute-done.16.refs_2_), channel_id=1, source_target_pairs={{4,0},{8,4},{12,8},{14,12},{10,14},{6,10},{2,6},{0,2},{5,1},{9,5},... | collective-permute-start | bytes 737288 | tf_op jit(solution)/shard_map/ppermute | solution.py:402
  57.2 5.0 %collective-permute-done.26.refs_4_ = bf16[256,384]{1,0:T(8,128)(2,1)S(1)} collective-permute-done((bf16[256,384]{1,0:T(8,128)(2,1)}, bf16[256,384]{1,0:T(8,128)(2,1)S(1)}, u32[]{:S(2)}, u32[]{:S(2)}) %collective-permute-start.26) | collective-permute-done | bytes 196640 | tf_op jit(solution)/shard_map/ppermute | solution.py:402
  62.9 1.7 %collective-permute-start.5 = (bf16[360,384]{1,0:T(8,128)(2,1)}, bf16[360,384]{1,0:T(8,128)(2,1)S(1)}, u32[]{:S(2)}, u32[]{:S(2)}) collective-permute-start(bf16[360,384]{1,0:T(8,128)(2,1)} %collective-permute-done.2.refs_1_), channel_id=1, source_target_pairs={{0,4},{4,8},{8,12},{12,14},{14,10},{10,6},{6,2},{2,0},{1,5},{5,9},... | collective-permute-start | bytes 829448 | tf_op jit(solution)/shard_map/ppermute | solution.py:400
  65.3 1.6 %collective-permute-start.27 = (bf16[256,384]{1,0:T(8,128)(2,1)S(1)}, bf16[256,384]{1,0:T(8,128)(2,1)S(1)}, u32[]{:S(2)}, u32[]{:S(2)}) collective-permute-start(bf16[256,384]{1,0:T(8,128)(2,1)S(1)} %collective-permute-done.25.refs_3_), channel_id=1, source_target_pairs={{0,4},{4,8},{8,12},{12,14},{14,10},{10,6},{6,2},{2,0},{1,5},{5,9},... | collective-permute-start | bytes 589832 | tf_op jit(solution)/shard_map/ppermute | solution.py:400
  67.2 6.0 %collective-permute-done.27.refs_5_ = bf16[256,384]{1,0:T(8,128)(2,1)S(1)} collective-permute-done((bf16[256,384]{1,0:T(8,128)(2,1)S(1)}, bf16[256,384]{1,0:T(8,128)(2,1)S(1)}, u32[]{:S(2)}, u32[]{:S(2)}) %collective-permute-start.27) | collective-permute-done | bytes 196640 | tf_op jit(solution)/shard_map/ppermute | solution.py:400
  73.2 2.5 %collective-permute-start.17 = (bf16[320,384]{1,0:T(8,128)(2,1)}, bf16[320,384]{1,0:T(8,128)(2,1)S(1)}, u32[]{:S(2)}, u32[]{:S(2)}) collective-permute-start(bf16[320,384]{1,0:T(8,128)(2,1)} %collective-permute-done.14.refs_1_), channel_id=1, source_target_pairs={{0,4},{4,8},{8,12},{12,14},{14,10},{10,6},{6,2},{2,0},{1,5},{5,9},... | collective-permute-start | bytes 737288 | tf_op jit(solution)/shard_map/ppermute | solution.py:400
  75.8 1.9 %collective-permute-start.7 = (bf16[360,384]{1,0:T(8,128)(2,1)S(1)}, bf16[360,384]{1,0:T(8,128)(2,1)S(1)}, u32[]{:S(2)}, u32[]{:S(2)}) collective-permute-start(bf16[360,384]{1,0:T(8,128)(2,1)S(1)} %collective-permute-done.5.refs_3_), channel_id=1, source_target_pairs={{0,4},{4,8},{8,12},{12,14},{14,10},{10,6},{6,2},{2,0},{1,5},{5,9},... | collective-permute-start | bytes 829448 | tf_op jit(solution)/shard_map/ppermute | solution.py:400
  77.8 1.3 constant_dynamic-update-slice_fusion
  79.2 3.9 %prepare.3.refs_8_ = bf16[3072,384]{1,0:T(8,128)(2,1)S(1)} custom-call(s32[17]{0:T(128)S(1)} %get-tuple-element.19.index_ref, s32[48,48]{1,0:T(8,128)S(1)} %copy-done.27, bf16[384,1536]{1,0:T(8,128)(2,1)} %collective-permute-done.10.refs_0_, bf16[384,1536]{1,0:T(8,128)(2,1)} %collective-permute-done.11.refs_1_), custom_call_target="tpu_custom_call" | custom-call | bytes 4718592 | tf_op jit(solution)/shard_map/prepare/pallas_call | solution.py:106
  83.2 1.0 product.13
  84.3 2.0 %collective-permute-start.33 = (bf16[192,384]{1,0:T(8,128)(2,1)S(1)}, bf16[192,384]{1,0:T(8,128)(2,1)S(1)}, u32[]{:S(2)}, u32[]{:S(2)}) collective-permute-start(bf16[192,384]{1,0:T(8,128)(2,1)S(1)} %copy-done.24), channel_id=1, source_target_pairs={{0,4},{4,8},{8,12},{12,14},{14,10},{10,6},{6,2},{2,0},{1,5},{5,9},... | collective-permute-start | bytes 442376 | tf_op jit(solution)/shard_map/ppermute | solution.py:400
  87.0 2.7 %product.11 = f32[320,384]{1,0:T(8,128)S(1)} custom-call(bf16[320,384]{1,0:T(8,128)(2,1)S(1)} %copy-done.2, bf16[320,384]{1,0:T(8,128)(2,1)} %collective-permute-done.14.refs_1_, bf16[320,384]{1,0:T(8,128)(2,1)} %collective-permute-done.16.refs_2_, bf16[320,384]{1,0:T(8,128)(2,1)S(1)} %collective-permute-done.17.refs_3_, ...), custom_call_target="tpu_custom_call" | custom-call | flops 754974720 | bytes 4325376 | tf_op jit(solution)/shard_map/product/pallas_call | solution.py:153
  90.2 1.6 %collective-permute-start.20 = (f32[320,384]{1,0:T(8,128)S(1)}, f32[320,384]{1,0:T(8,128)S(1)}, u32[]{:S(2)}, u32[]{:S(2)}) collective-permute-start(f32[320,384]{1,0:T(8,128)S(1)} %product.11), channel_id=1, source_target_pairs={{0,1},{1,0},{2,3},{3,2},{4,5},{5,4},{6,7},{7,6},{8,9},{9,8},{10,11... | collective-permute-start | bytes 1474568 | tf_op jit(solution)/shard_map/ppermute | solution.py:406
  91.8 2.7 %product.9 = f32[360,384]{1,0:T(8,128)S(1)} custom-call(bf16[360,384]{1,0:T(8,128)(2,1)S(1)} %copy-done.1, bf16[360,384]{1,0:T(8,128)(2,1)} %collective-permute-done.2.refs_1_, bf16[360,384]{1,0:T(8,128)(2,1)} %collective-permute-done.4.refs_2_, bf16[360,384]{1,0:T(8,128)(2,1)S(1)} %collective-permute-done.5.refs_3_, ...), custom_call_target="tpu_custom_call" | custom-call | flops 849346560 | bytes 4571136 | tf_op jit(solution)/shard_map/product/pallas_call | solution.py:153
  95.0 2.9 %fusion.refs_9_ = f32[1128,384]{1,0:T(8,128)S(1)} fusion(bf16[2256,384]{1,0:T(8,128)(2,1)S(1)} %constant_dynamic-update-slice_fusion, bf16[1128,2256]{1,0:T(8,128)(2,1)S(1)} %bitcast.11, bf16[1128,384]{1,0:T(8,128)(2,1)S(1)} %copy-done.28, f32[1128]{0:T(1024)S(1)} %select_reduce_fusion), kind=kOutput, calls=%fused_computation.1 | convolution fusion | flops 1955681280 | bytes 9425568 | tf_op jit(solution)/shard_map/dot_general | solution.py:392
  97.9 3.0 %prepare.2.refs_8_ = bf16[3072,384]{1,0:T(8,128)(2,1)S(1)} custom-call(s32[17]{0:T(128)S(1)} %get-tuple-element.20.index_ref, s32[48,48]{1,0:T(8,128)S(1)} %copy-done.27, bf16[384,1536]{1,0:T(8,128)(2,1)S(1)} %parts.3.refs_0_, bf16[384,1536]{1,0:T(8,128)(2,1)S(1)} %collective-permute-done.8.refs_1_), custom_call_target="tpu_custom_call" | custom-call | bytes 4718592 | tf_op jit(solution)/shard_map/prepare/pallas_call | solution.py:106
  101.0 0.8 product.15
  101.7 1.7 %collective-permute-start.36 = (f32[192,384]{1,0:T(8,128)S(1)}, f32[192,384]{1,0:T(8,128)S(1)}, u32[]{:S(2)}, u32[]{:S(2)}) collective-permute-start(f32[192,384]{1,0:T(8,128)S(1)} %product.15), channel_id=1, source_target_pairs={{0,1},{1,0},{2,3},{3,2},{4,5},{5,4},{6,7},{7,6},{8,9},{9,8},{10,11... | collective-permute-start | bytes 884744 | tf_op jit(solution)/shard_map/ppermute | solution.py:406
  103.4 2.8 %product.8 = f32[360,384]{1,0:T(8,128)S(1)} custom-call(bf16[360,384]{1,0:T(8,128)(2,1)S(1)} %copy-done.1, bf16[360,384]{1,0:T(8,128)(2,1)} %collective-permute-done.2.refs_1_, bf16[360,384]{1,0:T(8,128)(2,1)} %collective-permute-done.4.refs_2_, bf16[360,384]{1,0:T(8,128)(2,1)S(1)} %collective-permute-done.5.refs_3_, ...), custom_call_target="tpu_custom_call" | custom-call | flops 849346560 | bytes 4571136 | tf_op jit(solution)/shard_map/product/pallas_call | solution.py:153
  106.2 15.0 %collective-permute-done.12 = f32[360,384]{1,0:T(8,128)S(1)} collective-permute-done((f32[360,384]{1,0:T(8,128)S(1)}, f32[360,384]{1,0:T(8,128)S(1)}, u32[]{:S(2)}, u32[]{:S(2)}) %collective-permute-start.12) | collective-permute-done | bytes 552992 | tf_op jit(solution)/shard_map/ppermute | solution.py:406
  121.4 2.7 %product.10 = f32[320,384]{1,0:T(8,128)S(1)} custom-call(bf16[320,384]{1,0:T(8,128)(2,1)S(1)} %copy-done.2, bf16[320,384]{1,0:T(8,128)(2,1)} %collective-permute-done.14.refs_1_, bf16[320,384]{1,0:T(8,128)(2,1)} %collective-permute-done.16.refs_2_, bf16[320,384]{1,0:T(8,128)(2,1)S(1)} %collective-permute-done.17.refs_3_, ...), custom_call_target="tpu_custom_call" | custom-call | flops 754974720 | bytes 4325376 | tf_op jit(solution)/shard_map/product/pallas_call | solution.py:153
  124.7 1.0 product.12
  126.4 0.8 product.14
  127.8 3.9 %mirror_early.1.refs_5_ = f32[1136,3,128]{2,1,0:T(4,128)S(1)} custom-call(s32[1128]{0:T(1024)S(1)} %maximum_select_fusion.index_ref, f32[360,384]{1,0:T(8,128)S(1)} %add.79.refs_0_, f32[320,384]{1,0:T(8,128)S(1)} %add.80.refs_1_, f32[256,384]{1,0:T(8,128)S(1)} %add.81.refs_2_, f32[360,384]{1,0:T(8,128)S(1)} %collective-permute-done.38.refs_3_, ...), custom_call_target="tpu_custom_call" | custom-call | flops 433152 | bytes 5197824 | tf_op jit(solution)/shard_map/mirror_early/pallas_call | solution.py:307
  131.7 3.3 %mirror_late.1 = (f32[1128,384]{1,0:T(8,128)}, f32[1136,3,128]{2,1,0:T(4,128)S(1)}) custom-call(s32[384]{0:T(512)S(1)} %and_select_fusion.2.target_ref, f32[360,384]{1,0:T(8,128)S(1)} %add.79.refs_0_, f32[320,384]{1,0:T(8,128)S(1)} %add.80.refs_1_, f32[256,384]{1,0:T(8,128)S(1)} %add.81.refs_2_, ...), custom_call_target="tpu_custom_call", output_to_operand_aliasing={{1}: (6, {})} | custom-call | flops 433152 | bytes 5197824 | tf_op jit(solution)/shard_map/mirror_late/pallas_call | solution.py:317
  (133 shorter events, 14.2 us)
Async XLA Ops:
  0.0 47.6 %copy-start = (bf16[384,3072]{1,0:T(8,128)(2,1)S(1)}, bf16[384,3072]{1,0:T(8,128)(2,1)}, u32[]{:S(2)}) copy-start(bf16[384,3072]{1,0:T(8,128)(2,1)} %refs_0_.3) | copy-start | bytes 7077892
  3.1 34.9 %collective-permute-start.10 = (bf16[384,1536]{1,0:T(8,128)(2,1)}, bf16[384,1536]{1,0:T(8,128)(2,1)}, u32[]{:S(2)}, u32[]{:S(2)}) collective-permute-start(bf16[384,1536]{1,0:T(8,128)(2,1)} %get-tuple-element.12), channel_id=1, source_target_pairs={{0,1},{1,0},{2,3},{3,2},{4,5},{5,4},{6,7},{7,6},{8,9},{9,8},{10,11... | collective-permute-start | bytes 3538952 | tf_op jit(solution)/shard_map/ppermute | solution.py:378
  6.1 12.7 %collective-permute-start.21 = (bf16[256,384]{1,0:T(8,128)(2,1)}, bf16[256,384]{1,0:T(8,128)(2,1)S(1)}, u32[]{:S(2)}, u32[]{:S(2)}) collective-permute-start(bf16[256,384]{1,0:T(8,128)(2,1)} %get-tuple-element.14.refs_0_), channel_id=1, source_target_pairs={{0,4},{4,8},{8,12},{12,14},{14,10},{10,6},{6,2},{2,0},{1,5},{5,9},... | collective-permute-start | bytes 589832 | tf_op jit(solution)/shard_map/ppermute | solution.py:400
  7.7 6.9 %collective-permute-start.31 = (bf16[192,384]{1,0:T(8,128)(2,1)}, bf16[192,384]{1,0:T(8,128)(2,1)S(1)}, u32[]{:S(2)}, u32[]{:S(2)}) collective-permute-start(bf16[192,384]{1,0:T(8,128)(2,1)} %get-tuple-element.15.refs_0_), channel_id=1, source_target_pairs={{4,0},{8,4},{12,8},{14,12},{10,14},{6,10},{2,6},{0,2},{5,1},{9,5},... | collective-permute-start | bytes 442376 | tf_op jit(solution)/shard_map/ppermute | solution.py:402
  8.2 9.1 %collective-permute-start.29 = (bf16[192,384]{1,0:T(8,128)(2,1)}, bf16[192,384]{1,0:T(8,128)(2,1)S(1)}, u32[]{:S(2)}, u32[]{:S(2)}) collective-permute-start(bf16[192,384]{1,0:T(8,128)(2,1)} %get-tuple-element.15.refs_0_), channel_id=1, source_target_pairs={{0,4},{4,8},{8,12},{12,14},{14,10},{10,6},{6,2},{2,0},{1,5},{5,9},... | collective-permute-start | bytes 442376 | tf_op jit(solution)/shard_map/ppermute | solution.py:400
  9.7 9.6 %collective-permute-start.23 = (bf16[256,384]{1,0:T(8,128)(2,1)}, bf16[256,384]{1,0:T(8,128)(2,1)S(1)}, u32[]{:S(2)}, u32[]{:S(2)}) collective-permute-start(bf16[256,384]{1,0:T(8,128)(2,1)} %get-tuple-element.14.refs_0_), channel_id=1, source_target_pairs={{4,0},{8,4},{12,8},{14,12},{10,14},{6,10},{2,6},{0,2},{5,1},{9,5},... | collective-permute-start | bytes 589832 | tf_op jit(solution)/shard_map/ppermute | solution.py:402
  14.7 16.2 %collective-permute-start.1 = (bf16[360,384]{1,0:T(8,128)(2,1)}, bf16[360,384]{1,0:T(8,128)(2,1)}, u32[]{:S(2)}, u32[]{:S(2)}) collective-permute-start(bf16[360,384]{1,0:T(8,128)(2,1)} %get-tuple-element.11.refs_0_), channel_id=1, source_target_pairs={{0,4},{4,8},{8,12},{12,14},{14,10},{10,6},{6,2},{2,0},{1,5},{5,9},... | collective-permute-start | bytes 829448 | tf_op jit(solution)/shard_map/ppermute | solution.py:400
  17.3 8.5 %collective-permute-start.15 = (bf16[320,384]{1,0:T(8,128)(2,1)}, bf16[320,384]{1,0:T(8,128)(2,1)}, u32[]{:S(2)}, u32[]{:S(2)}) collective-permute-start(bf16[320,384]{1,0:T(8,128)(2,1)} %get-tuple-element.13.refs_0_), channel_id=1, source_target_pairs={{4,0},{8,4},{12,8},{14,12},{10,14},{6,10},{2,6},{0,2},{5,1},{9,5},... | collective-permute-start | bytes 737288 | tf_op jit(solution)/shard_map/ppermute | solution.py:402
  18.8 10.5 %collective-permute-start.13 = (bf16[320,384]{1,0:T(8,128)(2,1)}, bf16[320,384]{1,0:T(8,128)(2,1)}, u32[]{:S(2)}, u32[]{:S(2)}) collective-permute-start(bf16[320,384]{1,0:T(8,128)(2,1)} %get-tuple-element.13.refs_0_), channel_id=1, source_target_pairs={{0,4},{4,8},{8,12},{12,14},{14,10},{10,6},{6,2},{2,0},{1,5},{5,9},... | collective-permute-start | bytes 737288 | tf_op jit(solution)/shard_map/ppermute | solution.py:400
  19.3 13.3 %collective-permute-start.3 = (bf16[360,384]{1,0:T(8,128)(2,1)}, bf16[360,384]{1,0:T(8,128)(2,1)}, u32[]{:S(2)}, u32[]{:S(2)}) collective-permute-start(bf16[360,384]{1,0:T(8,128)(2,1)} %get-tuple-element.11.refs_0_), channel_id=1, source_target_pairs={{4,0},{8,4},{12,8},{14,12},{10,14},{6,10},{2,6},{0,2},{5,1},{9,5},... | collective-permute-start | bytes 829448 | tf_op jit(solution)/shard_map/ppermute | solution.py:402
  25.8 12.2 %collective-permute-start.22 = (bf16[256,384]{1,0:T(8,128)(2,1)S(1)}, bf16[256,384]{1,0:T(8,128)(2,1)S(1)}, u32[]{:S(2)}, u32[]{:S(2)}) collective-permute-start(bf16[256,384]{1,0:T(8,128)(2,1)S(1)} %collective-permute-done.21.refs_6_), channel_id=1, source_target_pairs={{0,4},{4,8},{8,12},{12,14},{14,10},{10,6},{6,2},{2,0},{1,5},{5,9},... | collective-permute-start | bytes 589832 | tf_op jit(solution)/shard_map/ppermute | solution.py:400
  29.3 6.7 %collective-permute-start.32 = (bf16[192,384]{1,0:T(8,128)(2,1)S(1)}, bf16[192,384]{1,0:T(8,128)(2,1)S(1)}, u32[]{:S(2)}, u32[]{:S(2)}) collective-permute-start(bf16[192,384]{1,0:T(8,128)(2,1)S(1)} %collective-permute-done.31.refs_7_), channel_id=1, source_target_pairs={{4,0},{8,4},{12,8},{14,12},{10,14},{6,10},{2,6},{0,2},{5,1},{9,5},... | collective-permute-start | bytes 442376 | tf_op jit(solution)/shard_map/ppermute | solution.py:402
  30.8 6.1 %collective-permute-start.30 = (bf16[192,384]{1,0:T(8,128)(2,1)S(1)}, bf16[192,384]{1,0:T(8,128)(2,1)S(1)}, u32[]{:S(2)}, u32[]{:S(2)}) collective-permute-start(bf16[192,384]{1,0:T(8,128)(2,1)S(1)} %collective-permute-done.29.refs_6_), channel_id=1, source_target_pairs={{0,4},{4,8},{8,12},{12,14},{14,10},{10,6},{6,2},{2,0},{1,5},{5,9},... | collective-permute-start | bytes 442376 | tf_op jit(solution)/shard_map/ppermute | solution.py:400
  32.6 7.0 %collective-permute-start.24 = (bf16[256,384]{1,0:T(8,128)(2,1)S(1)}, bf16[256,384]{1,0:T(8,128)(2,1)S(1)}, u32[]{:S(2)}, u32[]{:S(2)}) collective-permute-start(bf16[256,384]{1,0:T(8,128)(2,1)S(1)} %collective-permute-done.23.refs_7_), channel_id=1, source_target_pairs={{4,0},{8,4},{12,8},{14,12},{10,14},{6,10},{2,6},{0,2},{5,1},{9,5},... | collective-permute-start | bytes 589832 | tf_op jit(solution)/shard_map/ppermute | solution.py:402
  36.0 11.8 %collective-permute-start.16 = (bf16[320,384]{1,0:T(8,128)(2,1)}, bf16[320,384]{1,0:T(8,128)(2,1)}, u32[]{:S(2)}, u32[]{:S(2)}) collective-permute-start(bf16[320,384]{1,0:T(8,128)(2,1)} %collective-permute-done.15.refs_7_), channel_id=1, source_target_pairs={{4,0},{8,4},{12,8},{14,12},{10,14},{6,10},{2,6},{0,2},{5,1},{9,5},... | collective-permute-start | bytes 737288 | tf_op jit(solution)/shard_map/ppermute | solution.py:402
  36.9 11.0 %collective-permute-start.14 = (bf16[320,384]{1,0:T(8,128)(2,1)}, bf16[320,384]{1,0:T(8,128)(2,1)}, u32[]{:S(2)}, u32[]{:S(2)}) collective-permute-start(bf16[320,384]{1,0:T(8,128)(2,1)} %collective-permute-done.13.refs_6_), channel_id=1, source_target_pairs={{0,4},{4,8},{8,12},{12,14},{14,10},{10,6},{6,2},{2,0},{1,5},{5,9},... | collective-permute-start | bytes 737288 | tf_op jit(solution)/shard_map/ppermute | solution.py:400
  38.0 37.8 %collective-permute-start.11 = (bf16[384,1536]{1,0:T(8,128)(2,1)}, bf16[384,1536]{1,0:T(8,128)(2,1)}, u32[]{:S(2)}, u32[]{:S(2)}) collective-permute-start(bf16[384,1536]{1,0:T(8,128)(2,1)} %collective-permute-done.10.refs_0_), channel_id=1, source_target_pairs={{0,16},{16,0},{1,17},{17,1},{2,18},{18,2},{3,19},{19,3},{4,20},{20... | collective-permute-start | bytes 3538952 | tf_op jit(solution)/shard_map/ppermute | solution.py:35
  38.0 7.5 %collective-permute-start.34 = (bf16[192,384]{1,0:T(8,128)(2,1)S(1)}, bf16[192,384]{1,0:T(8,128)(2,1)S(1)}, u32[]{:S(2)}, u32[]{:S(2)}) collective-permute-start(bf16[192,384]{1,0:T(8,128)(2,1)S(1)} %collective-permute-done.32.refs_2_), channel_id=1, source_target_pairs={{4,0},{8,4},{12,8},{14,12},{10,14},{6,10},{2,6},{0,2},{5,1},{9,5},... | collective-permute-start | bytes 442376 | tf_op jit(solution)/shard_map/ppermute | solution.py:402
  39.7 9.7 %collective-permute-start.2 = (bf16[360,384]{1,0:T(8,128)(2,1)}, bf16[360,384]{1,0:T(8,128)(2,1)}, u32[]{:S(2)}, u32[]{:S(2)}) collective-permute-start(bf16[360,384]{1,0:T(8,128)(2,1)} %collective-permute-done.1.refs_6_), channel_id=1, source_target_pairs={{0,4},{4,8},{8,12},{12,14},{14,10},{10,6},{6,2},{2,0},{1,5},{5,9},... | collective-permute-start | bytes 829448 | tf_op jit(solution)/shard_map/ppermute | solution.py:400
  46.2 8.0 %collective-permute-start.4 = (bf16[360,384]{1,0:T(8,128)(2,1)}, bf16[360,384]{1,0:T(8,128)(2,1)}, u32[]{:S(2)}, u32[]{:S(2)}) collective-permute-start(bf16[360,384]{1,0:T(8,128)(2,1)} %collective-permute-done.3.refs_7_), channel_id=1, source_target_pairs={{4,0},{8,4},{12,8},{14,12},{10,14},{6,10},{2,6},{0,2},{5,1},{9,5},... | collective-permute-start | bytes 829448 | tf_op jit(solution)/shard_map/ppermute | solution.py:402
  47.6 9.5 %copy-start.30 = (s32[1128,2]{0,1:T(2,128)S(1)}, s32[1128,2]{0,1:T(2,128)}, u32[]{:S(2)}) copy-start(s32[1128,2]{0,1:T(2,128)} %param.13) | copy-start | bytes 27076
  47.6 9.5 %copy-start.31 = (f32[48]{0:T(128)S(1)}, f32[48]{0:T(128)}, u32[]{:S(2)}) copy-start(f32[48]{0:T(128)} %param.12) | copy-start | bytes 580
  47.8 27.8 %collective-permute-start.9 = (bf16[1128,384]{1,0:T(8,128)(2,1)}, bf16[1128,384]{1,0:T(8,128)(2,1)}, u32[]{:S(2)}, u32[]{:S(2)}) collective-permute-start(bf16[1128,384]{1,0:T(8,128)(2,1)} %refs_1_.1), channel_id=1, source_target_pairs={{0,16},{16,0},{1,17},{17,1},{2,18},{18,2},{3,19},{19,3},{4,20},{20... | collective-permute-start | bytes 2598920 | tf_op jit(solution)/shard_map/ppermute | solution.py:35
  47.9 7.5 %collective-permute-start.25 = (bf16[256,384]{1,0:T(8,128)(2,1)}, bf16[256,384]{1,0:T(8,128)(2,1)S(1)}, u32[]{:S(2)}, u32[]{:S(2)}) collective-permute-start(bf16[256,384]{1,0:T(8,128)(2,1)} %copy-done.8), channel_id=1, source_target_pairs={{0,4},{4,8},{8,12},{12,14},{14,10},{10,6},{6,2},{2,0},{1,5},{5,9},... | collective-permute-start | bytes 589832 | tf_op jit(solution)/shard_map/ppermute | solution.py:400
  49.3 45.2 %collective-permute-start.8 = (bf16[384,1536]{1,0:T(8,128)(2,1)S(1)}, bf16[384,1536]{1,0:T(8,128)(2,1)S(1)}, u32[]{:S(2)}, u32[]{:S(2)}) collective-permute-start(bf16[384,1536]{1,0:T(8,128)(2,1)S(1)} %parts.3.refs_0_), channel_id=1, source_target_pairs={{0,16},{16,0},{1,17},{17,1},{2,18},{18,2},{3,19},{19,3},{4,20},{20... | collective-permute-start | bytes 3538952 | tf_op jit(solution)/shard_map/ppermute | solution.py:35
  54.2 8.0 %collective-permute-start.26 = (bf16[256,384]{1,0:T(8,128)(2,1)}, bf16[256,384]{1,0:T(8,128)(2,1)S(1)}, u32[]{:S(2)}, u32[]{:S(2)}) collective-permute-start(bf16[256,384]{1,0:T(8,128)(2,1)} %copy-done.10), channel_id=1, source_target_pairs={{4,0},{8,4},{12,8},{14,12},{10,14},{6,10},{2,6},{0,2},{5,1},{9,5},... | collective-permute-start | bytes 589832 | tf_op jit(solution)/shard_map/ppermute | solution.py:402
  55.4 11.8 %copy-start.12 = (bf16[256,384]{1,0:T(8,128)(2,1)}, bf16[256,384]{1,0:T(8,128)(2,1)S(1)}, u32[]{:S(2)}) copy-start(bf16[256,384]{1,0:T(8,128)(2,1)S(1)} %collective-permute-done.25.refs_3_) | copy-start | bytes 589828
  55.4 9.9 %collective-permute-start.18 = (bf16[320,384]{1,0:T(8,128)(2,1)}, bf16[320,384]{1,0:T(8,128)(2,1)}, u32[]{:S(2)}, u32[]{:S(2)}) collective-permute-start(bf16[320,384]{1,0:T(8,128)(2,1)} %collective-permute-done.16.refs_2_), channel_id=1, source_target_pairs={{4,0},{8,4},{12,8},{14,12},{10,14},{6,10},{2,6},{0,2},{5,1},{9,5},... | collective-permute-start | bytes 737288 | tf_op jit(solution)/shard_map/ppermute | solution.py:402
  62.9 12.7 %collective-permute-start.5 = (bf16[360,384]{1,0:T(8,128)(2,1)}, bf16[360,384]{1,0:T(8,128)(2,1)S(1)}, u32[]{:S(2)}, u32[]{:S(2)}) collective-permute-start(bf16[360,384]{1,0:T(8,128)(2,1)} %collective-permute-done.2.refs_1_), channel_id=1, source_target_pairs={{0,4},{4,8},{8,12},{12,14},{14,10},{10,6},{6,2},{2,0},{1,5},{5,9},... | collective-permute-start | bytes 829448 | tf_op jit(solution)/shard_map/ppermute | solution.py:400
  65.3 7.9 %collective-permute-start.27 = (bf16[256,384]{1,0:T(8,128)(2,1)S(1)}, bf16[256,384]{1,0:T(8,128)(2,1)S(1)}, u32[]{:S(2)}, u32[]{:S(2)}) collective-permute-start(bf16[256,384]{1,0:T(8,128)(2,1)S(1)} %collective-permute-done.25.refs_3_), channel_id=1, source_target_pairs={{0,4},{4,8},{8,12},{12,14},{14,10},{10,6},{6,2},{2,0},{1,5},{5,9},... | collective-permute-start | bytes 589832 | tf_op jit(solution)/shard_map/ppermute | solution.py:400
  67.0 12.1 %copy-start.27 = (s32[48,48]{1,0:T(8,128)S(1)}, s32[48,48]{1,0:T(8,128)}, u32[]{:S(2)}) copy-start(s32[48,48]{1,0:T(8,128)} %map_hbm.3) | copy-start | bytes 27652
  73.2 11.1 %collective-permute-start.17 = (bf16[320,384]{1,0:T(8,128)(2,1)}, bf16[320,384]{1,0:T(8,128)(2,1)S(1)}, u32[]{:S(2)}, u32[]{:S(2)}) collective-permute-start(bf16[320,384]{1,0:T(8,128)(2,1)} %collective-permute-done.14.refs_1_), channel_id=1, source_target_pairs={{0,4},{4,8},{8,12},{12,14},{14,10},{10,6},{6,2},{2,0},{1,5},{5,9},... | collective-permute-start | bytes 737288 | tf_op jit(solution)/shard_map/ppermute | solution.py:400
  75.7 14.0 %collective-permute-start.6 = (bf16[360,384]{1,0:T(8,128)(2,1)}, bf16[360,384]{1,0:T(8,128)(2,1)S(1)}, u32[]{:S(2)}, u32[]{:S(2)}) collective-permute-start(bf16[360,384]{1,0:T(8,128)(2,1)} %collective-permute-done.4.refs_2_), channel_id=1, source_target_pairs={{4,0},{8,4},{12,8},{14,12},{10,14},{6,10},{2,6},{0,2},{5,1},{9,5},... | collective-permute-start | bytes 829448 | tf_op jit(solution)/shard_map/ppermute | solution.py:402
  75.7 10.9 %collective-permute-start.19 = (bf16[320,384]{1,0:T(8,128)(2,1)}, bf16[320,384]{1,0:T(8,128)(2,1)S(1)}, u32[]{:S(2)}, u32[]{:S(2)}) collective-permute-start(bf16[320,384]{1,0:T(8,128)(2,1)} %collective-permute-done.18.refs_4_), channel_id=1, source_target_pairs={{4,0},{8,4},{12,8},{14,12},{10,14},{6,10},{2,6},{0,2},{5,1},{9,5},... | collective-permute-start | bytes 737288 | tf_op jit(solution)/shard_map/ppermute | solution.py:402
  75.8 14.3 %collective-permute-start.7 = (bf16[360,384]{1,0:T(8,128)(2,1)S(1)}, bf16[360,384]{1,0:T(8,128)(2,1)S(1)}, u32[]{:S(2)}, u32[]{:S(2)}) collective-permute-start(bf16[360,384]{1,0:T(8,128)(2,1)S(1)} %collective-permute-done.5.refs_3_), channel_id=1, source_target_pairs={{0,4},{4,8},{8,12},{12,14},{14,10},{10,6},{6,2},{2,0},{1,5},{5,9},... | collective-permute-start | bytes 829448 | tf_op jit(solution)/shard_map/ppermute | solution.py:400
  83.2 11.8 %slice-start = ((s8[5197824]{0:T(1024)(128)(4,1)}), s8[4194304]{0:T(1024)(128)(4,1)S(1)}, s32[]{:S(2)}) async-start(s8[5197824]{0:T(1024)(128)(4,1)} %bitcast.10), calls=%async_computation | async-start | bytes 8388608
  84.2 10.8 %slice-start.1 = ((s8[5197824]{0:T(1024)(128)(4,1)}), s8[1003520]{0:T(1024)(128)(4,1)S(1)}, s32[]{:S(2)}) async-start(s8[5197824]{0:T(1024)(128)(4,1)} %bitcast.10), calls=%async_computation.1 | async-start | bytes 2007040
  84.3 16.6 %collective-permute-start.33 = (bf16[192,384]{1,0:T(8,128)(2,1)S(1)}, bf16[192,384]{1,0:T(8,128)(2,1)S(1)}, u32[]{:S(2)}, u32[]{:S(2)}) collective-permute-start(bf16[192,384]{1,0:T(8,128)(2,1)S(1)} %copy-done.24), channel_id=1, source_target_pairs={{0,4},{4,8},{8,12},{12,14},{14,10},{10,6},{6,2},{2,0},{1,5},{5,9},... | collective-permute-start | bytes 442376 | tf_op jit(solution)/shard_map/ppermute | solution.py:400
  86.6 14.3 %collective-permute-start.35 = (bf16[192,384]{1,0:T(8,128)(2,1)S(1)}, bf16[192,384]{1,0:T(8,128)(2,1)S(1)}, u32[]{:S(2)}, u32[]{:S(2)}) collective-permute-start(bf16[192,384]{1,0:T(8,128)(2,1)S(1)} %copy-done.26), channel_id=1, source_target_pairs={{4,0},{8,4},{12,8},{14,12},{10,14},{6,10},{2,6},{0,2},{5,1},{9,5},... | collective-permute-start | bytes 442376 | tf_op jit(solution)/shard_map/ppermute | solution.py:402
  89.7 36.1 %collective-permute-start.28 = (f32[256,384]{1,0:T(8,128)S(1)}, f32[256,384]{1,0:T(8,128)S(1)}, u32[]{:S(2)}, u32[]{:S(2)}) collective-permute-start(f32[256,384]{1,0:T(8,128)S(1)} %product.13), channel_id=1, source_target_pairs={{0,1},{1,0},{2,3},{3,2},{4,5},{5,4},{6,7},{7,6},{8,9},{9,8},{10,11... | collective-permute-start | bytes 1179656 | tf_op jit(solution)/shard_map/ppermute | solution.py:406
  90.2 34.0 %collective-permute-start.20 = (f32[320,384]{1,0:T(8,128)S(1)}, f32[320,384]{1,0:T(8,128)S(1)}, u32[]{:S(2)}, u32[]{:S(2)}) collective-permute-start(f32[320,384]{1,0:T(8,128)S(1)} %product.11), channel_id=1, source_target_pairs={{0,1},{1,0},{2,3},{3,2},{4,5},{5,4},{6,7},{7,6},{8,9},{9,8},{10,11... | collective-permute-start | bytes 1474568 | tf_op jit(solution)/shard_map/ppermute | solution.py:406
  94.5 26.7 %collective-permute-start.12 = (f32[360,384]{1,0:T(8,128)S(1)}, f32[360,384]{1,0:T(8,128)S(1)}, u32[]{:S(2)}, u32[]{:S(2)}) collective-permute-start(f32[360,384]{1,0:T(8,128)S(1)} %product.9), channel_id=1, source_target_pairs={{0,1},{1,0},{2,3},{3,2},{4,5},{5,4},{6,7},{7,6},{8,9},{9,8},{10,11... | collective-permute-start | bytes 1658888 | tf_op jit(solution)/shard_map/ppermute | solution.py:406
  101.7 25.4 %collective-permute-start.36 = (f32[192,384]{1,0:T(8,128)S(1)}, f32[192,384]{1,0:T(8,128)S(1)}, u32[]{:S(2)}, u32[]{:S(2)}) collective-permute-start(f32[192,384]{1,0:T(8,128)S(1)} %product.15), channel_id=1, source_target_pairs={{0,1},{1,0},{2,3},{3,2},{4,5},{5,4},{6,7},{7,6},{8,9},{9,8},{10,11... | collective-permute-start | bytes 884744 | tf_op jit(solution)/shard_map/ppermute | solution.py:406
  121.3 6.4 %collective-permute-start.38 = (f32[360,384]{1,0:T(8,128)S(1)}, f32[360,384]{1,0:T(8,128)S(1)}, u32[]{:S(2)}, u32[]{:S(2)}) collective-permute-start(f32[360,384]{1,0:T(8,128)S(1)} %add.79.refs_0_), channel_id=1, source_target_pairs={{0,16},{16,0},{1,17},{17,1},{2,18},{18,2},{3,19},{19,3},{4,20},{20... | collective-permute-start | bytes 1658888 | tf_op jit(solution)/shard_map/ppermute | solution.py:35
  124.2 3.6 %collective-permute-start.39 = (f32[320,384]{1,0:T(8,128)S(1)}, f32[320,384]{1,0:T(8,128)S(1)}, u32[]{:S(2)}, u32[]{:S(2)}) collective-permute-start(f32[320,384]{1,0:T(8,128)S(1)} %add.80.refs_1_), channel_id=1, source_target_pairs={{0,16},{16,0},{1,17},{17,1},{2,18},{18,2},{3,19},{19,3},{4,20},{20... | collective-permute-start | bytes 1474568 | tf_op jit(solution)/shard_map/ppermute | solution.py:35
  125.8 2.0 %collective-permute-start.40 = (f32[256,384]{1,0:T(8,128)S(1)}, f32[256,384]{1,0:T(8,128)S(1)}, u32[]{:S(2)}, u32[]{:S(2)}) collective-permute-start(f32[256,384]{1,0:T(8,128)S(1)} %add.81.refs_2_), channel_id=1, source_target_pairs={{0,16},{16,0},{1,17},{17,1},{2,18},{18,2},{3,19},{19,3},{4,20},{20... | collective-permute-start | bytes 1179656 | tf_op jit(solution)/shard_map/ppermute | solution.py:35
  125.9 1.7 %collective-permute-start = (s32[1128]{0:T(1024)S(1)}, s32[1128]{0:T(1024)S(1)}, u32[]{:S(2)}, u32[]{:S(2)}) collective-permute-start(s32[1128]{0:T(1024)S(1)} %copy-done.29), channel_id=1, source_target_pairs={{0,16},{16,0},{1,17},{17,1},{2,18},{18,2},{3,19},{19,3},{4,20},{20... | collective-permute-start | bytes 13544 | tf_op jit(solution)/shard_map/ppermute | solution.py:35
  127.2 4.5 %collective-permute-start.37 = (f32[192,384]{1,0:T(8,128)S(1)}, f32[192,384]{1,0:T(8,128)S(1)}, u32[]{:S(2)}, u32[]{:S(2)}) collective-permute-start(f32[192,384]{1,0:T(8,128)S(1)} %add.82.refs_3_), channel_id=1, source_target_pairs={{0,16},{16,0},{1,17},{17,1},{2,18},{18,2},{3,19},{19,3},{4,20},{20... | collective-permute-start | bytes 884744 | tf_op jit(solution)/shard_map/ppermute | solution.py:35
  (27 other events, 76.3 us)

commit v3 on v2

--- a/solution.py
+++ b/solution.py
@@ -246,7 +246,7 @@
         for c in range(piece.shape[1] // TILE):
             whole[pl.ds(offset + at, 8), c, :] = piece[pl.ds(at, 8), c * TILE : (c + 1) * TILE]
 
-    for_groups(piece.shape[0] // 8, 6, spread)
+    for_groups(piece.shape[0] // 8, 24, spread)
 
 
 def early_kernel(index_ref, *refs):
@@ -260,7 +260,7 @@
         for j in range(8):
             picked[g * 8 + j] = whole[index_ref[g * 8 + j]]
 
-    for_groups(index_ref.shape[0] // 8, 6, pick)
+    for_groups(index_ref.shape[0] // 8, 48, pick)
 
 
 def late_kernel(target_ref, *refs):
@@ -272,7 +272,7 @@
         for j in range(8):
             picked[target_ref[g * 8 + j]] = whole[g * 8 + j]
 
-    for_groups(target_ref.shape[0] // 8, 6, put)
+    for_groups(target_ref.shape[0] // 8, 24, put)
 
     odd = lax.broadcasted_iota(jnp.int32, (8, TILE), 1) % 2 == 1
 

time: 136 us -> 135 us (level)
  no operation moved by 1% of the time
where the time goes in v3:
time: 135 us
  waiting for transfers between devices  50.4 us (37%)
  starting transfers between devices  41.4 us (31%)
  Pallas kernels  31.2 us (23%)
  local copies, waits for them, and re-layouts  6.64 us (5%)
  matrix products  2.87 us (2%)
    ppermute x14, waiting for transfers between devices, shards(): blocks[-step] = lax.ppermute(blocks[1 - step], 'vir', backward)  26.4 us
    ppermute x14, starting transfers between devices, shards(): blocks[step] = lax.ppermute(blocks[step - 1], 'vir', forward)  20.7 us
    ppermute x4, waiting for transfers between devices, shards(): from_near = lax.ppermute(for_near, 'vir', across)  15.1 us
    pallas_call x8, Pallas kernels, product(): pl.pallas_call(functools.partial(product_kernel, len(blocks), fetched, st...  14.4 us
    ppermute x14, starting transfers between devices, shards(): blocks[-step] = lax.ppermute(blocks[1 - step], 'vir', backward)  11.8 us
    ppermute x14, waiting for transfers between devices, shards(): blocks[step] = lax.ppermute(blocks[step - 1], 'vir', forward)  8.78 us
    pallas_call x2, Pallas kernels, prepare(): pl.pallas_call(functools.partial(prepare_kernel, cols), out_shape=jax.Sha...  6.91 us
    unnamed x68, local copies, waits for them, and re-layouts  4.83 us
  transfers between devices with their start and end apart: 41, of which 14 were waited for; matrix products, arithmetic and copies ran while one was open for 4% of the time, Pallas kernels for 19%

profile of v3, /device:TPU:0, one launch (start us, length us, event | category | flops | bytes accessed | tf_op | source)
XLA Modules:
  0.0 134.6 jit_solution(2261071937309474764)
XLA Ops:
  0.0 3.1 %parts.2 = (bf16[384,1536]{1,0:T(8,128)(2,1)}, bf16[360,384]{1,0:T(8,128)(2,1)}, bf16[320,384]{1,0:T(8,128)(2,1)}, bf16[256,384]{1,0:T(8,128)(2,1)}, bf16[192,384]{1,0:T(8,128)(2,1)}) custom-call(s32[1]{0:T(128)} %bitcast.side_ref, bf16[384,3072]{1,0:T(8,128)(2,1)} %refs_0_.3, bf16[1128,384]{1,0:T(8,128)(2,1)} %refs_1_.1), custom_call_target="tpu_custom_call" | custom-call | bytes 4718592 | tf_op jit(solution)/shard_map/parts/pallas_call | solution.py:66
  3.1 3.0 %collective-permute-start.10 = (bf16[384,1536]{1,0:T(8,128)(2,1)}, bf16[384,1536]{1,0:T(8,128)(2,1)}, u32[]{:S(2)}, u32[]{:S(2)}) collective-permute-start(bf16[384,1536]{1,0:T(8,128)(2,1)} %get-tuple-element.12), channel_id=1, source_target_pairs={{0,1},{1,0},{2,3},{3,2},{4,5},{5,4},{6,7},{7,6},{8,9},{9,8},{10,11... | collective-permute-start | bytes 3538952 | tf_op jit(solution)/shard_map/ppermute | solution.py:378
  6.1 1.6 %collective-permute-start.21 = (bf16[256,384]{1,0:T(8,128)(2,1)}, bf16[256,384]{1,0:T(8,128)(2,1)S(1)}, u32[]{:S(2)}, u32[]{:S(2)}) collective-permute-start(bf16[256,384]{1,0:T(8,128)(2,1)} %get-tuple-element.14.refs_0_), channel_id=1, source_target_pairs={{0,4},{4,8},{8,12},{12,14},{14,10},{10,6},{6,2},{2,0},{1,5},{5,9},... | collective-permute-start | bytes 589832 | tf_op jit(solution)/shard_map/ppermute | solution.py:400
  8.2 1.6 %collective-permute-start.29 = (bf16[192,384]{1,0:T(8,128)(2,1)}, bf16[192,384]{1,0:T(8,128)(2,1)S(1)}, u32[]{:S(2)}, u32[]{:S(2)}) collective-permute-start(bf16[192,384]{1,0:T(8,128)(2,1)} %get-tuple-element.15.refs_0_), channel_id=1, source_target_pairs={{0,4},{4,8},{8,12},{12,14},{14,10},{10,6},{6,2},{2,0},{1,5},{5,9},... | collective-permute-start | bytes 442376 | tf_op jit(solution)/shard_map/ppermute | solution.py:400
  10.2 4.5 %collective-permute-done.31.refs_7_ = bf16[192,384]{1,0:T(8,128)(2,1)S(1)} collective-permute-done((bf16[192,384]{1,0:T(8,128)(2,1)}, bf16[192,384]{1,0:T(8,128)(2,1)S(1)}, u32[]{:S(2)}, u32[]{:S(2)}) %collective-permute-start.31) | collective-permute-done | bytes 147488 | tf_op jit(solution)/shard_map/ppermute | solution.py:402
  14.7 1.6 %collective-permute-start.1 = (bf16[360,384]{1,0:T(8,128)(2,1)}, bf16[360,384]{1,0:T(8,128)(2,1)}, u32[]{:S(2)}, u32[]{:S(2)}) collective-permute-start(bf16[360,384]{1,0:T(8,128)(2,1)} %get-tuple-element.11.refs_0_), channel_id=1, source_target_pairs={{0,4},{4,8},{8,12},{12,14},{14,10},{10,6},{6,2},{2,0},{1,5},{5,9},... | collective-permute-start | bytes 829448 | tf_op jit(solution)/shard_map/ppermute | solution.py:400
  16.2 1.1 collective-permute-done.29.refs_6_
  17.3 1.5 %collective-permute-start.15 = (bf16[320,384]{1,0:T(8,128)(2,1)}, bf16[320,384]{1,0:T(8,128)(2,1)}, u32[]{:S(2)}, u32[]{:S(2)}) collective-permute-start(bf16[320,384]{1,0:T(8,128)(2,1)} %get-tuple-element.13.refs_0_), channel_id=1, source_target_pairs={{4,0},{8,4},{12,8},{14,12},{10,14},{6,10},{2,6},{0,2},{5,1},{9,5},... | collective-permute-start | bytes 737288 | tf_op jit(solution)/shard_map/ppermute | solution.py:402
  19.3 1.5 %collective-permute-start.3 = (bf16[360,384]{1,0:T(8,128)(2,1)}, bf16[360,384]{1,0:T(8,128)(2,1)}, u32[]{:S(2)}, u32[]{:S(2)}) collective-permute-start(bf16[360,384]{1,0:T(8,128)(2,1)} %get-tuple-element.11.refs_0_), channel_id=1, source_target_pairs={{4,0},{8,4},{12,8},{14,12},{10,14},{6,10},{2,6},{0,2},{5,1},{9,5},... | collective-permute-start | bytes 829448 | tf_op jit(solution)/shard_map/ppermute | solution.py:402
  20.8 5.0 %collective-permute-done.15.refs_7_ = bf16[320,384]{1,0:T(8,128)(2,1)} collective-permute-done((bf16[320,384]{1,0:T(8,128)(2,1)}, bf16[320,384]{1,0:T(8,128)(2,1)}, u32[]{:S(2)}, u32[]{:S(2)}) %collective-permute-start.15) | collective-permute-done | bytes 245792 | tf_op jit(solution)/shard_map/ppermute | solution.py:402
  25.8 1.6 %collective-permute-start.22 = (bf16[256,384]{1,0:T(8,128)(2,1)S(1)}, bf16[256,384]{1,0:T(8,128)(2,1)S(1)}, u32[]{:S(2)}, u32[]{:S(2)}) collective-permute-start(bf16[256,384]{1,0:T(8,128)(2,1)S(1)} %collective-permute-done.21.refs_6_), channel_id=1, source_target_pairs={{0,4},{4,8},{8,12},{12,14},{14,10},{10,6},{6,2},{2,0},{1,5},{5,9},... | collective-permute-start | bytes 589832 | tf_op jit(solution)/shard_map/ppermute | solution.py:400
  28.1 1.2 collective-permute-done.13.refs_6_
  29.3 0.9 collective-permute-start.32
  30.8 1.1 collective-permute-start.30
  32.6 0.9 collective-permute-start.24
  34.2 1.8 %collective-permute-done.32.refs_2_ = bf16[192,384]{1,0:T(8,128)(2,1)S(1)} collective-permute-done((bf16[192,384]{1,0:T(8,128)(2,1)S(1)}, bf16[192,384]{1,0:T(8,128)(2,1)S(1)}, u32[]{:S(2)}, u32[]{:S(2)}) %collective-permute-start.32) | collective-permute-done | bytes 147488 | tf_op jit(solution)/shard_map/ppermute | solution.py:402
  36.0 0.9 collective-permute-start.16
  36.9 1.1 collective-permute-start.14
  38.0 1.0 collective-permute-start.34
  39.7 1.2 collective-permute-start.2
  40.9 4.7 %collective-permute-done.34.refs_4_ = bf16[192,384]{1,0:T(8,128)(2,1)S(1)} collective-permute-done((bf16[192,384]{1,0:T(8,128)(2,1)S(1)}, bf16[192,384]{1,0:T(8,128)(2,1)S(1)}, u32[]{:S(2)}, u32[]{:S(2)}) %collective-permute-start.34) | collective-permute-done | bytes 147488 | tf_op jit(solution)/shard_map/ppermute | solution.py:402
  46.2 1.4 %collective-permute-start.4 = (bf16[360,384]{1,0:T(8,128)(2,1)}, bf16[360,384]{1,0:T(8,128)(2,1)}, u32[]{:S(2)}, u32[]{:S(2)}) collective-permute-start(bf16[360,384]{1,0:T(8,128)(2,1)} %collective-permute-done.3.refs_7_), channel_id=1, source_target_pairs={{4,0},{8,4},{12,8},{14,12},{10,14},{6,10},{2,6},{0,2},{5,1},{9,5},... | collective-permute-start | bytes 829448 | tf_op jit(solution)/shard_map/ppermute | solution.py:402
  49.5 4.7 %collective-permute-done.4.refs_2_ = bf16[360,384]{1,0:T(8,128)(2,1)} collective-permute-done((bf16[360,384]{1,0:T(8,128)(2,1)}, bf16[360,384]{1,0:T(8,128)(2,1)}, u32[]{:S(2)}, u32[]{:S(2)}) %collective-permute-start.4) | collective-permute-done | bytes 276512 | tf_op jit(solution)/shard_map/ppermute | solution.py:402
  55.4 1.6 %collective-permute-start.18 = (bf16[320,384]{1,0:T(8,128)(2,1)}, bf16[320,384]{1,0:T(8,128)(2,1)}, u32[]{:S(2)}, u32[]{:S(2)}) collective-permute-start(bf16[320,384]{1,0:T(8,128)(2,1)} %collective-permute-done.16.refs_2_), channel_id=1, source_target_pairs={{4,0},{8,4},{12,8},{14,12},{10,14},{6,10},{2,6},{0,2},{5,1},{9,5},... | collective-permute-start | bytes 737288 | tf_op jit(solution)/shard_map/ppermute | solution.py:402
  57.2 5.0 %collective-permute-done.26.refs_4_ = bf16[256,384]{1,0:T(8,128)(2,1)S(1)} collective-permute-done((bf16[256,384]{1,0:T(8,128)(2,1)}, bf16[256,384]{1,0:T(8,128)(2,1)S(1)}, u32[]{:S(2)}, u32[]{:S(2)}) %collective-permute-start.26) | collective-permute-done | bytes 196640 | tf_op jit(solution)/shard_map/ppermute | solution.py:402
  62.9 1.7 %collective-permute-start.5 = (bf16[360,384]{1,0:T(8,128)(2,1)}, bf16[360,384]{1,0:T(8,128)(2,1)S(1)}, u32[]{:S(2)}, u32[]{:S(2)}) collective-permute-start(bf16[360,384]{1,0:T(8,128)(2,1)} %collective-permute-done.2.refs_1_), channel_id=1, source_target_pairs={{0,4},{4,8},{8,12},{12,14},{14,10},{10,6},{6,2},{2,0},{1,5},{5,9},... | collective-permute-start | bytes 829448 | tf_op jit(solution)/shard_map/ppermute | solution.py:400
  65.3 1.6 %collective-permute-start.27 = (bf16[256,384]{1,0:T(8,128)(2,1)S(1)}, bf16[256,384]{1,0:T(8,128)(2,1)S(1)}, u32[]{:S(2)}, u32[]{:S(2)}) collective-permute-start(bf16[256,384]{1,0:T(8,128)(2,1)S(1)} %collective-permute-done.25.refs_3_), channel_id=1, source_target_pairs={{0,4},{4,8},{8,12},{12,14},{14,10},{10,6},{6,2},{2,0},{1,5},{5,9},... | collective-permute-start | bytes 589832 | tf_op jit(solution)/shard_map/ppermute | solution.py:400
  67.2 6.0 %collective-permute-done.27.refs_5_ = bf16[256,384]{1,0:T(8,128)(2,1)S(1)} collective-permute-done((bf16[256,384]{1,0:T(8,128)(2,1)S(1)}, bf16[256,384]{1,0:T(8,128)(2,1)S(1)}, u32[]{:S(2)}, u32[]{:S(2)}) %collective-permute-start.27) | collective-permute-done | bytes 196640 | tf_op jit(solution)/shard_map/ppermute | solution.py:400
  73.2 2.5 %collective-permute-start.17 = (bf16[320,384]{1,0:T(8,128)(2,1)}, bf16[320,384]{1,0:T(8,128)(2,1)S(1)}, u32[]{:S(2)}, u32[]{:S(2)}) collective-permute-start(bf16[320,384]{1,0:T(8,128)(2,1)} %collective-permute-done.14.refs_1_), channel_id=1, source_target_pairs={{0,4},{4,8},{8,12},{12,14},{14,10},{10,6},{6,2},{2,0},{1,5},{5,9},... | collective-permute-start | bytes 737288 | tf_op jit(solution)/shard_map/ppermute | solution.py:400
  75.8 1.9 %collective-permute-start.7 = (bf16[360,384]{1,0:T(8,128)(2,1)S(1)}, bf16[360,384]{1,0:T(8,128)(2,1)S(1)}, u32[]{:S(2)}, u32[]{:S(2)}) collective-permute-start(bf16[360,384]{1,0:T(8,128)(2,1)S(1)} %collective-permute-done.5.refs_3_), channel_id=1, source_target_pairs={{0,4},{4,8},{8,12},{12,14},{14,10},{10,6},{6,2},{2,0},{1,5},{5,9},... | collective-permute-start | bytes 829448 | tf_op jit(solution)/shard_map/ppermute | solution.py:400
  77.8 1.3 constant_dynamic-update-slice_fusion
  79.2 3.9 %prepare.3.refs_8_ = bf16[3072,384]{1,0:T(8,128)(2,1)S(1)} custom-call(s32[17]{0:T(128)S(1)} %get-tuple-element.19.index_ref, s32[48,48]{1,0:T(8,128)S(1)} %copy-done.27, bf16[384,1536]{1,0:T(8,128)(2,1)} %collective-permute-done.10.refs_0_, bf16[384,1536]{1,0:T(8,128)(2,1)} %collective-permute-done.11.refs_1_), custom_call_target="tpu_custom_call" | custom-call | bytes 4718592 | tf_op jit(solution)/shard_map/prepare/pallas_call | solution.py:106
  83.2 1.0 product.13
  84.3 2.0 %collective-permute-start.33 = (bf16[192,384]{1,0:T(8,128)(2,1)S(1)}, bf16[192,384]{1,0:T(8,128)(2,1)S(1)}, u32[]{:S(2)}, u32[]{:S(2)}) collective-permute-start(bf16[192,384]{1,0:T(8,128)(2,1)S(1)} %copy-done.24), channel_id=1, source_target_pairs={{0,4},{4,8},{8,12},{12,14},{14,10},{10,6},{6,2},{2,0},{1,5},{5,9},... | collective-permute-start | bytes 442376 | tf_op jit(solution)/shard_map/ppermute | solution.py:400
  87.0 2.7 %product.11 = f32[320,384]{1,0:T(8,128)S(1)} custom-call(bf16[320,384]{1,0:T(8,128)(2,1)S(1)} %copy-done.2, bf16[320,384]{1,0:T(8,128)(2,1)} %collective-permute-done.14.refs_1_, bf16[320,384]{1,0:T(8,128)(2,1)} %collective-permute-done.16.refs_2_, bf16[320,384]{1,0:T(8,128)(2,1)S(1)} %collective-permute-done.17.refs_3_, ...), custom_call_target="tpu_custom_call" | custom-call | flops 754974720 | bytes 4325376 | tf_op jit(solution)/shard_map/product/pallas_call | solution.py:153
  90.2 1.6 %collective-permute-start.20 = (f32[320,384]{1,0:T(8,128)S(1)}, f32[320,384]{1,0:T(8,128)S(1)}, u32[]{:S(2)}, u32[]{:S(2)}) collective-permute-start(f32[320,384]{1,0:T(8,128)S(1)} %product.11), channel_id=1, source_target_pairs={{0,1},{1,0},{2,3},{3,2},{4,5},{5,4},{6,7},{7,6},{8,9},{9,8},{10,11... | collective-permute-start | bytes 1474568 | tf_op jit(solution)/shard_map/ppermute | solution.py:406
  91.8 2.7 %product.9 = f32[360,384]{1,0:T(8,128)S(1)} custom-call(bf16[360,384]{1,0:T(8,128)(2,1)S(1)} %copy-done.1, bf16[360,384]{1,0:T(8,128)(2,1)} %collective-permute-done.2.refs_1_, bf16[360,384]{1,0:T(8,128)(2,1)} %collective-permute-done.4.refs_2_, bf16[360,384]{1,0:T(8,128)(2,1)S(1)} %collective-permute-done.5.refs_3_, ...), custom_call_target="tpu_custom_call" | custom-call | flops 849346560 | bytes 4571136 | tf_op jit(solution)/shard_map/product/pallas_call | solution.py:153
  95.0 2.9 %fusion.refs_9_ = f32[1128,384]{1,0:T(8,128)S(1)} fusion(bf16[2256,384]{1,0:T(8,128)(2,1)S(1)} %constant_dynamic-update-slice_fusion, bf16[1128,2256]{1,0:T(8,128)(2,1)S(1)} %bitcast.11, bf16[1128,384]{1,0:T(8,128)(2,1)S(1)} %copy-done.28, f32[1128]{0:T(1024)S(1)} %select_reduce_fusion), kind=kOutput, calls=%fused_computation.1 | convolution fusion | flops 1955681280 | bytes 9425568 | tf_op jit(solution)/shard_map/dot_general | solution.py:392
  97.9 3.0 %prepare.2.refs_8_ = bf16[3072,384]{1,0:T(8,128)(2,1)S(1)} custom-call(s32[17]{0:T(128)S(1)} %get-tuple-element.20.index_ref, s32[48,48]{1,0:T(8,128)S(1)} %copy-done.27, bf16[384,1536]{1,0:T(8,128)(2,1)S(1)} %parts.3.refs_0_, bf16[384,1536]{1,0:T(8,128)(2,1)S(1)} %collective-permute-done.8.refs_1_), custom_call_target="tpu_custom_call" | custom-call | bytes 4718592 | tf_op jit(solution)/shard_map/prepare/pallas_call | solution.py:106
  101.0 0.8 product.15
  101.7 1.7 %collective-permute-start.36 = (f32[192,384]{1,0:T(8,128)S(1)}, f32[192,384]{1,0:T(8,128)S(1)}, u32[]{:S(2)}, u32[]{:S(2)}) collective-permute-start(f32[192,384]{1,0:T(8,128)S(1)} %product.15), channel_id=1, source_target_pairs={{0,1},{1,0},{2,3},{3,2},{4,5},{5,4},{6,7},{7,6},{8,9},{9,8},{10,11... | collective-permute-start | bytes 884744 | tf_op jit(solution)/shard_map/ppermute | solution.py:406
  103.4 2.8 %product.8 = f32[360,384]{1,0:T(8,128)S(1)} custom-call(bf16[360,384]{1,0:T(8,128)(2,1)S(1)} %copy-done.1, bf16[360,384]{1,0:T(8,128)(2,1)} %collective-permute-done.2.refs_1_, bf16[360,384]{1,0:T(8,128)(2,1)} %collective-permute-done.4.refs_2_, bf16[360,384]{1,0:T(8,128)(2,1)S(1)} %collective-permute-done.5.refs_3_, ...), custom_call_target="tpu_custom_call" | custom-call | flops 849346560 | bytes 4571136 | tf_op jit(solution)/shard_map/product/pallas_call | solution.py:153
  106.2 15.0 %collective-permute-done.12 = f32[360,384]{1,0:T(8,128)S(1)} collective-permute-done((f32[360,384]{1,0:T(8,128)S(1)}, f32[360,384]{1,0:T(8,128)S(1)}, u32[]{:S(2)}, u32[]{:S(2)}) %collective-permute-start.12) | collective-permute-done | bytes 552992 | tf_op jit(solution)/shard_map/ppermute | solution.py:406
  121.4 2.7 %product.10 = f32[320,384]{1,0:T(8,128)S(1)} custom-call(bf16[320,384]{1,0:T(8,128)(2,1)S(1)} %copy-done.2, bf16[320,384]{1,0:T(8,128)(2,1)} %collective-permute-done.14.refs_1_, bf16[320,384]{1,0:T(8,128)(2,1)} %collective-permute-done.16.refs_2_, bf16[320,384]{1,0:T(8,128)(2,1)S(1)} %collective-permute-done.17.refs_3_, ...), custom_call_target="tpu_custom_call" | custom-call | flops 754974720 | bytes 4325376 | tf_op jit(solution)/shard_map/product/pallas_call | solution.py:153
  124.7 1.0 product.12
  126.4 0.8 product.14
  127.8 3.5 %mirror_early.1.refs_5_ = f32[1136,3,128]{2,1,0:T(4,128)S(1)} custom-call(s32[1128]{0:T(1024)S(1)} %maximum_select_fusion.index_ref, f32[360,384]{1,0:T(8,128)S(1)} %add.79.refs_0_, f32[320,384]{1,0:T(8,128)S(1)} %add.80.refs_1_, f32[256,384]{1,0:T(8,128)S(1)} %add.81.refs_2_, f32[360,384]{1,0:T(8,128)S(1)} %collective-permute-done.38.refs_3_, ...), custom_call_target="tpu_custom_call" | custom-call | flops 433152 | bytes 5197824 | tf_op jit(solution)/shard_map/mirror_early/pallas_call | solution.py:307
  131.3 3.1 %mirror_late.1 = (f32[1128,384]{1,0:T(8,128)}, f32[1136,3,128]{2,1,0:T(4,128)S(1)}) custom-call(s32[384]{0:T(512)S(1)} %and_select_fusion.2.target_ref, f32[360,384]{1,0:T(8,128)S(1)} %add.79.refs_0_, f32[320,384]{1,0:T(8,128)S(1)} %add.80.refs_1_, f32[256,384]{1,0:T(8,128)S(1)} %add.81.refs_2_, ...), custom_call_target="tpu_custom_call", output_to_operand_aliasing={{1}: (6, {})} | custom-call | flops 433152 | bytes 5197824 | tf_op jit(solution)/shard_map/mirror_late/pallas_call | solution.py:317
  (133 shorter events, 14.2 us)
Async XLA Ops:
  0.0 47.6 %copy-start = (bf16[384,3072]{1,0:T(8,128)(2,1)S(1)}, bf16[384,3072]{1,0:T(8,128)(2,1)}, u32[]{:S(2)}) copy-start(bf16[384,3072]{1,0:T(8,128)(2,1)} %refs_0_.3) | copy-start | bytes 7077892
  3.1 34.9 %collective-permute-start.10 = (bf16[384,1536]{1,0:T(8,128)(2,1)}, bf16[384,1536]{1,0:T(8,128)(2,1)}, u32[]{:S(2)}, u32[]{:S(2)}) collective-permute-start(bf16[384,1536]{1,0:T(8,128)(2,1)} %get-tuple-element.12), channel_id=1, source_target_pairs={{0,1},{1,0},{2,3},{3,2},{4,5},{5,4},{6,7},{7,6},{8,9},{9,8},{10,11... | collective-permute-start | bytes 3538952 | tf_op jit(solution)/shard_map/ppermute | solution.py:378
  6.1 12.7 %collective-permute-start.21 = (bf16[256,384]{1,0:T(8,128)(2,1)}, bf16[256,384]{1,0:T(8,128)(2,1)S(1)}, u32[]{:S(2)}, u32[]{:S(2)}) collective-permute-start(bf16[256,384]{1,0:T(8,128)(2,1)} %get-tuple-element.14.refs_0_), channel_id=1, source_target_pairs={{0,4},{4,8},{8,12},{12,14},{14,10},{10,6},{6,2},{2,0},{1,5},{5,9},... | collective-permute-start | bytes 589832 | tf_op jit(solution)/shard_map/ppermute | solution.py:400
  7.7 6.9 %collective-permute-start.31 = (bf16[192,384]{1,0:T(8,128)(2,1)}, bf16[192,384]{1,0:T(8,128)(2,1)S(1)}, u32[]{:S(2)}, u32[]{:S(2)}) collective-permute-start(bf16[192,384]{1,0:T(8,128)(2,1)} %get-tuple-element.15.refs_0_), channel_id=1, source_target_pairs={{4,0},{8,4},{12,8},{14,12},{10,14},{6,10},{2,6},{0,2},{5,1},{9,5},... | collective-permute-start | bytes 442376 | tf_op jit(solution)/shard_map/ppermute | solution.py:402
  8.2 9.1 %collective-permute-start.29 = (bf16[192,384]{1,0:T(8,128)(2,1)}, bf16[192,384]{1,0:T(8,128)(2,1)S(1)}, u32[]{:S(2)}, u32[]{:S(2)}) collective-permute-start(bf16[192,384]{1,0:T(8,128)(2,1)} %get-tuple-element.15.refs_0_), channel_id=1, source_target_pairs={{0,4},{4,8},{8,12},{12,14},{14,10},{10,6},{6,2},{2,0},{1,5},{5,9},... | collective-permute-start | bytes 442376 | tf_op jit(solution)/shard_map/ppermute | solution.py:400
  9.7 9.6 %collective-permute-start.23 = (bf16[256,384]{1,0:T(8,128)(2,1)}, bf16[256,384]{1,0:T(8,128)(2,1)S(1)}, u32[]{:S(2)}, u32[]{:S(2)}) collective-permute-start(bf16[256,384]{1,0:T(8,128)(2,1)} %get-tuple-element.14.refs_0_), channel_id=1, source_target_pairs={{4,0},{8,4},{12,8},{14,12},{10,14},{6,10},{2,6},{0,2},{5,1},{9,5},... | collective-permute-start | bytes 589832 | tf_op jit(solution)/shard_map/ppermute | solution.py:402
  14.7 16.2 %collective-permute-start.1 = (bf16[360,384]{1,0:T(8,128)(2,1)}, bf16[360,384]{1,0:T(8,128)(2,1)}, u32[]{:S(2)}, u32[]{:S(2)}) collective-permute-start(bf16[360,384]{1,0:T(8,128)(2,1)} %get-tuple-element.11.refs_0_), channel_id=1, source_target_pairs={{0,4},{4,8},{8,12},{12,14},{14,10},{10,6},{6,2},{2,0},{1,5},{5,9},... | collective-permute-start | bytes 829448 | tf_op jit(solution)/shard_map/ppermute | solution.py:400
  17.3 8.5 %collective-permute-start.15 = (bf16[320,384]{1,0:T(8,128)(2,1)}, bf16[320,384]{1,0:T(8,128)(2,1)}, u32[]{:S(2)}, u32[]{:S(2)}) collective-permute-start(bf16[320,384]{1,0:T(8,128)(2,1)} %get-tuple-element.13.refs_0_), channel_id=1, source_target_pairs={{4,0},{8,4},{12,8},{14,12},{10,14},{6,10},{2,6},{0,2},{5,1},{9,5},... | collective-permute-start | bytes 737288 | tf_op jit(solution)/shard_map/ppermute | solution.py:402
  18.8 10.5 %collective-permute-start.13 = (bf16[320,384]{1,0:T(8,128)(2,1)}, bf16[320,384]{1,0:T(8,128)(2,1)}, u32[]{:S(2)}, u32[]{:S(2)}) collective-permute-start(bf16[320,384]{1,0:T(8,128)(2,1)} %get-tuple-element.13.refs_0_), channel_id=1, source_target_pairs={{0,4},{4,8},{8,12},{12,14},{14,10},{10,6},{6,2},{2,0},{1,5},{5,9},... | collective-permute-start | bytes 737288 | tf_op jit(solution)/shard_map/ppermute | solution.py:400
  19.3 13.3 %collective-permute-start.3 = (bf16[360,384]{1,0:T(8,128)(2,1)}, bf16[360,384]{1,0:T(8,128)(2,1)}, u32[]{:S(2)}, u32[]{:S(2)}) collective-permute-start(bf16[360,384]{1,0:T(8,128)(2,1)} %get-tuple-element.11.refs_0_), channel_id=1, source_target_pairs={{4,0},{8,4},{12,8},{14,12},{10,14},{6,10},{2,6},{0,2},{5,1},{9,5},... | collective-permute-start | bytes 829448 | tf_op jit(solution)/shard_map/ppermute | solution.py:402
  25.8 12.2 %collective-permute-start.22 = (bf16[256,384]{1,0:T(8,128)(2,1)S(1)}, bf16[256,384]{1,0:T(8,128)(2,1)S(1)}, u32[]{:S(2)}, u32[]{:S(2)}) collective-permute-start(bf16[256,384]{1,0:T(8,128)(2,1)S(1)} %collective-permute-done.21.refs_6_), channel_id=1, source_target_pairs={{0,4},{4,8},{8,12},{12,14},{14,10},{10,6},{6,2},{2,0},{1,5},{5,9},... | collective-permute-start | bytes 589832 | tf_op jit(solution)/shard_map/ppermute | solution.py:400
  29.3 6.7 %collective-permute-start.32 = (bf16[192,384]{1,0:T(8,128)(2,1)S(1)}, bf16[192,384]{1,0:T(8,128)(2,1)S(1)}, u32[]{:S(2)}, u32[]{:S(2)}) collective-permute-start(bf16[192,384]{1,0:T(8,128)(2,1)S(1)} %collective-permute-done.31.refs_7_), channel_id=1, source_target_pairs={{4,0},{8,4},{12,8},{14,12},{10,14},{6,10},{2,6},{0,2},{5,1},{9,5},... | collective-permute-start | bytes 442376 | tf_op jit(solution)/shard_map/ppermute | solution.py:402
  30.8 6.1 %collective-permute-start.30 = (bf16[192,384]{1,0:T(8,128)(2,1)S(1)}, bf16[192,384]{1,0:T(8,128)(2,1)S(1)}, u32[]{:S(2)}, u32[]{:S(2)}) collective-permute-start(bf16[192,384]{1,0:T(8,128)(2,1)S(1)} %collective-permute-done.29.refs_6_), channel_id=1, source_target_pairs={{0,4},{4,8},{8,12},{12,14},{14,10},{10,6},{6,2},{2,0},{1,5},{5,9},... | collective-permute-start | bytes 442376 | tf_op jit(solution)/shard_map/ppermute | solution.py:400
  32.6 7.0 %collective-permute-start.24 = (bf16[256,384]{1,0:T(8,128)(2,1)S(1)}, bf16[256,384]{1,0:T(8,128)(2,1)S(1)}, u32[]{:S(2)}, u32[]{:S(2)}) collective-permute-start(bf16[256,384]{1,0:T(8,128)(2,1)S(1)} %collective-permute-done.23.refs_7_), channel_id=1, source_target_pairs={{4,0},{8,4},{12,8},{14,12},{10,14},{6,10},{2,6},{0,2},{5,1},{9,5},... | collective-permute-start | bytes 589832 | tf_op jit(solution)/shard_map/ppermute | solution.py:402
  36.0 11.8 %collective-permute-start.16 = (bf16[320,384]{1,0:T(8,128)(2,1)}, bf16[320,384]{1,0:T(8,128)(2,1)}, u32[]{:S(2)}, u32[]{:S(2)}) collective-permute-start(bf16[320,384]{1,0:T(8,128)(2,1)} %collective-permute-done.15.refs_7_), channel_id=1, source_target_pairs={{4,0},{8,4},{12,8},{14,12},{10,14},{6,10},{2,6},{0,2},{5,1},{9,5},... | collective-permute-start | bytes 737288 | tf_op jit(solution)/shard_map/ppermute | solution.py:402
  36.9 11.0 %collective-permute-start.14 = (bf16[320,384]{1,0:T(8,128)(2,1)}, bf16[320,384]{1,0:T(8,128)(2,1)}, u32[]{:S(2)}, u32[]{:S(2)}) collective-permute-start(bf16[320,384]{1,0:T(8,128)(2,1)} %collective-permute-done.13.refs_6_), channel_id=1, source_target_pairs={{0,4},{4,8},{8,12},{12,14},{14,10},{10,6},{6,2},{2,0},{1,5},{5,9},... | collective-permute-start | bytes 737288 | tf_op jit(solution)/shard_map/ppermute | solution.py:400
  38.0 37.8 %collective-permute-start.11 = (bf16[384,1536]{1,0:T(8,128)(2,1)}, bf16[384,1536]{1,0:T(8,128)(2,1)}, u32[]{:S(2)}, u32[]{:S(2)}) collective-permute-start(bf16[384,1536]{1,0:T(8,128)(2,1)} %collective-permute-done.10.refs_0_), channel_id=1, source_target_pairs={{0,16},{16,0},{1,17},{17,1},{2,18},{18,2},{3,19},{19,3},{4,20},{20... | collective-permute-start | bytes 3538952 | tf_op jit(solution)/shard_map/ppermute | solution.py:35
  38.0 7.5 %collective-permute-start.34 = (bf16[192,384]{1,0:T(8,128)(2,1)S(1)}, bf16[192,384]{1,0:T(8,128)(2,1)S(1)}, u32[]{:S(2)}, u32[]{:S(2)}) collective-permute-start(bf16[192,384]{1,0:T(8,128)(2,1)S(1)} %collective-permute-done.32.refs_2_), channel_id=1, source_target_pairs={{4,0},{8,4},{12,8},{14,12},{10,14},{6,10},{2,6},{0,2},{5,1},{9,5},... | collective-permute-start | bytes 442376 | tf_op jit(solution)/shard_map/ppermute | solution.py:402
  39.7 9.7 %collective-permute-start.2 = (bf16[360,384]{1,0:T(8,128)(2,1)}, bf16[360,384]{1,0:T(8,128)(2,1)}, u32[]{:S(2)}, u32[]{:S(2)}) collective-permute-start(bf16[360,384]{1,0:T(8,128)(2,1)} %collective-permute-done.1.refs_6_), channel_id=1, source_target_pairs={{0,4},{4,8},{8,12},{12,14},{14,10},{10,6},{6,2},{2,0},{1,5},{5,9},... | collective-permute-start | bytes 829448 | tf_op jit(solution)/shard_map/ppermute | solution.py:400
  46.2 8.0 %collective-permute-start.4 = (bf16[360,384]{1,0:T(8,128)(2,1)}, bf16[360,384]{1,0:T(8,128)(2,1)}, u32[]{:S(2)}, u32[]{:S(2)}) collective-permute-start(bf16[360,384]{1,0:T(8,128)(2,1)} %collective-permute-done.3.refs_7_), channel_id=1, source_target_pairs={{4,0},{8,4},{12,8},{14,12},{10,14},{6,10},{2,6},{0,2},{5,1},{9,5},... | collective-permute-start | bytes 829448 | tf_op jit(solution)/shard_map/ppermute | solution.py:402
  47.6 9.5 %copy-start.30 = (s32[1128,2]{0,1:T(2,128)S(1)}, s32[1128,2]{0,1:T(2,128)}, u32[]{:S(2)}) copy-start(s32[1128,2]{0,1:T(2,128)} %param.13) | copy-start | bytes 27076
  47.6 9.5 %copy-start.31 = (f32[48]{0:T(128)S(1)}, f32[48]{0:T(128)}, u32[]{:S(2)}) copy-start(f32[48]{0:T(128)} %param.12) | copy-start | bytes 580
  47.8 27.8 %collective-permute-start.9 = (bf16[1128,384]{1,0:T(8,128)(2,1)}, bf16[1128,384]{1,0:T(8,128)(2,1)}, u32[]{:S(2)}, u32[]{:S(2)}) collective-permute-start(bf16[1128,384]{1,0:T(8,128)(2,1)} %refs_1_.1), channel_id=1, source_target_pairs={{0,16},{16,0},{1,17},{17,1},{2,18},{18,2},{3,19},{19,3},{4,20},{20... | collective-permute-start | bytes 2598920 | tf_op jit(solution)/shard_map/ppermute | solution.py:35
  47.9 7.5 %collective-permute-start.25 = (bf16[256,384]{1,0:T(8,128)(2,1)}, bf16[256,384]{1,0:T(8,128)(2,1)S(1)}, u32[]{:S(2)}, u32[]{:S(2)}) collective-permute-start(bf16[256,384]{1,0:T(8,128)(2,1)} %copy-done.8), channel_id=1, source_target_pairs={{0,4},{4,8},{8,12},{12,14},{14,10},{10,6},{6,2},{2,0},{1,5},{5,9},... | collective-permute-start | bytes 589832 | tf_op jit(solution)/shard_map/ppermute | solution.py:400
  49.3 45.2 %collective-permute-start.8 = (bf16[384,1536]{1,0:T(8,128)(2,1)S(1)}, bf16[384,1536]{1,0:T(8,128)(2,1)S(1)}, u32[]{:S(2)}, u32[]{:S(2)}) collective-permute-start(bf16[384,1536]{1,0:T(8,128)(2,1)S(1)} %parts.3.refs_0_), channel_id=1, source_target_pairs={{0,16},{16,0},{1,17},{17,1},{2,18},{18,2},{3,19},{19,3},{4,20},{20... | collective-permute-start | bytes 3538952 | tf_op jit(solution)/shard_map/ppermute | solution.py:35
  54.2 8.0 %collective-permute-start.26 = (bf16[256,384]{1,0:T(8,128)(2,1)}, bf16[256,384]{1,0:T(8,128)(2,1)S(1)}, u32[]{:S(2)}, u32[]{:S(2)}) collective-permute-start(bf16[256,384]{1,0:T(8,128)(2,1)} %copy-done.10), channel_id=1, source_target_pairs={{4,0},{8,4},{12,8},{14,12},{10,14},{6,10},{2,6},{0,2},{5,1},{9,5},... | collective-permute-start | bytes 589832 | tf_op jit(solution)/shard_map/ppermute | solution.py:402
  55.4 11.8 %copy-start.12 = (bf16[256,384]{1,0:T(8,128)(2,1)}, bf16[256,384]{1,0:T(8,128)(2,1)S(1)}, u32[]{:S(2)}) copy-start(bf16[256,384]{1,0:T(8,128)(2,1)S(1)} %collective-permute-done.25.refs_3_) | copy-start | bytes 589828
  55.4 9.9 %collective-permute-start.18 = (bf16[320,384]{1,0:T(8,128)(2,1)}, bf16[320,384]{1,0:T(8,128)(2,1)}, u32[]{:S(2)}, u32[]{:S(2)}) collective-permute-start(bf16[320,384]{1,0:T(8,128)(2,1)} %collective-permute-done.16.refs_2_), channel_id=1, source_target_pairs={{4,0},{8,4},{12,8},{14,12},{10,14},{6,10},{2,6},{0,2},{5,1},{9,5},... | collective-permute-start | bytes 737288 | tf_op jit(solution)/shard_map/ppermute | solution.py:402
  62.9 12.7 %collective-permute-start.5 = (bf16[360,384]{1,0:T(8,128)(2,1)}, bf16[360,384]{1,0:T(8,128)(2,1)S(1)}, u32[]{:S(2)}, u32[]{:S(2)}) collective-permute-start(bf16[360,384]{1,0:T(8,128)(2,1)} %collective-permute-done.2.refs_1_), channel_id=1, source_target_pairs={{0,4},{4,8},{8,12},{12,14},{14,10},{10,6},{6,2},{2,0},{1,5},{5,9},... | collective-permute-start | bytes 829448 | tf_op jit(solution)/shard_map/ppermute | solution.py:400
  65.3 7.9 %collective-permute-start.27 = (bf16[256,384]{1,0:T(8,128)(2,1)S(1)}, bf16[256,384]{1,0:T(8,128)(2,1)S(1)}, u32[]{:S(2)}, u32[]{:S(2)}) collective-permute-start(bf16[256,384]{1,0:T(8,128)(2,1)S(1)} %collective-permute-done.25.refs_3_), channel_id=1, source_target_pairs={{0,4},{4,8},{8,12},{12,14},{14,10},{10,6},{6,2},{2,0},{1,5},{5,9},... | collective-permute-start | bytes 589832 | tf_op jit(solution)/shard_map/ppermute | solution.py:400
  67.0 12.1 %copy-start.27 = (s32[48,48]{1,0:T(8,128)S(1)}, s32[48,48]{1,0:T(8,128)}, u32[]{:S(2)}) copy-start(s32[48,48]{1,0:T(8,128)} %map_hbm.3) | copy-start | bytes 27652
  73.2 11.1 %collective-permute-start.17 = (bf16[320,384]{1,0:T(8,128)(2,1)}, bf16[320,384]{1,0:T(8,128)(2,1)S(1)}, u32[]{:S(2)}, u32[]{:S(2)}) collective-permute-start(bf16[320,384]{1,0:T(8,128)(2,1)} %collective-permute-done.14.refs_1_), channel_id=1, source_target_pairs={{0,4},{4,8},{8,12},{12,14},{14,10},{10,6},{6,2},{2,0},{1,5},{5,9},... | collective-permute-start | bytes 737288 | tf_op jit(solution)/shard_map/ppermute | solution.py:400
  75.7 14.0 %collective-permute-start.6 = (bf16[360,384]{1,0:T(8,128)(2,1)}, bf16[360,384]{1,0:T(8,128)(2,1)S(1)}, u32[]{:S(2)}, u32[]{:S(2)}) collective-permute-start(bf16[360,384]{1,0:T(8,128)(2,1)} %collective-permute-done.4.refs_2_), channel_id=1, source_target_pairs={{4,0},{8,4},{12,8},{14,12},{10,14},{6,10},{2,6},{0,2},{5,1},{9,5},... | collective-permute-start | bytes 829448 | tf_op jit(solution)/shard_map/ppermute | solution.py:402
  75.7 10.9 %collective-permute-start.19 = (bf16[320,384]{1,0:T(8,128)(2,1)}, bf16[320,384]{1,0:T(8,128)(2,1)S(1)}, u32[]{:S(2)}, u32[]{:S(2)}) collective-permute-start(bf16[320,384]{1,0:T(8,128)(2,1)} %collective-permute-done.18.refs_4_), channel_id=1, source_target_pairs={{4,0},{8,4},{12,8},{14,12},{10,14},{6,10},{2,6},{0,2},{5,1},{9,5},... | collective-permute-start | bytes 737288 | tf_op jit(solution)/shard_map/ppermute | solution.py:402
  75.8 14.3 %collective-permute-start.7 = (bf16[360,384]{1,0:T(8,128)(2,1)S(1)}, bf16[360,384]{1,0:T(8,128)(2,1)S(1)}, u32[]{:S(2)}, u32[]{:S(2)}) collective-permute-start(bf16[360,384]{1,0:T(8,128)(2,1)S(1)} %collective-permute-done.5.refs_3_), channel_id=1, source_target_pairs={{0,4},{4,8},{8,12},{12,14},{14,10},{10,6},{6,2},{2,0},{1,5},{5,9},... | collective-permute-start | bytes 829448 | tf_op jit(solution)/shard_map/ppermute | solution.py:400
  83.2 11.8 %slice-start = ((s8[5197824]{0:T(1024)(128)(4,1)}), s8[4194304]{0:T(1024)(128)(4,1)S(1)}, s32[]{:S(2)}) async-start(s8[5197824]{0:T(1024)(128)(4,1)} %bitcast.10), calls=%async_computation | async-start | bytes 8388608
  84.2 10.8 %slice-start.1 = ((s8[5197824]{0:T(1024)(128)(4,1)}), s8[1003520]{0:T(1024)(128)(4,1)S(1)}, s32[]{:S(2)}) async-start(s8[5197824]{0:T(1024)(128)(4,1)} %bitcast.10), calls=%async_computation.1 | async-start | bytes 2007040
  84.3 16.6 %collective-permute-start.33 = (bf16[192,384]{1,0:T(8,128)(2,1)S(1)}, bf16[192,384]{1,0:T(8,128)(2,1)S(1)}, u32[]{:S(2)}, u32[]{:S(2)}) collective-permute-start(bf16[192,384]{1,0:T(8,128)(2,1)S(1)} %copy-done.24), channel_id=1, source_target_pairs={{0,4},{4,8},{8,12},{12,14},{14,10},{10,6},{6,2},{2,0},{1,5},{5,9},... | collective-permute-start | bytes 442376 | tf_op jit(solution)/shard_map/ppermute | solution.py:400
  86.6 14.3 %collective-permute-start.35 = (bf16[192,384]{1,0:T(8,128)(2,1)S(1)}, bf16[192,384]{1,0:T(8,128)(2,1)S(1)}, u32[]{:S(2)}, u32[]{:S(2)}) collective-permute-start(bf16[192,384]{1,0:T(8,128)(2,1)S(1)} %copy-done.26), channel_id=1, source_target_pairs={{4,0},{8,4},{12,8},{14,12},{10,14},{6,10},{2,6},{0,2},{5,1},{9,5},... | collective-permute-start | bytes 442376 | tf_op jit(solution)/shard_map/ppermute | solution.py:402
  89.7 36.1 %collective-permute-start.28 = (f32[256,384]{1,0:T(8,128)S(1)}, f32[256,384]{1,0:T(8,128)S(1)}, u32[]{:S(2)}, u32[]{:S(2)}) collective-permute-start(f32[256,384]{1,0:T(8,128)S(1)} %product.13), channel_id=1, source_target_pairs={{0,1},{1,0},{2,3},{3,2},{4,5},{5,4},{6,7},{7,6},{8,9},{9,8},{10,11... | collective-permute-start | bytes 1179656 | tf_op jit(solution)/shard_map/ppermute | solution.py:406
  90.2 34.0 %collective-permute-start.20 = (f32[320,384]{1,0:T(8,128)S(1)}, f32[320,384]{1,0:T(8,128)S(1)}, u32[]{:S(2)}, u32[]{:S(2)}) collective-permute-start(f32[320,384]{1,0:T(8,128)S(1)} %product.11), channel_id=1, source_target_pairs={{0,1},{1,0},{2,3},{3,2},{4,5},{5,4},{6,7},{7,6},{8,9},{9,8},{10,11... | collective-permute-start | bytes 1474568 | tf_op jit(solution)/shard_map/ppermute | solution.py:406
  94.5 26.7 %collective-permute-start.12 = (f32[360,384]{1,0:T(8,128)S(1)}, f32[360,384]{1,0:T(8,128)S(1)}, u32[]{:S(2)}, u32[]{:S(2)}) collective-permute-start(f32[360,384]{1,0:T(8,128)S(1)} %product.9), channel_id=1, source_target_pairs={{0,1},{1,0},{2,3},{3,2},{4,5},{5,4},{6,7},{7,6},{8,9},{9,8},{10,11... | collective-permute-start | bytes 1658888 | tf_op jit(solution)/shard_map/ppermute | solution.py:406
  101.7 25.4 %collective-permute-start.36 = (f32[192,384]{1,0:T(8,128)S(1)}, f32[192,384]{1,0:T(8,128)S(1)}, u32[]{:S(2)}, u32[]{:S(2)}) collective-permute-start(f32[192,384]{1,0:T(8,128)S(1)} %product.15), channel_id=1, source_target_pairs={{0,1},{1,0},{2,3},{3,2},{4,5},{5,4},{6,7},{7,6},{8,9},{9,8},{10,11... | collective-permute-start | bytes 884744 | tf_op jit(solution)/shard_map/ppermute | solution.py:406
  121.3 6.4 %collective-permute-start.38 = (f32[360,384]{1,0:T(8,128)S(1)}, f32[360,384]{1,0:T(8,128)S(1)}, u32[]{:S(2)}, u32[]{:S(2)}) collective-permute-start(f32[360,384]{1,0:T(8,128)S(1)} %add.79.refs_0_), channel_id=1, source_target_pairs={{0,16},{16,0},{1,17},{17,1},{2,18},{18,2},{3,19},{19,3},{4,20},{20... | collective-permute-start | bytes 1658888 | tf_op jit(solution)/shard_map/ppermute | solution.py:35
  124.2 3.6 %collective-permute-start.39 = (f32[320,384]{1,0:T(8,128)S(1)}, f32[320,384]{1,0:T(8,128)S(1)}, u32[]{:S(2)}, u32[]{:S(2)}) collective-permute-start(f32[320,384]{1,0:T(8,128)S(1)} %add.80.refs_1_), channel_id=1, source_target_pairs={{0,16},{16,0},{1,17},{17,1},{2,18},{18,2},{3,19},{19,3},{4,20},{20... | collective-permute-start | bytes 1474568 | tf_op jit(solution)/shard_map/ppermute | solution.py:35
  125.8 2.0 %collective-permute-start.40 = (f32[256,384]{1,0:T(8,128)S(1)}, f32[256,384]{1,0:T(8,128)S(1)}, u32[]{:S(2)}, u32[]{:S(2)}) collective-permute-start(f32[256,384]{1,0:T(8,128)S(1)} %add.81.refs_2_), channel_id=1, source_target_pairs={{0,16},{16,0},{1,17},{17,1},{2,18},{18,2},{3,19},{19,3},{4,20},{20... | collective-permute-start | bytes 1179656 | tf_op jit(solution)/shard_map/ppermute | solution.py:35
  125.9 1.7 %collective-permute-start = (s32[1128]{0:T(1024)S(1)}, s32[1128]{0:T(1024)S(1)}, u32[]{:S(2)}, u32[]{:S(2)}) collective-permute-start(s32[1128]{0:T(1024)S(1)} %copy-done.29), channel_id=1, source_target_pairs={{0,16},{16,0},{1,17},{17,1},{2,18},{18,2},{3,19},{19,3},{4,20},{20... | collective-permute-start | bytes 13544 | tf_op jit(solution)/shard_map/ppermute | solution.py:35
  127.2 4.1 %collective-permute-start.37 = (f32[192,384]{1,0:T(8,128)S(1)}, f32[192,384]{1,0:T(8,128)S(1)}, u32[]{:S(2)}, u32[]{:S(2)}) collective-permute-start(f32[192,384]{1,0:T(8,128)S(1)} %add.82.refs_3_), channel_id=1, source_target_pairs={{0,16},{16,0},{1,17},{17,1},{2,18},{18,2},{3,19},{19,3},{4,20},{20... | collective-permute-start | bytes 884744 | tf_op jit(solution)/shard_map/ppermute | solution.py:35
  (27 other events, 76.3 us)
